TPU v7x, 32 devices: a whole 2x2x4 slice. The times are simulated.
32 devices in a mesh: by: 4 (over y, core), bx: 8 (over z, x).
Axes of the slice: x: 2, y: 2, z: 4, core: 2. Of those that a mesh axis runs over, the one named last changes fastest.
Arguments:
- fields: float32 [3, 8, 1024, 2048], P(None, None, 'by', 'bx'), may hold values from -6 to 6
- level_count: int32 [1024, 2048], P('by', 'bx'), may hold values from 0 to 8, as said below
- thickness: float32 [8], replicated, may hold values from 0.05 to 0.3
- old_pressure: float32 [1024, 2048], P('by', 'bx'), may hold values from -6 to 6
Outputs:
- pressure: float32 [1024, 2048], P('by', 'bx')
- residual: float32 [1024, 2048], P('by', 'bx')
Inputs may be any that keep to these rules, and one draw needn't show every extreme that they name: `level_count`: land comes in aligned squares of 8 x 8 cells, except that the cell at row 1, column 0 is always ocean with all 8 levels.
All inputs are finite; a program needn't handle non-finite values.
Results may differ from a plain program's by a relative error of at most 0.00024.
Values sent between devices are 32-bit elements; how exact they have to be, the bound alone decides.
No kernel may reach another device: no remote copies, remote signals or barrier semaphores. Data moves between devices by JAX's collectives and lax.ppermute only.
A program may use at most 128 MiB of HBM per device.

v0:
```python
import jax
import jax.numpy as jnp
from jax import lax
from jax.sharding import PartitionSpec as P

ITERS = 4


VISCOSITY = 0.05
IMPLICIT = 0.05


def padded(array, sides, width):
    for axis, dim in sides:
        size, length = (lax.axis_size(axis), array.shape[dim])
        up = [(i, (i + 1) % size) for i in range(size)]
        down = [(j, i) for i, j in up]
        last = lax.slice_in_dim(array, length - width, length, axis=dim)
        initial = lax.slice_in_dim(array, 0, width, axis=dim)
        before = lax.ppermute(last, axis, up)
        after = lax.ppermute(initial, axis, down)
        array = jnp.concatenate([before, array, after], axis=dim)
    return array


def laplace(field):
    return (
        field[..., 1:-1, 2:]
        + field[..., 1:-1, :-2]
        + field[..., 2:, 1:-1]
        + field[..., :-2, 1:-1]
        - 4.0 * field[..., 1:-1, 1:-1]
    )


def level_divergence(extended):
    zonal = extended[0]
    meridional = extended[1]
    baroclinic = extended[2]
    tend_zonal = -VISCOSITY * laplace(laplace(zonal)) - 0.5 * (
        baroclinic[..., 2:-2, 3:-1] - baroclinic[..., 2:-2, 1:-3]
    )
    tend_merid = -VISCOSITY * laplace(laplace(meridional)) - 0.5 * (
        baroclinic[..., 3:-1, 2:-2] - baroclinic[..., 1:-3, 2:-2]
    )
    return 0.5 * (tend_zonal[..., 1:-1, 2:] - tend_zonal[..., 1:-1, :-2]) + 0.5 * (
        tend_merid[..., 2:, 1:-1] - tend_merid[..., :-2, 1:-1]
    )


def corner_min(extended_depth):
    return jnp.minimum(
        jnp.minimum(extended_depth[:-1, :-1], extended_depth[:-1, 1:]),
        jnp.minimum(extended_depth[1:, :-1], extended_depth[1:, 1:]),
    )


def operate(extended, corner):
    west_south = extended[:-1, :-1]
    east_south = extended[:-1, 1:]
    west_north = extended[1:, :-1]
    east_north = extended[1:, 1:]
    east_slope = 0.5 * (east_south + east_north - west_south - west_north)
    north_slope = 0.5 * (west_north + east_north - west_south - east_south)
    plus_flux = 0.5 * corner * (east_slope + north_slope)
    minus_flux = 0.5 * corner * (east_slope - north_slope)
    return (
        IMPLICIT * extended[1:-1, 1:-1]
        + plus_flux[:-1, :-1]
        - plus_flux[1:, 1:]
        + minus_flux[1:, :-1]
        - minus_flux[:-1, 1:]
    )


def strip_extend(field):
    rows_ext = padded(field, ((("by", "bx"), 0),), 1)
    return jnp.pad(rows_ext, ((0, 0), (1, 1)), mode="wrap")


def paired_dots(residual, precond, image_field):
    return lax.psum((jnp.sum(residual * precond), jnp.sum(precond * image_field)), ("by", "bx"))


def solve(right_side, column_depth, first_guess, extend):
    corner = corner_min(extend(column_depth))
    diagonal = IMPLICIT + 0.5 * (
        corner[1:, 1:] + corner[1:, :-1] + corner[:-1, 1:] + corner[:-1, :-1]
    )
    pressure = first_guess
    residual = right_side - operate(extend(pressure), corner)
    precond = residual / diagonal
    image_field = operate(extend(precond), corner)
    norm_now, curvature = paired_dots(residual, precond, image_field)
    step_length = norm_now / curvature
    direction = precond
    image_dir = image_field
    for iteration in range(ITERS):
        pressure = pressure + step_length * direction
        residual = residual - step_length * image_dir
        if iteration + 1 < ITERS:
            precond = residual / diagonal
            image_field = operate(extend(precond), corner)
            norm_next, curvature = paired_dots(residual, precond, image_field)
            ratio_next = norm_next / norm_now
            step_length = norm_next / (curvature - ratio_next * norm_next / step_length)
            direction = precond + ratio_next * direction
            image_dir = image_field + ratio_next * image_dir
            norm_now = norm_next
    return (pressure, residual)


def shards(fields, level_count, thickness, old_pressure):
    levels = jnp.arange(thickness.shape[0], dtype=jnp.int32)[:, None, None]
    wet_mask = (levels < level_count[None]).astype(jnp.float32)
    weights = thickness[:, None, None] * wet_mask
    column_depth = jnp.sum(weights, axis=0)
    extended = padded(fields, (("by", 2), ("bx", 3)), 3)
    forcing_sum = jnp.sum(weights * level_divergence(extended), axis=0)
    ocean_mask = (level_count > 0).astype(jnp.float32)
    right_side = ocean_mask * (forcing_sum + IMPLICIT * old_pressure)
    first_guess = ocean_mask * old_pressure
    strip_side, strip_depth, strip_guess = (
        lax.all_to_all(right_side, "bx", split_axis=0, concat_axis=1, tiled=True),
        lax.all_to_all(column_depth, "bx", split_axis=0, concat_axis=1, tiled=True),
        lax.all_to_all(first_guess, "bx", split_axis=0, concat_axis=1, tiled=True),
    )
    strip_pressure, strip_residual = solve(strip_side, strip_depth, strip_guess, strip_extend)
    pressure, residual = (
        lax.all_to_all(strip_pressure, "bx", split_axis=1, concat_axis=0, tiled=True),
        lax.all_to_all(strip_residual, "bx", split_axis=1, concat_axis=0, tiled=True),
    )
    return (pressure, residual)


def solution(mesh):
    placed = (P(None, None, "by", "bx"), P("by", "bx"), P(), P("by", "bx"))
    return jax.shard_map(
        shards,
        mesh=mesh,
        in_specs=placed,
        out_specs=(P("by", "bx"), P("by", "bx")),
        check_vma=False,
    )
```

profile of v0, /device:TPU:0, one launch (start us, length us, event | category | flops | bytes accessed | tf_op | source)
XLA Modules:
  0.0 334.4 jit_solution(8251102713640462767)
XLA Ops:
  0.6 1.1 fusion.36
  1.7 0.5 collective-permute-start
  2.3 0.6 copy.58
  2.9 2.0 collective-permute-start.1
  4.9 6.7 %copy.48 = f32[3,8,256,256]{2,1,3,0:T(8,128)} copy(f32[3,8,256,256]{3,2,1,0:T(8,128)} %param.4) | data formatting | bytes 12582912 | tf_op args[0]
  11.7 0.8 copy.41
  12.5 1.1 copy.47
  13.7 2.6 copy.49
  16.3 1.9 pad_maximum_fusion.27
  18.2 2.3 collective-permute-start.2
  20.4 3.1 collective-permute-start.3
  23.6 0.8 copy.42
  24.4 4.2 %all-to-all-start = ((f32[8,32,256]{2,1,0:T(8,128)}), f32[8,32,256]{2,1,0:T(8,128)}, u32[]{:S(2)}, u32[]{:S(2)}) async-start(f32[8,32,256]{2,1,0:T(8,128)} %bitcast), calls=%async_computation | async-start | bytes 524288 | tf_op jit(solution)/shard_map/all_to_all | solution.py:126
  28.7 7.2 %pad_maximum_fusion = f32[3,8,262,262]{2,1,3,0:T(8,128)S(1)} fusion(f32[3,8,262,3]{2,1,3,0:T(8,128)S(1)} %collective-permute-done.3, f32[3,8,3,256]{2,1,3,0:T(8,128)} %copy.49, f32[3,8,256,256]{2,1,3,0:T(8,128)} %copy.48, f32[3,8,3,256]{2,1,3,0:T(8,128)} %copy-done, f32[3,8,262,3]{2,1,3,0:T(8,128)S(1)} %collective-permute-done.2), kind=kLoop, calls=%fused_computation | loop fusion | flops 6589824 | bytes 13179648 | tf_op jit(solution)/shard_map/concatenate | solution.py:22
  35.9 2.3 slice_bitcast_fusion.2
  38.2 7.0 %fusion = (f32[8,260,260]{1,0,2:T(8,128)S(1)}, f32[8,260,260]{1,0,2:T(8,128)S(1)}) fusion(f32[8,262,262]{1,0,2:T(8,128)S(1)} %get-tuple-element.54, f32[8,262,262]{1,0,2:T(8,128)S(1)} %get-tuple-element.53), kind=kLoop, calls=%fused_computation.5 | loop fusion | flops 5408000 | bytes 25958400 | tf_op jit(solution)/shard_map/sub | solution.py:28
  45.2 17.3 %fusion.7 = (f32[8,258,258]{1,0,2:T(8,128)}, f32[8,258,258]{1,0,2:T(8,128)}) fusion(f32[8,262,262]{1,0,2:T(8,128)} %get-tuple-element.55, f32[8,260,260]{1,0,2:T(8,128)S(1)} %get-tuple-element.85, f32[8,260,260]{1,0,2:T(8,128)S(1)} %get-tuple-element.84), kind=kLoop, calls=%fused_computation.25 | loop fusion | flops 9585216 | bytes 34080768 | tf_op jit(solution)/shard_map/sub | solution.py:40
  62.5 6.4 %fusion.10 = (f32[256,256]{0,1:T(8,128)S(1)}, f32[256,256]{0,1:T(8,128)S(1)}) fusion(f32[8,258,258]{1,0,2:T(8,128)} %get-tuple-element.59, f32[8,258,258]{1,0,2:T(8,128)} %get-tuple-element.58, f32[8]{0:T(128)S(1)} %copy-done.5, s32[256,256]{0,1:T(8,128)S(1)} %copy.40), kind=kLoop, calls=%fused_computation.34 | loop fusion | flops 4587520 | bytes 9175072 | tf_op jit(solution)/shard_map/reduce_sum | solution.py:119
  68.9 0.8 copy.53
  69.8 5.7 %all-to-all-start.2 = ((f32[8,32,256]{2,1,0:T(8,128)}), f32[8,32,256]{2,1,0:T(8,128)S(1)}, u32[]{:S(2)}, u32[]{:S(2)}) async-start(f32[8,32,256]{2,1,0:T(8,128)} %bitcast.7), calls=%async_computation.2 | async-start | bytes 524288 | tf_op jit(solution)/shard_map/all_to_all | solution.py:125
  75.5 0.8 copy.51
  76.4 1.0 copy.61
  77.4 0.9 fusion.42
  78.2 2.1 collective-permute-start.6
  80.3 3.3 collective-permute-start.7
  83.6 0.4 all-to-all-done.2
  84.1 3.5 %all-to-all-start.1 = ((f32[8,32,256]{2,1,0:T(8,128)}), f32[8,32,256]{2,1,0:T(8,128)S(1)}, u32[]{:S(2)}, u32[]{:S(2)}) async-start(f32[8,32,256]{2,1,0:T(8,128)} %bitcast.5), calls=%async_computation.1 | async-start | bytes 524288 | tf_op jit(solution)/shard_map/all_to_all | solution.py:124
  87.6 2.1 collective-permute-start.4
  89.7 3.3 collective-permute-start.5
  93.1 0.2 fusion.21
  93.3 3.0 all-to-all-done.1
  96.3 0.2 fusion.25
  96.5 0.3 add_multiply_fusion.4
  96.8 0.4 fusion.32
  97.2 1.5 collective-permute-start.8
  98.7 3.9 %collective-permute-start.9 = (f32[1,2048]{1,0:T(1,128)S(1)}, f32[1,2048]{1,0:T(1,128)S(1)}, u32[]{:S(2)}, u32[]{:S(2)}) collective-permute-start(f32[1,2048]{1,0:T(1,128)S(1)} %get-tuple-element.79), channel_id=1, source_target_pairs={{1,0},{2,1},{3,2},{4,3},{5,4},{6,5},{7,6},{8,7},{9,8},{10,9},{11,1... | collective-permute-start | bytes 24584 | tf_op jit(solution)/shard_map/ppermute | solution.py:21
  102.6 1.3 collective-permute-done.8
  104.0 0.2 fusion.19
  104.5 0.8 multiply_reduce_fusion.6
  105.3 39.7 %all-reduce.3 = (f32[]{:T(128)}, f32[]{:T(128)}) all-reduce(f32[]{:T(128)} %get-tuple-element.11, f32[]{:T(128)} %get-tuple-element.10), channel_id=1, replica_groups=mesh['by'=4,'bx'=8] {'by','bx'}, use_global_device_ids=true, to_apply=%region_3.4 | all-reduce | flops 2 | bytes 16 | tf_op jit(solution)/shard_map/psum | solution.py:82
  146.5 2.3 collective-permute-start.10
  148.8 3.1 collective-permute-start.11
  151.9 1.3 collective-permute-done.10
  153.7 0.9 multiply_reduce_fusion.4
  154.6 41.1 %all-reduce.2 = (f32[]{:T(128)}, f32[]{:T(128)}) all-reduce(f32[]{:T(128)} %get-tuple-element.9, f32[]{:T(128)} %get-tuple-element.8), channel_id=1, replica_groups=mesh['by'=4,'bx'=8] {'by','bx'}, use_global_device_ids=true, to_apply=%region_7.8 | all-reduce | flops 2 | bytes 16 | tf_op jit(solution)/shard_map/psum | solution.py:82
  200.5 2.3 collective-permute-start.12
  202.9 3.1 collective-permute-start.13
  205.9 1.3 collective-permute-done.12
  207.7 0.8 multiply_reduce_fusion.2
  208.6 40.8 %all-reduce.1 = (f32[]{:T(128)}, f32[]{:T(128)}) all-reduce(f32[]{:T(128)} %get-tuple-element.7, f32[]{:T(128)} %get-tuple-element.6), channel_id=1, replica_groups=mesh['by'=4,'bx'=8] {'by','bx'}, use_global_device_ids=true, to_apply=%region_11.12 | all-reduce | flops 2 | bytes 16 | tf_op jit(solution)/shard_map/psum | solution.py:82
  253.6 2.3 collective-permute-start.14
  255.9 3.1 collective-permute-start.15
  259.0 1.3 collective-permute-done.14
  260.3 0.2 fusion.13
  260.8 0.8 multiply_reduce_fusion
  261.6 41.1 %all-reduce = (f32[]{:T(128)}, f32[]{:T(128)}) all-reduce(f32[]{:T(128)} %get-tuple-element.5, f32[]{:T(128)} %get-tuple-element.4), channel_id=1, replica_groups=mesh['by'=4,'bx'=8] {'by','bx'}, use_global_device_ids=true, to_apply=%region_15.16 | all-reduce | flops 2 | bytes 16 | tf_op jit(solution)/shard_map/psum | solution.py:82
  306.9 0.7 copy.66
  307.6 5.6 %all-to-all-start.4 = ((f32[32,8,256]{2,0,1:T(8,128)}), f32[32,8,256]{2,0,1:T(8,128)S(1)}, u32[]{:S(2)}, u32[]{:S(2)}) async-start(f32[32,8,256]{2,0,1:T(8,128)} %bitcast.34), calls=%async_computation.4 | async-start | bytes 524288 | tf_op jit(solution)/shard_map/all_to_all | solution.py:131
  313.3 0.7 copy.67
  314.0 7.4 %all-to-all-done.4 = f32[32,8,256]{2,0,1:T(8,128)S(1)} async-done(((f32[32,8,256]{2,0,1:T(8,128)}), f32[32,8,256]{2,0,1:T(8,128)S(1)}, u32[]{:S(2)}, u32[]{:S(2)}) %all-to-all-start.4) | async-done | bytes 262176 | tf_op jit(solution)/shard_map/all_to_all | solution.py:131
  321.4 3.4 %all-to-all-start.3 = ((f32[32,8,256]{2,0,1:T(8,128)}), f32[32,8,256]{2,0,1:T(8,128)S(1)}, u32[]{:S(2)}, u32[]{:S(2)}) async-start(f32[32,8,256]{2,0,1:T(8,128)} %bitcast.35), calls=%async_computation.3 | async-start | bytes 524288 | tf_op jit(solution)/shard_map/all_to_all | solution.py:130
  324.8 8.2 %all-to-all-done.3 = f32[32,8,256]{2,0,1:T(8,128)S(1)} async-done(((f32[32,8,256]{2,0,1:T(8,128)}), f32[32,8,256]{2,0,1:T(8,128)S(1)}, u32[]{:S(2)}, u32[]{:S(2)}) %all-to-all-start.3) | async-done | bytes 262176 | tf_op jit(solution)/shard_map/all_to_all | solution.py:130
  333.0 0.7 copy.70
  333.7 0.7 copy.71
  (52 shorter events, 2.4 us)
Async XLA Ops:
  1.7 10.8 %collective-permute-start = (f32[3,8,3,256]{3,1,2,0:T(8,128)S(1)}, f32[3,8,3,256]{3,1,2,0:T(8,128)S(1)}, u32[]{:S(2)}, u32[]{:S(2)}) collective-permute-start(f32[3,8,3,256]{3,1,2,0:T(8,128)S(1)} %copy.57), channel_id=1, source_target_pairs={{0,8},{8,16},{16,24},{24,0},{1,9},{9,17},{17,25},{25,1},{2,10},{10... | collective-permute-start | bytes 221192 | tf_op jit(solution)/shard_map/ppermute | solution.py:20
  2.9 8.6 %copy-start.3 = (s32[256,256]{1,0:T(8,128)S(1)}, s32[256,256]{1,0:T(8,128)}, u32[]{:S(2)}) copy-start(s32[256,256]{1,0:T(8,128)} %param.5) | copy-start | bytes 786436
  2.9 8.8 %copy-start.4 = (f32[256,256]{1,0:T(8,128)S(1)}, f32[256,256]{1,0:T(8,128)}, u32[]{:S(2)}) copy-start(f32[256,256]{1,0:T(8,128)} %param.7) | copy-start | bytes 786436
  2.9 10.7 %collective-permute-start.1 = (f32[3,8,3,256]{3,1,2,0:T(8,128)}, f32[3,8,3,256]{3,1,2,0:T(8,128)S(1)}, u32[]{:S(2)}, u32[]{:S(2)}) collective-permute-start(f32[3,8,3,256]{3,1,2,0:T(8,128)} %copy.58), channel_id=1, source_target_pairs={{8,0},{16,8},{24,16},{0,24},{9,1},{17,9},{25,17},{1,25},{10,2},{18... | collective-permute-start | bytes 221192 | tf_op jit(solution)/shard_map/ppermute | solution.py:21
  13.6 4.5 %copy-start = (f32[3,8,3,256]{2,1,3,0:T(8,128)}, f32[3,8,3,256]{2,1,3,0:T(8,128)S(1)}, u32[]{:S(2)}) copy-start(f32[3,8,3,256]{2,1,3,0:T(8,128)S(1)} %copy.47) | copy-start | bytes 221188
  16.3 7.2 %copy-start.1 = (f32[256,256]{0,1:T(8,128)S(1)}, f32[256,256]{0,1:T(8,128)}, u32[]{:S(2)}) copy-start(f32[256,256]{0,1:T(8,128)} %copy.41) | copy-start | bytes 786436
  18.2 10.5 %collective-permute-start.2 = (f32[3,8,262,3]{2,1,3,0:T(8,128)}, f32[3,8,262,3]{2,1,3,0:T(8,128)S(1)}, u32[]{:S(2)}, u32[]{:S(2)}) collective-permute-start(f32[3,8,262,3]{2,1,3,0:T(8,128)} %get-tuple-element.51), channel_id=1, source_target_pairs={{0,1},{1,2},{2,3},{3,4},{4,5},{5,6},{6,7},{7,0},{8,9},{9,10},{10,1... | collective-permute-start | bytes 226376 | tf_op jit(solution)/shard_map/ppermute | solution.py:20
  20.4 8.2 %collective-permute-start.3 = (f32[3,8,262,3]{2,1,3,0:T(8,128)}, f32[3,8,262,3]{2,1,3,0:T(8,128)S(1)}, u32[]{:S(2)}, u32[]{:S(2)}) collective-permute-start(f32[3,8,262,3]{2,1,3,0:T(8,128)} %get-tuple-element.52), channel_id=1, source_target_pairs={{1,0},{2,1},{3,2},{4,3},{5,4},{6,5},{7,6},{0,7},{9,8},{10,9},{11,1... | collective-permute-start | bytes 226376 | tf_op jit(solution)/shard_map/ppermute | solution.py:21
  24.4 45.4 %all-to-all-start = ((f32[8,32,256]{2,1,0:T(8,128)}), f32[8,32,256]{2,1,0:T(8,128)}, u32[]{:S(2)}, u32[]{:S(2)}) async-start(f32[8,32,256]{2,1,0:T(8,128)} %bitcast), calls=%async_computation | async-start | bytes 524288 | tf_op jit(solution)/shard_map/all_to_all | solution.py:126
  45.2 17.3 %copy-start.5 = (f32[8]{0:T(128)S(1)}, f32[8]{0:T(128)}, u32[]{:S(2)}) copy-start(f32[8]{0:T(128)} %param.6) | copy-start | bytes 100
  62.5 13.0 %copy-start.2 = (f32[256,256]{0,1:T(8,128)S(1)}, f32[256,256]{0,1:T(8,128)}, u32[]{:S(2)}) copy-start(f32[256,256]{0,1:T(8,128)} %copy.41) | copy-start | bytes 786436
  69.8 14.3 %all-to-all-start.2 = ((f32[8,32,256]{2,1,0:T(8,128)}), f32[8,32,256]{2,1,0:T(8,128)S(1)}, u32[]{:S(2)}, u32[]{:S(2)}) async-start(f32[8,32,256]{2,1,0:T(8,128)} %bitcast.7), calls=%async_computation.2 | async-start | bytes 524288 | tf_op jit(solution)/shard_map/all_to_all | solution.py:125
  78.2 14.8 %collective-permute-start.6 = (f32[1,2048]{1,0:T(1,128)S(1)}, f32[1,2048]{1,0:T(1,128)S(1)}, u32[]{:S(2)}, u32[]{:S(2)}) collective-permute-start(f32[1,2048]{1,0:T(1,128)S(1)} %bitcast.50), channel_id=1, source_target_pairs={{0,1},{1,2},{2,3},{3,4},{4,5},{5,6},{6,7},{7,8},{8,9},{9,10},{10,1... | collective-permute-start | bytes 24584 | tf_op jit(solution)/shard_map/ppermute | solution.py:20
  80.3 12.7 %collective-permute-start.7 = (f32[1,2048]{1,0:T(1,128)S(1)}, f32[1,2048]{1,0:T(1,128)S(1)}, u32[]{:S(2)}, u32[]{:S(2)}) collective-permute-start(f32[1,2048]{1,0:T(1,128)S(1)} %bitcast.48), channel_id=1, source_target_pairs={{1,0},{2,1},{3,2},{4,3},{5,4},{6,5},{7,6},{8,7},{9,8},{10,9},{11,1... | collective-permute-start | bytes 24584 | tf_op jit(solution)/shard_map/ppermute | solution.py:21
  84.1 12.2 %all-to-all-start.1 = ((f32[8,32,256]{2,1,0:T(8,128)}), f32[8,32,256]{2,1,0:T(8,128)S(1)}, u32[]{:S(2)}, u32[]{:S(2)}) async-start(f32[8,32,256]{2,1,0:T(8,128)} %bitcast.5), calls=%async_computation.1 | async-start | bytes 524288 | tf_op jit(solution)/shard_map/all_to_all | solution.py:124
  87.6 8.6 %collective-permute-start.4 = (f32[1,2048]{1,0:T(1,128)S(1)}, f32[1,2048]{1,0:T(1,128)S(1)}, u32[]{:S(2)}, u32[]{:S(2)}) collective-permute-start(f32[1,2048]{1,0:T(1,128)S(1)} %bitcast.51), channel_id=1, source_target_pairs={{0,1},{1,2},{2,3},{3,4},{4,5},{5,6},{6,7},{7,8},{8,9},{9,10},{10,1... | collective-permute-start | bytes 24584 | tf_op jit(solution)/shard_map/ppermute | solution.py:20
  89.7 6.6 %collective-permute-start.5 = (f32[1,2048]{1,0:T(1,128)S(1)}, f32[1,2048]{1,0:T(1,128)S(1)}, u32[]{:S(2)}, u32[]{:S(2)}) collective-permute-start(f32[1,2048]{1,0:T(1,128)S(1)} %bitcast.49), channel_id=1, source_target_pairs={{1,0},{2,1},{3,2},{4,3},{5,4},{6,5},{7,6},{8,7},{9,8},{10,9},{11,1... | collective-permute-start | bytes 24584 | tf_op jit(solution)/shard_map/ppermute | solution.py:21
  97.2 6.7 %collective-permute-start.8 = (f32[1,2048]{1,0:T(1,128)S(1)}, f32[1,2048]{1,0:T(1,128)S(1)}, u32[]{:S(2)}, u32[]{:S(2)}) collective-permute-start(f32[1,2048]{1,0:T(1,128)S(1)} %get-tuple-element.78), channel_id=1, source_target_pairs={{0,1},{1,2},{2,3},{3,4},{4,5},{5,6},{6,7},{7,8},{8,9},{9,10},{10,1... | collective-permute-start | bytes 24584 | tf_op jit(solution)/shard_map/ppermute | solution.py:20
  98.7 5.3 %collective-permute-start.9 = (f32[1,2048]{1,0:T(1,128)S(1)}, f32[1,2048]{1,0:T(1,128)S(1)}, u32[]{:S(2)}, u32[]{:S(2)}) collective-permute-start(f32[1,2048]{1,0:T(1,128)S(1)} %get-tuple-element.79), channel_id=1, source_target_pairs={{1,0},{2,1},{3,2},{4,3},{5,4},{6,5},{7,6},{8,7},{9,8},{10,9},{11,1... | collective-permute-start | bytes 24584 | tf_op jit(solution)/shard_map/ppermute | solution.py:21
  146.5 6.7 %collective-permute-start.10 = (f32[1,2048]{1,0:T(1,128)S(1)}, f32[1,2048]{1,0:T(1,128)S(1)}, u32[]{:S(2)}, u32[]{:S(2)}) collective-permute-start(f32[1,2048]{1,0:T(1,128)S(1)} %get-tuple-element.76), channel_id=1, source_target_pairs={{0,1},{1,2},{2,3},{3,4},{4,5},{5,6},{6,7},{7,8},{8,9},{9,10},{10,1... | collective-permute-start | bytes 24584 | tf_op jit(solution)/shard_map/ppermute | solution.py:20
  148.8 4.4 %collective-permute-start.11 = (f32[1,2048]{1,0:T(1,128)S(1)}, f32[1,2048]{1,0:T(1,128)S(1)}, u32[]{:S(2)}, u32[]{:S(2)}) collective-permute-start(f32[1,2048]{1,0:T(1,128)S(1)} %get-tuple-element.77), channel_id=1, source_target_pairs={{1,0},{2,1},{3,2},{4,3},{5,4},{6,5},{7,6},{8,7},{9,8},{10,9},{11,1... | collective-permute-start | bytes 24584 | tf_op jit(solution)/shard_map/ppermute | solution.py:21
  200.5 6.7 %collective-permute-start.12 = (f32[1,2048]{1,0:T(1,128)S(1)}, f32[1,2048]{1,0:T(1,128)S(1)}, u32[]{:S(2)}, u32[]{:S(2)}) collective-permute-start(f32[1,2048]{1,0:T(1,128)S(1)} %get-tuple-element.74), channel_id=1, source_target_pairs={{0,1},{1,2},{2,3},{3,4},{4,5},{5,6},{6,7},{7,8},{8,9},{9,10},{10,1... | collective-permute-start | bytes 24584 | tf_op jit(solution)/shard_map/ppermute | solution.py:20
  202.9 4.4 %collective-permute-start.13 = (f32[1,2048]{1,0:T(1,128)S(1)}, f32[1,2048]{1,0:T(1,128)S(1)}, u32[]{:S(2)}, u32[]{:S(2)}) collective-permute-start(f32[1,2048]{1,0:T(1,128)S(1)} %get-tuple-element.75), channel_id=1, source_target_pairs={{1,0},{2,1},{3,2},{4,3},{5,4},{6,5},{7,6},{8,7},{9,8},{10,9},{11,1... | collective-permute-start | bytes 24584 | tf_op jit(solution)/shard_map/ppermute | solution.py:21
  253.6 6.7 %collective-permute-start.14 = (f32[1,2048]{1,0:T(1,128)S(1)}, f32[1,2048]{1,0:T(1,128)S(1)}, u32[]{:S(2)}, u32[]{:S(2)}) collective-permute-start(f32[1,2048]{1,0:T(1,128)S(1)} %get-tuple-element.72), channel_id=1, source_target_pairs={{0,1},{1,2},{2,3},{3,4},{4,5},{5,6},{6,7},{7,8},{8,9},{9,10},{10,1... | collective-permute-start | bytes 24584 | tf_op jit(solution)/shard_map/ppermute | solution.py:20
  255.9 4.4 %collective-permute-start.15 = (f32[1,2048]{1,0:T(1,128)S(1)}, f32[1,2048]{1,0:T(1,128)S(1)}, u32[]{:S(2)}, u32[]{:S(2)}) collective-permute-start(f32[1,2048]{1,0:T(1,128)S(1)} %get-tuple-element.73), channel_id=1, source_target_pairs={{1,0},{2,1},{3,2},{4,3},{5,4},{6,5},{7,6},{8,7},{9,8},{10,9},{11,1... | collective-permute-start | bytes 24584 | tf_op jit(solution)/shard_map/ppermute | solution.py:21
  307.6 13.8 %all-to-all-start.4 = ((f32[32,8,256]{2,0,1:T(8,128)}), f32[32,8,256]{2,0,1:T(8,128)S(1)}, u32[]{:S(2)}, u32[]{:S(2)}) async-start(f32[32,8,256]{2,0,1:T(8,128)} %bitcast.34), calls=%async_computation.4 | async-start | bytes 524288 | tf_op jit(solution)/shard_map/all_to_all | solution.py:131
  321.4 11.6 %all-to-all-start.3 = ((f32[32,8,256]{2,0,1:T(8,128)}), f32[32,8,256]{2,0,1:T(8,128)S(1)}, u32[]{:S(2)}, u32[]{:S(2)}) async-start(f32[32,8,256]{2,0,1:T(8,128)} %bitcast.35), calls=%async_computation.3 | async-start | bytes 524288 | tf_op jit(solution)/shard_map/all_to_all | solution.py:130
where the time goes:
time: 336 us; the launch traced here: 334 us
  blocking collectives  163 us (49%)
  starting transfers between devices  62.7 us (19%)
  other arithmetic  46.6 us (14%)
  waiting for transfers between devices  24.4 us (7%)
  local copies, waits for them, and re-layouts  22.7 us (7%)
  between operations  15.1 us (4%)
    psum x4, blocking collectives, paired_dots(): lax.psum((jnp.sum(residual * precond), jnp.sum(precond * image_field)), (...  163 us
    ppermute x8, starting transfers between devices, padded(): after = lax.ppermute(initial, axis, down)  24.8 us
    sub x1, other arithmetic, level_divergence(): -VISCOSITY * laplace(laplace(zonal))  17.3 us
    ppermute x8, starting transfers between devices, padded(): before = lax.ppermute(last, axis, up)  15.5 us
    unnamed x19, local copies, waits for them, and re-layouts  9.72 us
    all_to_all x1, waiting for transfers between devices, shards(): lax.all_to_all(strip_pressure, 'bx', split_axis=1, concat_axis=0, tiled=T...  8.16 us
    all_to_all x1, waiting for transfers between devices, shards(): lax.all_to_all(strip_residual, 'bx', split_axis=1, concat_axis=0, tiled=T...  7.37 us
    concatenate x1, other arithmetic, padded(): array = jnp.concatenate([before, array, after], axis=dim)  7.22 us
  transfers between devices with their start and end apart: 21, of which 8 were waited for; matrix products, arithmetic and copies ran while one was open for 16% of the time, Pallas kernels for 0%

commit v1 on v0

v1 whole, which is shorter than its diff:
```python
import functools

import jax
import jax.numpy as jnp
from jax import lax
from jax.experimental import pallas as pl
from jax.experimental.pallas import tpu as pltpu
from jax.sharding import PartitionSpec as P

ITERS = 4
VISCOSITY = 0.05
IMPLICIT = 0.05

ROWS = 8
PAD = 8
LANES = 128
REACH = 3
DEEP = ITERS
EDGE = ITERS + 1

OUT_AT = 0
VMEM = pltpu.VMEM


def message_rows(levels):
    forcing_at = REACH * levels
    count_at = forcing_at + DEEP
    pressure_at = count_at + EDGE
    total = pressure_at + EDGE
    return forcing_at, count_at, pressure_at, -(-total // 8) * 8


def east(value):
    return pltpu.roll(value, value.shape[1] - 1, 1)


def west(value):
    return pltpu.roll(value, 1, 1)


def lane_index(rows):
    return lax.broadcasted_iota(jnp.int32, (rows, LANES), 1)


def forcing_kernel(
    thick, fields, south, north, count, old, part, depth, guess, to_east, to_west,
    zonal, merid, baro, mixed, lap, wet, pack_e, pack_w,
):
    level = pl.program_id(0)
    levels = pl.num_programs(0)
    static_levels = (south.shape[0] - 2) // 3
    height, width = count.shape
    ext = height + 2 * ROWS
    full = width + LANES
    base = PAD + ROWS
    forcing_at, count_at, pressure_at, _ = message_rows(static_levels)

    @pl.when(level == 0)
    def _():
        for buf in (zonal, merid, baro):
            buf[:, width:] = jnp.zeros((ext + 2 * PAD, LANES), jnp.float32)
        for buf in (zonal, merid, baro, mixed, lap):
            buf[:PAD, :] = jnp.zeros((PAD, full), jnp.float32)
            buf[PAD + ext :, :] = jnp.zeros((PAD, full), jnp.float32)
        part[...] = jnp.zeros_like(part)
        depth[...] = jnp.zeros_like(depth)
        pack_e[...] = jnp.zeros_like(pack_e)
        pack_w[...] = jnp.zeros_like(pack_w)
        wet[:ROWS, :] = south[3 * static_levels]
        wet[ROWS : ROWS + height, :] = count[...].astype(jnp.float32)
        wet[ROWS + height :, :] = north[3 * static_levels]

    for which, buf in enumerate((zonal, merid, baro)):
        buf[PAD:base, :width] = south[which * static_levels + level]
        buf[base : base + height, :width] = fields[which, 0]
        buf[base + height : base + height + ROWS, :width] = north[which * static_levels + level]

    step = 8
    starts = range(PAD, PAD + ext, step)
    for r in starts:
        row = zonal[r : r + step, :]
        up = merid[r + 1 : r + 1 + step, :]
        down = merid[r - 1 : r - 1 + step, :]
        mixed[r : r + step, :] = (east(row) - west(row)) + (up - down)
    for r in starts:
        row = mixed[r : r + step, :]
        lap[r : r + step, :] = (
            (east(row) + west(row))
            + (mixed[r + 1 : r + 1 + step, :] + mixed[r - 1 : r - 1 + step, :])
            - 4.0 * row
        )
    thickness = thick[level]
    level_number = level.astype(jnp.float32)
    lane = lane_index(step)
    for r in starts:
        row = lap[r : r + step, :]
        second = (
            (east(row) + west(row))
            + (lap[r + 1 : r + 1 + step, :] + lap[r - 1 : r - 1 + step, :])
            - 4.0 * row
        )
        centre = baro[r : r + step, :]
        spread = (
            (pltpu.roll(centre, full - 2, 1) + pltpu.roll(centre, 2, 1))
            + (baro[r + 2 : r + 2 + step, :] + baro[r - 2 : r - 2 + step, :])
            - 4.0 * centre
        )
        div = (-0.5 * VISCOSITY) * second - 0.25 * spread
        e = r - PAD
        weight = jnp.where(wet[e : e + step, :] > level_number, thickness, 0.0)
        part[e : e + step, :] += weight * div[:, :width]
        depth[e : e + step, :] += weight
        outside = div[:, width:]
        going_east = jnp.where(lane < REACH, outside, 0.0)
        going_west = jnp.where(lane >= LANES - REACH, outside, 0.0)
        pack_e[e : e + step, :] += pltpu.roll(going_east, REACH * level, 1)
        pack_w[e : e + step, :] += pltpu.roll(going_west, REACH * level + REACH, 1)

    @pl.when(level == levels - 1)
    def _():
        for e in range(0, ext, step):
            if e < ROWS:
                pressure = south[3 * static_levels + 1]
            elif e >= ROWS + height:
                pressure = north[3 * static_levels + 1]
            else:
                pressure = old[e - ROWS : e - ROWS + step, :]
            start = jnp.where(depth[e : e + step, :] > 0.0, pressure, 0.0)
            guess[e : e + step, :] = start
            for pack, at, inner in ((pack_e, width - LANES, True), (pack_w, 0, False)):
                tile = pack[e : e + step, :]
                pieces = (
                    (part[e : e + step, at : at + LANES], forcing_at, DEEP),
                    (wet[e : e + step, at : at + LANES], count_at, EDGE),
                    (start[:, at : at + LANES], pressure_at, EDGE),
                )
                for piece, lane_at, size in pieces:
                    shift = lane_at + size if inner else lane_at
                    moved = pltpu.roll(piece, shift, 1)
                    inside = (lane >= lane_at) & (lane < lane_at + size)
                    tile = jnp.where(inside, moved, tile)
                pack[e : e + step, :] = tile
        for pack, message in ((pack_e, to_east), (pack_w, to_west)):
            for at in range(0, message.shape[1], LANES):
                turned = jnp.transpose(pack[at : at + LANES, :])
                message[:, at : at + LANES] = turned[: message.shape[0], :]


def solve_kernel(
    thick, part, depth, guess, to_east, to_west, from_west, from_east,
    base0, base1, base2, base3, base4, diag_out, moments,
    turned, deep, start, half, half_w, diag, inverse, right, vec_a, vec_b,
):
    ext, width = part.shape
    height = ext - 2 * ROWS
    full = width + LANES
    levels = thick.shape[0]
    forcing_at, count_at, pressure_at, _ = message_rows(levels)

    def weights(counts):
        return [jnp.where(counts > float(k), thick[k], 0.0) for k in range(levels)]

    def weighted(counts, message):
        total = None
        for k, weight in enumerate(weights(counts)):
            term = weight * message[REACH * k : REACH * k + REACH, :]
            total = term if total is None else total + term
        return total

    def rows(message, at, size):
        return message[at : at + size, :]

    skip = EDGE - REACH
    turned[...] = jnp.zeros_like(turned)
    edge_forcing = rows(from_east, forcing_at, DEEP)
    turned[0:DEEP, :] = edge_forcing
    turned[0:REACH, :] += weighted(rows(from_east, count_at, REACH), to_east)
    turned[LANES - DEEP : LANES, :] = rows(from_west, forcing_at, DEEP)
    turned[LANES - REACH : LANES, :] += weighted(rows(from_west, count_at + skip, REACH), to_west)
    turned[40 : 40 + EDGE, :] = sum(weights(rows(from_east, count_at, EDGE)))
    turned[40 - EDGE : 40, :] = sum(weights(rows(from_west, count_at, EDGE)))
    turned[60 : 60 + EDGE, :] = rows(from_east, pressure_at, EDGE)
    turned[60 - EDGE : 60, :] = rows(from_west, pressure_at, EDGE)
    turned[80 : 80 + REACH, :] = weighted(rows(to_west, count_at, REACH), from_west)
    turned[80 - REACH : 80, :] = weighted(rows(to_east, count_at + skip, REACH), from_east)

    step = 8
    lane = lane_index(step)
    for buf in (deep, start, half, half_w, vec_a, vec_b):
        buf[:PAD, :] = jnp.zeros((PAD, full), jnp.float32)
        buf[PAD + ext :, :] = jnp.zeros((PAD, full), jnp.float32)
    for at in range(0, ext, LANES):
        block = jnp.transpose(turned[:, at : at + LANES])
        for e in range(at, min(at + LANES, ext), step):
            r = e + PAD
            tile = block[e - at : e - at + step, :]
            near = (lane < EDGE) | (lane >= LANES - EDGE)
            deep[r : r + step, :width] = depth[e : e + step, :]
            deep[r : r + step, width:] = jnp.where(near, pltpu.roll(tile, LANES - 40, 1), 0.0)
            start[r : r + step, :width] = guess[e : e + step, :]
            start[r : r + step, width:] = jnp.where(near, pltpu.roll(tile, LANES - 60, 1), 0.0)
            fix = pltpu.roll(tile, LANES - 80, 1)
            right[e : e + step, :width] = part[e : e + step, :]
            right[e : e + step, :LANES] += jnp.where(lane < REACH, fix, 0.0)
            right[e : e + step, width - LANES : width] += jnp.where(lane >= LANES - REACH, fix, 0.0)
            close = (lane < DEEP) | (lane >= LANES - DEEP)
            right[e : e + step, width:] = jnp.where(close, tile, 0.0)

    starts = range(PAD, PAD + ext, step)
    for r in starts:
        here = deep[r : r + step, :]
        above = deep[r + 1 : r + 1 + step, :]
        low = jnp.minimum(here, above)
        corner = 0.5 * jnp.minimum(low, east(low))
        half[r : r + step, :] = corner
        half_w[r : r + step, :] = west(corner)

    for r in starts:
        e = r - PAD
        ch = half[r : r + step, :]
        chw = half_w[r : r + step, :]
        ch_s = half[r - 1 : r - 1 + step, :]
        chw_s = half_w[r - 1 : r - 1 + step, :]
        diagonal = IMPLICIT + ((ch + chw) + (ch_s + chw_s))
        inv = 1.0 / diagonal
        diag[e : e + step, :] = diagonal
        inverse[e : e + step, :] = inv
        here = start[r : r + step, :]
        up = start[r + 1 : r + 1 + step, :]
        down = start[r - 1 : r - 1 + step, :]
        image = IMPLICIT * here + (
            (ch * (here - east(up)) + chw * (here - west(up)))
            + (ch_s * (here - east(down)) + chw_s * (here - west(down)))
        )
        side = jnp.where(
            deep[r : r + step, :] > 0.0, right[e : e + step, :] + IMPLICIT * here, 0.0
        )
        vec_a[r : r + step, :] = (side - image) * inv

    outs = (base0, base1, base2, base3, base4)
    for r in starts:
        e = r - PAD
        if ROWS <= e < ROWS + height:
            o = e - ROWS
            base0[o : o + step, :] = vec_a[r : r + step, :width]
            diag_out[o : o + step, :] = diag[e : e + step, :width]
    buffers = (vec_a, vec_b)
    sums = []
    for j in range(ITERS):
        source, target = buffers[j % 2], buffers[(j + 1) % 2]
        even = jnp.zeros((step, LANES), jnp.float32)
        odd = jnp.zeros((step, LANES), jnp.float32)
        for r in starts:
            e = r - PAD
            up = source[r + 1 : r + 1 + step, :]
            down = source[r - 1 : r - 1 + step, :]
            value = inverse[e : e + step, :] * (
                (half[r : r + step, :] * east(up) + half_w[r : r + step, :] * west(up))
                + (
                    half[r - 1 : r - 1 + step, :] * east(down)
                    + half_w[r - 1 : r - 1 + step, :] * west(down)
                )
            )
            target[r : r + step, :] = value
            if ROWS <= e < ROWS + height:
                o = e - ROWS
                inner = value[:, :width]
                outs[j + 1][o : o + step, :] = inner
                now = source[r : r + step, :width]
                scaled = diag[e : e + step, :width] * now
                first = scaled * now
                second = scaled * inner
                for at in range(0, width, LANES):
                    even = even + first[:, at : at + LANES]
                    odd = odd + second[:, at : at + LANES]
        sums += [even, odd]
    lane_row = lax.broadcasted_iota(jnp.int32, (1, LANES), 1)
    found = jnp.zeros((1, LANES), jnp.float32)
    for m, acc in enumerate(sums):
        found = jnp.where(lane_row == m, jnp.sum(acc), found)
    for d in range(moments.shape[0]):
        moments[d] = found


def combine_kernel(moments, guess, base0, base1, base2, base3, base4, diag, pressure, residual):
    height, width = pressure.shape
    step = 8
    total = jnp.sum(moments[...], axis=0)
    shape = (step, width)
    h = [jnp.broadcast_to(total[:, m : m + 1], (step, LANES)) for m in range(2 * ITERS)]
    one, zero = jnp.ones((step, LANES), jnp.float32), None

    def plus(a, b):
        return b if a is None else a if b is None else a + b

    def times(a, b):
        return None if a is None or b is None else a * b

    def minus_n(poly):
        moved = [zero] + list(poly)
        return [
            a if b is None else (-b if a is None else a - b)
            for a, b in zip(list(poly) + [zero], moved)
        ]

    def inner(left, right):
        total = None
        for i, a in enumerate(left):
            part = None
            for j, b in enumerate(right):
                part = plus(part, times(b, h[i + j]))
            total = plus(total, times(a, part))
        return total

    rest, direction, answer = [one], [one], []
    norm = h[0]
    for iteration in range(ITERS):
        image = minus_n(direction)
        alpha = norm / inner(direction, image)
        answer = [
            plus(answer[i] if i < len(answer) else None, alpha * c)
            for i, c in enumerate(direction)
        ]
        rest = [
            plus(rest[i] if i < len(rest) else None, -(alpha * c)) for i, c in enumerate(image)
        ]
        if iteration + 1 < ITERS:
            following = inner(rest, rest)
            ratio = following / norm
            direction = [
                plus(c, ratio * direction[i] if i < len(direction) else None)
                for i, c in enumerate(rest)
            ]
            norm = following
    spread = lambda c: jnp.broadcast_to(c[:1, :1], shape)
    answer = [spread(c) for c in answer]
    rest = [spread(c) for c in rest]
    bases = (base0, base1, base2, base3, base4)
    for o in range(0, height, step):
        vecs = [b[o : o + step, :] for b in bases]
        moved = sum(c * v for c, v in zip(answer, vecs))
        left = sum(c * v for c, v in zip(rest, vecs))
        pressure[o : o + step, :] = guess[ROWS + o : ROWS + o + step, :] + moved
        residual[o : o + step, :] = diag[o : o + step, :] * left


def shift(value, axis, by):
    size = lax.axis_size(axis)
    return lax.ppermute(value, axis, [(i, (i + by) % size) for i in range(size)])


def shards(fields, level_count, thickness, old_pressure):
    levels, height, width = fields.shape[1:]
    ext, full, tall = height + 2 * ROWS, width + LANES, height + LANES
    f32 = jnp.float32
    counts = level_count.astype(f32)

    def edge(at):
        pick = lambda a: lax.slice_in_dim(a, at, at + ROWS, axis=a.ndim - 2)
        flat = pick(fields).reshape(3 * levels, ROWS, width)
        return jnp.concatenate([flat, pick(counts)[None], pick(old_pressure)[None]], axis=0)

    south = shift(edge(height - ROWS), "by", 1)
    north = shift(edge(0), "by", -1)

    message = message_rows(levels)[3]
    smem = pl.BlockSpec(memory_space=pltpu.SMEM)
    whole = lambda *dims: pl.BlockSpec(dims, lambda k: (0,) * len(dims))
    halo = whole(3 * levels + 2, ROWS, width)
    block = whole(ext, width)
    scratch = lambda r, c: pltpu.VMEM((r, c), f32)
    part, depth, guess, to_east, to_west = pl.pallas_call(
        forcing_kernel,
        grid=(levels,),
        in_specs=[
            smem,
            pl.BlockSpec((3, 1, height, width), lambda k: (0, k, 0, 0)),
            halo, halo, whole(height, width), whole(height, width),
        ],
        out_specs=[block, block, block, whole(message, tall), whole(message, tall)],
        out_shape=[jax.ShapeDtypeStruct((ext, width), f32)] * 3
        + [jax.ShapeDtypeStruct((message, tall), f32)] * 2,
        scratch_shapes=[scratch(ext + 2 * PAD, full)] * 5
        + [scratch(ext, width)]
        + [scratch(tall, LANES)] * 2,
        name="forcing",
    )(thickness, fields, south, north, level_count, old_pressure)

    from_west = shift(to_east, "bx", 1)
    from_east = shift(to_west, "bx", -1)

    devices = lax.axis_size("by") * lax.axis_size("bx")
    vmem = pl.BlockSpec(memory_space=pltpu.VMEM)
    out = jax.ShapeDtypeStruct((height, width), f32)
    *bases, diag, moments = pl.pallas_call(
        solve_kernel,
        in_specs=[smem] + [vmem] * 7,
        out_specs=[vmem] * (ITERS + 3),
        out_shape=[out] * (ITERS + 2) + [jax.ShapeDtypeStruct((devices, 1, LANES), f32)],
        scratch_shapes=[scratch(LANES, tall)]
        + [scratch(ext + 2 * PAD, full)] * 4
        + [scratch(ext, full)] * 3
        + [scratch(ext + 2 * PAD, full)] * 2,
        name="krylov",
    )(thickness, part, depth, guess, to_east, to_west, from_west, from_east)

    moments = lax.all_to_all(moments, ("by", "bx"), split_axis=0, concat_axis=0, tiled=True)
    return tuple(
        pl.pallas_call(
            combine_kernel,
            in_specs=[vmem] * (ITERS + 4),
            out_specs=[vmem] * 2,
            out_shape=[out] * 2,
            name="combine",
        )(moments, guess, *bases, diag)
    )


def solution(mesh):
    placed = (P(None, None, "by", "bx"), P("by", "bx"), P(), P("by", "bx"))
    return jax.shard_map(
        shards,
        mesh=mesh,
        in_specs=placed,
        out_specs=(P("by", "bx"), P("by", "bx")),
        check_vma=False,
    )
```

time: 336 us -> 72.5 us (0.22)
  blocking collectives: 163 us -> 14.1 us
  starting transfers between devices: 62.7 us -> 7.28 us
  other arithmetic: 46.6 us -> 1 us
  Pallas kernels: 0 us -> 37.5 us
  local copies, waits for them, and re-layouts: 22.7 us -> 3.1 us
  waiting for transfers between devices: 24.4 us -> 8.51 us
  between operations: 15.1 us -> 0.65 us
    psum x4 -> x0, blocking collectives: 163 us -> none  [paired_dots(): lax.psum((jnp.sum(residual * precond), jnp.sum(precond * image_field)), (...]
    pallas_call x0 -> x3, Pallas kernels: none -> 37.5 us  [the longest x1 27.8 us: shards(): pl.pallas_call(forcing_kernel, grid=(levels,), in_specs=[smem, pl.BlockSp...]
    ppermute x16 -> x4, starting transfers between devices: 40.3 us -> 7.28 us  [shift(): lax.ppermute(value, axis, [(i, (i + by) % size) for i in range(size)])]
    sub x3 -> x0, other arithmetic: 24.4 us -> none  [the longest x1 17.3 us: level_divergence(): -VISCOSITY * laplace(laplace(zonal))]
    all_to_all x5 -> x0, starting transfers between devices: 22.5 us -> none  [the longest x1 5.72 us: shards(): lax.all_to_all(column_depth, 'bx', split_axis=0, concat_axis=1, tiled=True)]
    all_to_all x5 -> x0, waiting for transfers between devices: 18.9 us -> none  [the longest x1 8.16 us: shards(): lax.all_to_all(strip_pressure, 'bx', split_axis=1, concat_axis=0, tiled=T...]
    all_to_all x0 -> x1, blocking collectives: none -> 14.1 us  [shards(): lax.all_to_all(moments, ('by', 'bx'), split_axis=0, concat_axis=0, tiled=...]
    reduce_sum x5 -> x0, other arithmetic: 9.82 us -> none  [the longest x1 6.41 us: shards(): forcing_sum = jnp.sum(weights * level_divergence(extended), axis=0)]
  transfers between devices with their start and end apart: 21 -> 4, of which waited for: 8 -> 3; matrix products, arithmetic and copies ran while one was open for 16% -> 0% of each run, Pallas kernels for 0% -> 0%
where the time goes in v1:
time: 72.5 us; the launch traced here: 72.1 us
  Pallas kernels  37.5 us (52%)
  blocking collectives  14.1 us (19%)
  waiting for transfers between devices  8.51 us (12%)
  starting transfers between devices  7.28 us (10%)
  local copies, waits for them, and re-layouts  3.1 us (4%)
  other arithmetic  1 us (1%)
    pallas_call x1, Pallas kernels, shards(): pl.pallas_call(forcing_kernel, grid=(levels,), in_specs=[smem, pl.BlockSp...  27.8 us
    all_to_all x1, blocking collectives, shards(): lax.all_to_all(moments, ('by', 'bx'), split_axis=0, concat_axis=0, tiled=...  14.1 us
    ppermute x4, waiting for transfers between devices, shift(): lax.ppermute(value, axis, [(i, (i + by) % size) for i in range(size)])  8.51 us
    ppermute x4, starting transfers between devices, shift(): lax.ppermute(value, axis, [(i, (i + by) % size) for i in range(size)])  7.28 us
    pallas_call x1, Pallas kernels, shards(): pl.pallas_call(solve_kernel, in_specs=[smem] + [vmem] * 7, out_specs=[vme...  7.16 us
    pallas_call x1, Pallas kernels, shards(): pl.pallas_call(combine_kernel, in_specs=[vmem] * (ITERS + 4), out_specs=[...  2.54 us
  transfers between devices with their start and end apart: 4, of which 3 were waited for; matrix products, arithmetic and copies ran while one was open for 0% of the time, Pallas kernels for 0%

profile of v1, /device:TPU:0, one launch (start us, length us, event | category | flops | bytes accessed | tf_op | source)
XLA Modules:
  0.0 72.1 jit_solution(12940906936533691988)
XLA Ops:
  0.6 1.0 %convert_element_type.3 = f32[256,256]{1,0:T(8,128)S(1)} convert(s32[256,256]{1,0:T(8,128)} %count.1) | non-fusion elementwise | flops 65536 | bytes 524288 | tf_op jit(solution)/shard_map/convert_element_type | solution.py:356
  1.6 1.1 %fusion = (f32[3,8,8,256]{3,2,1,0:T(8,128)S(1)}, f32[3,8,8,256]{3,2,1,0:T(8,128)S(1)}) fusion(f32[3,8,256,256]{3,2,1,0:T(8,128)} %fields.1), kind=kLoop, calls=%fused_computation.6 | loop fusion | bytes 786432 | tf_op jit(solution)/shard_map/slice | solution.py:359
  2.7 0.7 %slice_bitcast_fusion = (f32[1,8,256]{2,1,0:T(8,128)S(1)}, f32[1,8,256]{2,1,0:T(8,128)S(1)}, f32[1,8,256]{2,1,0:T(8,128)S(1)}, f32[1,8,256]{2,1,0:T(8,128)S(1)}) fusion(f32[256,256]{1,0:T(8,128)S(1)} %convert_element_type.3, f32[256,256]{1,0:T(8,128)} %old.1), kind=kLoop, calls=%fused_computation.2 | loop fusion | bytes 65536 | tf_op jit(solution)/shard_map/broadcast_in_dim | solution.py:361
  3.4 0.5 collective-permute-start
  4.0 2.0 %collective-permute-start.1 = (f32[26,8,256]{2,1,0:T(8,128)S(1)}, f32[26,8,256]{2,1,0:T(8,128)S(1)}, u32[]{:S(2)}, u32[]{:S(2)}) collective-permute-start(f32[26,8,256]{2,1,0:T(8,128)S(1)} %pad_maximum_fusion.1), channel_id=1, source_target_pairs={{0,24},{8,0},{16,8},{24,16},{1,25},{9,1},{17,9},{25,17},{2,26},{10... | collective-permute-start | bytes 638984 | tf_op jit(solution)/shard_map/ppermute | solution.py:349
  6.0 3.4 %collective-permute-done.south = f32[26,8,256]{2,1,0:T(8,128)S(1)} collective-permute-done((f32[26,8,256]{2,1,0:T(8,128)S(1)}, f32[26,8,256]{2,1,0:T(8,128)S(1)}, u32[]{:S(2)}, u32[]{:S(2)}) %collective-permute-start) | collective-permute-done | bytes 213024 | tf_op jit(solution)/shard_map/ppermute | solution.py:349
  9.4 0.0 copy-start
  9.4 2.1 %collective-permute-done.1.north = f32[26,8,256]{2,1,0:T(8,128)S(1)} collective-permute-done((f32[26,8,256]{2,1,0:T(8,128)S(1)}, f32[26,8,256]{2,1,0:T(8,128)S(1)}, u32[]{:S(2)}, u32[]{:S(2)}) %collective-permute-start.1) | collective-permute-done | bytes 213024 | tf_op jit(solution)/shard_map/ppermute | solution.py:349
  11.5 0.0 copy-done
  11.5 0.0 copy-start.1
  11.5 0.7 copy-done.1
  12.2 27.8 %forcing.1 = (f32[272,256]{1,0:T(8,128)}, f32[272,256]{1,0:T(8,128)}, f32[272,256]{1,0:T(8,128)}, f32[40,384]{1,0:T(8,128)}, f32[40,384]{1,0:T(8,128)}) custom-call(f32[8]{0:T(128)} %thick.3, f32[3,8,256,256]{3,2,1,0:T(8,128)} %fields.1, f32[26,8,256]{2,1,0:T(8,128)} %copy-done, f32[26,8,256]{2,1,0:T(8,128)} %copy-done.1, s32[256,256]{1,0:T(8,128)} %count.1, ...), custom_call_target="tpu_custom_call" | custom-call | tf_op jit(solution)/shard_map/forcing/pallas_call | solution.py:372
  40.0 1.5 %collective-permute-start.2 = (f32[40,384]{1,0:T(8,128)}, f32[40,384]{1,0:T(8,128)S(1)}, u32[]{:S(2)}, u32[]{:S(2)}) collective-permute-start(f32[40,384]{1,0:T(8,128)} %get-tuple-element.17.to_east), channel_id=1, source_target_pairs={{0,1},{1,2},{2,3},{3,4},{4,5},{5,6},{6,7},{7,0},{8,9},{9,10},{10,1... | collective-permute-start | bytes 184328 | tf_op jit(solution)/shard_map/ppermute | solution.py:349
  41.5 3.2 %collective-permute-start.3 = (f32[40,384]{1,0:T(8,128)}, f32[40,384]{1,0:T(8,128)S(1)}, u32[]{:S(2)}, u32[]{:S(2)}) collective-permute-start(f32[40,384]{1,0:T(8,128)} %get-tuple-element.18.to_west), channel_id=1, source_target_pairs={{0,7},{1,0},{2,1},{3,2},{4,3},{5,4},{6,5},{7,6},{8,15},{9,8},{10,9... | collective-permute-start | bytes 184328 | tf_op jit(solution)/shard_map/ppermute | solution.py:349
  44.7 3.0 %collective-permute-done.2.from_west = f32[40,384]{1,0:T(8,128)S(1)} collective-permute-done((f32[40,384]{1,0:T(8,128)}, f32[40,384]{1,0:T(8,128)S(1)}, u32[]{:S(2)}, u32[]{:S(2)}) %collective-permute-start.2) | collective-permute-done | bytes 61472 | tf_op jit(solution)/shard_map/ppermute | solution.py:349
  47.7 0.0 copy-start.2
  47.7 0.0 collective-permute-done.3.from_east
  47.7 0.0 copy-start.3
  47.7 0.6 copy-done.2
  48.3 0.0 copy-done.3
  48.3 7.2 %krylov.1 = (f32[256,256]{1,0:T(8,128)}, f32[256,256]{1,0:T(8,128)}, f32[256,256]{1,0:T(8,128)}, f32[256,256]{1,0:T(8,128)}, f32[256,256]{1,0:T(8,128)}, /*index=5*/f32[256,256]{1,0:T(8,128)}, f32[32,1,128]{2,1,0:T(1,128)}) custom-call(f32[8]{0:T(128)} %thick.3, f32[272,256]{1,0:T(8,128)} %get-tuple-element.14.part, f32[272,256]{1,0:T(8,128)} %get-tuple-element.15.depth, ...), custom_call_target="tpu_custom_call" | custom-call | tf_op jit(solution)/shard_map/krylov/pallas_call | solution.py:395
  55.5 14.1 %all_to_all.5.moments = f32[32,1,128]{2,1,0:T(1,128)} all-to-all(f32[32,1,128]{2,1,0:T(1,128)} %get-tuple-element.19), channel_id=1, replica_groups=mesh['by'=4,'bx'=8] {'by','bx'}, dimensions={0} | all-to-all | bytes 32768 | tf_op jit(solution)/shard_map/all_to_all | solution.py:407
  69.6 2.5 %combine.1 = (f32[256,256]{1,0:T(8,128)}, f32[256,256]{1,0:T(8,128)}) custom-call(f32[32,1,128]{2,1,0:T(1,128)} %all_to_all.5.moments, f32[272,256]{1,0:T(8,128)} %get-tuple-element.16.guess, f32[256,256]{1,0:T(8,128)} %get-tuple-element.20.base0, f32[256,256]{1,0:T(8,128)} %get-tuple-element.21.base1, f32[256,256]{1,0:T(8,128)} %get-tuple-element.22.base2, ...), custom_call_target="tpu_custom_call" | custom-call | tf_op jit(solution)/shard_map/combine/pallas_call | solution.py:409
  (2 shorter events, 0.0 us)
Async XLA Ops:
  3.4 6.0 %collective-permute-start = (f32[26,8,256]{2,1,0:T(8,128)S(1)}, f32[26,8,256]{2,1,0:T(8,128)S(1)}, u32[]{:S(2)}, u32[]{:S(2)}) collective-permute-start(f32[26,8,256]{2,1,0:T(8,128)S(1)} %pad_maximum_fusion), channel_id=1, source_target_pairs={{0,8},{8,16},{16,24},{24,0},{1,9},{9,17},{17,25},{25,1},{2,10},{10... | collective-permute-start | bytes 638984 | tf_op jit(solution)/shard_map/ppermute | solution.py:349
  4.0 7.6 %collective-permute-start.1 = (f32[26,8,256]{2,1,0:T(8,128)S(1)}, f32[26,8,256]{2,1,0:T(8,128)S(1)}, u32[]{:S(2)}, u32[]{:S(2)}) collective-permute-start(f32[26,8,256]{2,1,0:T(8,128)S(1)} %pad_maximum_fusion.1), channel_id=1, source_target_pairs={{0,24},{8,0},{16,8},{24,16},{1,25},{9,1},{17,9},{25,17},{2,26},{10... | collective-permute-start | bytes 638984 | tf_op jit(solution)/shard_map/ppermute | solution.py:349
  9.4 2.1 %copy-start = (f32[26,8,256]{2,1,0:T(8,128)}, f32[26,8,256]{2,1,0:T(8,128)S(1)}, u32[]{:S(2)}) copy-start(f32[26,8,256]{2,1,0:T(8,128)S(1)} %collective-permute-done.south) | copy-start | bytes 638980
  11.5 0.7 copy-start.1
  40.0 7.7 %collective-permute-start.2 = (f32[40,384]{1,0:T(8,128)}, f32[40,384]{1,0:T(8,128)S(1)}, u32[]{:S(2)}, u32[]{:S(2)}) collective-permute-start(f32[40,384]{1,0:T(8,128)} %get-tuple-element.17.to_east), channel_id=1, source_target_pairs={{0,1},{1,2},{2,3},{3,4},{4,5},{5,6},{6,7},{7,0},{8,9},{9,10},{10,1... | collective-permute-start | bytes 184328 | tf_op jit(solution)/shard_map/ppermute | solution.py:349
  41.5 6.2 %collective-permute-start.3 = (f32[40,384]{1,0:T(8,128)}, f32[40,384]{1,0:T(8,128)S(1)}, u32[]{:S(2)}, u32[]{:S(2)}) collective-permute-start(f32[40,384]{1,0:T(8,128)} %get-tuple-element.18.to_west), channel_id=1, source_target_pairs={{0,7},{1,0},{2,1},{3,2},{4,3},{5,4},{6,5},{7,6},{8,15},{9,8},{10,9... | collective-permute-start | bytes 184328 | tf_op jit(solution)/shard_map/ppermute | solution.py:349
  47.7 0.6 copy-start.2
  47.7 0.6 copy-start.3

commit v2 on v1

v2 whole, which is shorter than its diff:
```python
import jax
import jax.numpy as jnp
from jax import lax
from jax.experimental import pallas as pl
from jax.experimental.pallas import tpu as pltpu
from jax.sharding import PartitionSpec as P

ITERS = 4
VISCOSITY = 0.05
IMPLICIT = 0.05

ROWS = 8
PAD = 8
LANES = 128
REACH = 3
DEEP = ITERS
EDGE = ITERS + 1

STEP = 8


def message_rows(levels):
    forcing_at = REACH * levels
    count_at = forcing_at + DEEP
    pressure_at = count_at + EDGE
    total = pressure_at + EDGE
    return forcing_at, count_at, pressure_at, -(-total // 8) * 8


def lane_index():
    return lax.broadcasted_iota(jnp.int32, (STEP, LANES), 1)


def turn(value, by):
    return pltpu.roll(value, by % LANES, 1)


def neighbours(tiles, lane, by=1):
    count = len(tiles)
    back = [None if t is None else turn(t, -by) for t in tiles]
    forth = [None if t is None else turn(t, by) for t in tiles]

    def pick(mask, other, own):
        if other is None and own is None:
            return None
        zero = jnp.zeros((STEP, LANES), jnp.float32)
        return jnp.where(mask, zero if other is None else other, zero if own is None else own)

    east = [pick(lane >= LANES - by, back[(i + 1) % count], back[i]) for i in range(count)]
    west = [pick(lane < by, forth[i - 1], forth[i]) for i in range(count)]
    return east, west


def forcing_kernel(
    thick, fields, south, north, count, old, part, depth, guess, to_east, to_west,
    zonal, merid, baro, mixed, lap, wet, pack_e, pack_w,
):
    level = pl.program_id(0)
    levels = pl.num_programs(0)
    static_levels = (south.shape[0] - 2) // 3
    height, width = count.shape
    tiles = width // LANES
    ext = height + 2 * ROWS
    base = PAD + ROWS
    forcing_at, count_at, pressure_at, _ = message_rows(static_levels)
    lane = lane_index()
    cols = [pl.ds(t * LANES, LANES) for t in range(tiles)]

    def extended(e, lower, middle, upper):
        if e < ROWS:
            return lower
        if e >= ROWS + height:
            return upper
        return middle(e - ROWS)

    @pl.when(level == 0)
    def _():
        for buf in (merid, baro, mixed, lap, depth, guess):
            for at in (0, PAD + ext):
                buf[:, at : at + PAD, :] = jnp.zeros((buf.shape[0], PAD, LANES), jnp.float32)
        part[...] = jnp.zeros_like(part)
        depth[...] = jnp.zeros_like(depth)
        pack_e[...] = jnp.zeros_like(pack_e)
        pack_w[...] = jnp.zeros_like(pack_w)
        for t, c in enumerate(cols):
            wet[t, :ROWS, :] = south[3 * static_levels, :, c]
            wet[t, ROWS : ROWS + height, :] = count[:, c].astype(jnp.float32)
            wet[t, ROWS + height :, :] = north[3 * static_levels, :, c]

    for which, buf in enumerate((zonal, merid, baro)):
        for t, c in enumerate(cols):
            buf[t, PAD:base, :] = south[which * static_levels + level, :, c]
            buf[t, base : base + height, :] = fields[which, 0, :, c]
            buf[t, base + height : base + height + ROWS, :] = north[
                which * static_levels + level, :, c
            ]

    starts = range(PAD, PAD + ext, STEP)
    for r in starts:
        east, west = neighbours([zonal[t, r : r + STEP, :] for t in range(tiles)] + [None], lane)
        for t in range(tiles + 1):
            value = east[t] - west[t]
            if t < tiles:
                value += merid[t, r + 1 : r + 1 + STEP, :] - merid[t, r - 1 : r - 1 + STEP, :]
            mixed[t, r : r + STEP, :] = value

    def laplace(buf, r):
        own = [buf[t, r : r + STEP, :] for t in range(tiles + 1)]
        east, west = neighbours(own, lane)
        return [
            (east[t] + west[t])
            + (buf[t, r + 1 : r + 1 + STEP, :] + buf[t, r - 1 : r - 1 + STEP, :])
            - 4.0 * own[t]
            for t in range(tiles + 1)
        ]

    for r in starts:
        for t, value in enumerate(laplace(mixed, r)):
            lap[t, r : r + STEP, :] = value
    thickness = thick[level]
    level_number = level.astype(jnp.float32)
    for r in starts:
        e = r - PAD
        second = laplace(lap, r)
        own = [baro[t, r : r + STEP, :] for t in range(tiles)]
        east, west = neighbours(own + [None], lane, 2)
        for t in range(tiles + 1):
            spread = east[t] + west[t]
            if t < tiles:
                spread += baro[t, r + 2 : r + 2 + STEP, :] + baro[t, r - 2 : r - 2 + STEP, :]
                spread -= 4.0 * own[t]
            div = (-0.5 * VISCOSITY) * second[t] - 0.25 * spread
            if t < tiles:
                weight = jnp.where(wet[t, e : e + STEP, :] > level_number, thickness, 0.0)
                part[t, e : e + STEP, :] += weight * div
                depth[t, r : r + STEP, :] += weight
            else:
                going_east = jnp.where(lane < REACH, div, 0.0)
                going_west = jnp.where(lane >= LANES - REACH, div, 0.0)
                pack_e[e : e + STEP, :] += pltpu.roll(going_east, REACH * level, 1)
                pack_w[e : e + STEP, :] += pltpu.roll(going_west, REACH * level + REACH, 1)

    @pl.when(level == levels - 1)
    def _():
        for r in starts:
            e = r - PAD
            begin = []
            for t, c in enumerate(cols):
                pressure = extended(
                    e,
                    south[3 * static_levels + 1, :, c],
                    lambda o: old[o : o + STEP, c],
                    north[3 * static_levels + 1, :, c],
                )
                begin.append(jnp.where(depth[t, r : r + STEP, :] > 0.0, pressure, 0.0))
                guess[t, r : r + STEP, :] = begin[t]
            for pack, t, inner in ((pack_e, tiles - 1, True), (pack_w, 0, False)):
                tile = pack[e : e + STEP, :]
                pieces = (
                    (part[t, e : e + STEP, :], forcing_at, DEEP),
                    (wet[t, e : e + STEP, :], count_at, EDGE),
                    (begin[t], pressure_at, EDGE),
                )
                for piece, lane_at, size in pieces:
                    moved = turn(piece, lane_at + size if inner else lane_at)
                    inside = (lane >= lane_at) & (lane < lane_at + size)
                    tile = jnp.where(inside, moved, tile)
                pack[e : e + STEP, :] = tile
        for pack, message in ((pack_e, to_east), (pack_w, to_west)):
            for at in range(0, message.shape[1], LANES):
                turned = jnp.transpose(pack[at : at + LANES, :])
                message[:, at : at + LANES] = turned[: message.shape[0], :]


def solve_kernel(
    thick, part, depth, guess, to_east, to_west, from_west, from_east,
    base0, base1, base2, base3, base4, diag_out, moments,
    turned, fix, halo_part, halo_depth, halo_guess, half, half_w, diag, inverse,
    vec_a, vec_b, vec_e, vec_w,
):
    tiles, ext, _ = part.shape
    height = ext - 2 * ROWS
    levels = thick.shape[0]
    forcing_at, count_at, pressure_at, _ = message_rows(levels)
    lane = lane_index()

    def weights(counts):
        return [jnp.where(counts > float(k), thick[k], 0.0) for k in range(levels)]

    def weighted(counts, message):
        total = None
        for k, weight in enumerate(weights(counts)):
            term = weight * message[REACH * k : REACH * k + REACH, :]
            total = term if total is None else total + term
        return total

    def rows(message, at, size):
        return message[at : at + size, :]

    skip = EDGE - REACH
    turned[...] = jnp.zeros_like(turned)
    turned[0:DEEP, :] = rows(from_east, forcing_at, DEEP)
    turned[0:REACH, :] += weighted(rows(from_east, count_at, REACH), to_east)
    turned[LANES - DEEP : LANES, :] = rows(from_west, forcing_at, DEEP)
    turned[LANES - REACH : LANES, :] += weighted(rows(from_west, count_at + skip, REACH), to_west)
    turned[40 : 40 + EDGE, :] = sum(weights(rows(from_east, count_at, EDGE)))
    turned[40 - EDGE : 40, :] = sum(weights(rows(from_west, count_at, EDGE)))
    turned[60 : 60 + EDGE, :] = rows(from_east, pressure_at, EDGE)
    turned[60 - EDGE : 60, :] = rows(from_west, pressure_at, EDGE)
    turned[80 : 80 + REACH, :] = weighted(rows(to_west, count_at, REACH), from_west)
    turned[80 - REACH : 80, :] = weighted(rows(to_east, count_at + skip, REACH), from_east)

    for buf in (halo_depth, halo_guess):
        for at in (0, PAD + ext):
            buf[at : at + PAD, :] = jnp.zeros((PAD, LANES), jnp.float32)
    for buf in (half, half_w, vec_e, vec_w):
        for at in (0, PAD + ext):
            buf[:, at : at + PAD, :] = jnp.zeros((tiles + 1, PAD, LANES), jnp.float32)
    near = (lane < EDGE) | (lane >= LANES - EDGE)
    close = (lane < DEEP) | (lane >= LANES - DEEP)
    for at in range(0, ext, LANES):
        block = jnp.transpose(turned[:, at : at + LANES])
        for e in range(at, min(at + LANES, ext), STEP):
            r = e + PAD
            tile = block[e - at : e - at + STEP, :]
            halo_depth[r : r + STEP, :] = jnp.where(near, turn(tile, -40), 0.0)
            halo_guess[r : r + STEP, :] = jnp.where(near, turn(tile, -60), 0.0)
            halo_part[e : e + STEP, :] = jnp.where(close, tile, 0.0)
            fix[e : e + STEP, :] = turn(tile, -80)

    def read(main, halo, r):
        return [main[t, r : r + STEP, :] for t in range(tiles)] + [halo[r : r + STEP, :]]

    starts = range(PAD, PAD + ext, STEP)
    both = range(tiles + 1)
    for r in starts:
        low = [
            jnp.minimum(a, b)
            for a, b in zip(read(depth, halo_depth, r), read(depth, halo_depth, r + 1))
        ]
        east, _ = neighbours(low, lane)
        corner = [0.5 * jnp.minimum(a, b) for a, b in zip(low, east)]
        _, west = neighbours(corner, lane)
        begin = read(guess, halo_guess, r)
        begin_e, begin_w = neighbours(begin, lane)
        for t in both:
            half[t, r : r + STEP, :] = corner[t]
            half_w[t, r : r + STEP, :] = west[t]
            vec_e[t, r : r + STEP, :] = begin_e[t]
            vec_w[t, r : r + STEP, :] = begin_w[t]

    def around(t, r):
        pairs = []
        for at in (r, r - 1):
            there = at + 1 if at == r else at
            pairs.append((half[t, at : at + STEP, :], vec_e[t, there : there + STEP, :]))
            pairs.append((half_w[t, at : at + STEP, :], vec_w[t, there : there + STEP, :]))
        return pairs

    for r in starts:
        e = r - PAD
        begin = read(guess, halo_guess, r)
        wide = read(depth, halo_depth, r)
        fixes = fix[e : e + STEP, :]
        for t in both:
            pairs = around(t, r)
            (ch, ne), (chw, nw), (ch_s, se), (chw_s, sw) = pairs
            diagonal = IMPLICIT + ((ch + chw) + (ch_s + chw_s))
            inv = 1.0 / diagonal
            diag[t, e : e + STEP, :] = diagonal
            inverse[t, e : e + STEP, :] = inv
            here = begin[t]
            image = IMPLICIT * here + (
                (ch * (here - ne) + chw * (here - nw)) + (ch_s * (here - se) + chw_s * (here - sw))
            )
            total = halo_part[e : e + STEP, :] if t == tiles else part[t, e : e + STEP, :]
            if t == 0:
                total += jnp.where(lane < REACH, fixes, 0.0)
            if t == tiles - 1:
                total += jnp.where(lane >= LANES - REACH, fixes, 0.0)
            side = jnp.where(wide[t] > 0.0, total + IMPLICIT * here, 0.0)
            first = (side - image) * inv
            vec_a[t, e : e + STEP, :] = first
            if t < tiles and ROWS <= e < ROWS + height:
                o = e - ROWS
                base0[t, o : o + STEP, :] = first
                diag_out[t, o : o + STEP, :] = diagonal

    outs = (base0, base1, base2, base3, base4)
    buffers = (vec_a, vec_b)
    sums = []
    for j in range(ITERS):
        source, target = buffers[j % 2], buffers[(j + 1) % 2]
        for r in starts:
            e = r - PAD
            east, west = neighbours([source[t, e : e + STEP, :] for t in both], lane)
            for t in both:
                vec_e[t, r : r + STEP, :] = east[t]
                vec_w[t, r : r + STEP, :] = west[t]
        even = jnp.zeros((STEP, LANES), jnp.float32)
        odd = jnp.zeros((STEP, LANES), jnp.float32)
        for r in starts:
            e = r - PAD
            for t in both:
                (ch, ne), (chw, nw), (ch_s, se), (chw_s, sw) = around(t, r)
                value = inverse[t, e : e + STEP, :] * (
                    (ch * ne + chw * nw) + (ch_s * se + chw_s * sw)
                )
                if j + 1 < ITERS:
                    target[t, e : e + STEP, :] = value
                if t < tiles and ROWS <= e < ROWS + height:
                    o = e - ROWS
                    outs[j + 1][t, o : o + STEP, :] = value
                    now = source[t, e : e + STEP, :]
                    scaled = diag[t, e : e + STEP, :] * now
                    even = even + scaled * now
                    odd = odd + scaled * value
        sums += [even, odd]
    lane_row = lax.broadcasted_iota(jnp.int32, (1, LANES), 1)
    found = jnp.zeros((1, LANES), jnp.float32)
    for m, acc in enumerate(sums):
        found = jnp.where(lane_row == m, jnp.sum(acc), found)
    for d in range(moments.shape[0]):
        moments[d] = found


def combine_kernel(moments, guess, base0, base1, base2, base3, base4, diag, pressure, residual):
    height, width = pressure.shape
    total = jnp.sum(moments[...], axis=0)
    h = [jnp.broadcast_to(total[:, m : m + 1], (STEP, LANES)) for m in range(2 * ITERS)]
    one, zero = jnp.ones((STEP, LANES), jnp.float32), None

    def plus(a, b):
        return b if a is None else a if b is None else a + b

    def times(a, b):
        return None if a is None or b is None else a * b

    def minus_n(poly):
        moved = [zero] + list(poly)
        return [
            a if b is None else (-b if a is None else a - b)
            for a, b in zip(list(poly) + [zero], moved)
        ]

    def inner(left, right):
        total = None
        for i, a in enumerate(left):
            part = None
            for j, b in enumerate(right):
                part = plus(part, times(b, h[i + j]))
            total = plus(total, times(a, part))
        return total

    rest, direction, answer = [one], [one], []
    norm = h[0]
    for iteration in range(ITERS):
        image = minus_n(direction)
        alpha = norm / inner(direction, image)
        answer = [
            plus(answer[i] if i < len(answer) else None, alpha * c)
            for i, c in enumerate(direction)
        ]
        rest = [
            plus(rest[i] if i < len(rest) else None, -(alpha * c)) for i, c in enumerate(image)
        ]
        if iteration + 1 < ITERS:
            following = inner(rest, rest)
            ratio = following / norm
            direction = [
                plus(c, ratio * direction[i] if i < len(direction) else None)
                for i, c in enumerate(rest)
            ]
            norm = following
    bases = (base0, base1, base2, base3, base4)
    for t in range(width // LANES):
        for o in range(0, height, STEP):
            vecs = [b[t, o : o + STEP, :] for b in bases]
            moved = sum(c * v for c, v in zip(answer, vecs))
            left = sum(c * v for c, v in zip(rest, vecs))
            at = PAD + ROWS + o
            cols = pl.ds(t * LANES, LANES)
            pressure[o : o + STEP, cols] = guess[t, at : at + STEP, :] + moved
            residual[o : o + STEP, cols] = diag[t, o : o + STEP, :] * left


def shift(value, axis, by):
    size = lax.axis_size(axis)
    return lax.ppermute(value, axis, [(i, (i + by) % size) for i in range(size)])


def shards(fields, level_count, thickness, old_pressure):
    levels, height, width = fields.shape[1:]
    ext, tall = height + 2 * ROWS, height + LANES
    f32 = jnp.float32
    counts = level_count.astype(f32)

    def edge(at):
        pick = lambda a: lax.slice_in_dim(a, at, at + ROWS, axis=a.ndim - 2)
        flat = pick(fields).reshape(3 * levels, ROWS, width)
        return jnp.concatenate([flat, pick(counts)[None], pick(old_pressure)[None]], axis=0)

    south = shift(edge(height - ROWS), "by", 1)
    north = shift(edge(0), "by", -1)

    message = message_rows(levels)[3]
    tiles, padded = width // LANES, ext + 2 * PAD
    smem = pl.BlockSpec(memory_space=pltpu.SMEM)
    vmem = pl.BlockSpec(memory_space=pltpu.VMEM)
    whole = lambda *dims: pl.BlockSpec(dims, lambda k: (0,) * len(dims))
    halo = whole(3 * levels + 2, ROWS, width)
    shaped = lambda *dims: jax.ShapeDtypeStruct(dims, f32)
    scratch = lambda *dims: pltpu.VMEM(dims, f32)
    main = (tiles, ext, LANES)
    loose = (tiles, padded, LANES)
    results = (main, loose, loose, (message, tall), (message, tall))
    part, depth, guess, to_east, to_west = pl.pallas_call(
        forcing_kernel,
        grid=(levels,),
        in_specs=[
            smem,
            pl.BlockSpec((3, 1, height, width), lambda k: (0, k, 0, 0)),
            halo, halo, whole(height, width), whole(height, width),
        ],
        out_specs=[whole(*dims) for dims in results],
        out_shape=[shaped(*dims) for dims in results],
        scratch_shapes=[scratch(*loose)] * 3
        + [scratch(tiles + 1, padded, LANES)] * 2
        + [scratch(*main)]
        + [scratch(tall, LANES)] * 2,
        name="forcing",
    )(thickness, fields, south, north, level_count, old_pressure)

    from_west = shift(to_east, "bx", 1)
    from_east = shift(to_west, "bx", -1)

    devices = lax.axis_size("by") * lax.axis_size("bx")
    out = shaped(tiles, height, LANES)
    *bases, diag, moments = pl.pallas_call(
        solve_kernel,
        in_specs=[smem] + [vmem] * 7,
        out_specs=[vmem] * (ITERS + 3),
        out_shape=[out] * (ITERS + 2) + [shaped(devices, 1, LANES)],
        scratch_shapes=[scratch(LANES, tall), scratch(ext, LANES), scratch(ext, LANES)]
        + [scratch(padded, LANES)] * 2
        + [scratch(tiles + 1, padded, LANES)] * 2
        + [scratch(tiles + 1, ext, LANES)] * 4
        + [scratch(tiles + 1, padded, LANES)] * 2,
        name="krylov",
    )(thickness, part, depth, guess, to_east, to_west, from_west, from_east)

    moments = lax.all_to_all(moments, ("by", "bx"), split_axis=0, concat_axis=0, tiled=True)
    return tuple(
        pl.pallas_call(
            combine_kernel,
            in_specs=[vmem] * (ITERS + 4),
            out_specs=[vmem] * 2,
            out_shape=[shaped(height, width)] * 2,
            name="combine",
        )(moments, guess, *bases, diag)
    )


def solution(mesh):
    placed = (P(None, None, "by", "bx"), P("by", "bx"), P(), P("by", "bx"))
    return jax.shard_map(
        shards,
        mesh=mesh,
        in_specs=placed,
        out_specs=(P("by", "bx"), P("by", "bx")),
        check_vma=False,
    )
```

time: 72.5 us -> 70.3 us (0.970)
  Pallas kernels: 37.5 us -> 35.3 us
    pallas_call x1, Pallas kernels: 27.8 us -> 26.2 us  [shards(): pl.pallas_call(forcing_kernel, grid=(levels,), in_specs=[smem, pl.BlockSp...]
where the time goes in v2:
time: 70.3 us; the launch traced here: 70 us
  Pallas kernels  35.3 us (50%)
  blocking collectives  14.1 us (20%)
  waiting for transfers between devices  8.51 us (12%)
  starting transfers between devices  7.28 us (10%)
  local copies, waits for them, and re-layouts  3.1 us (4%)
  other arithmetic  1 us (1%)
    pallas_call x1, Pallas kernels, shards(): pl.pallas_call(forcing_kernel, grid=(levels,), in_specs=[smem, pl.BlockSp...  26.2 us
    all_to_all x1, blocking collectives, shards(): lax.all_to_all(moments, ('by', 'bx'), split_axis=0, concat_axis=0, tiled=...  14.1 us
    ppermute x4, waiting for transfers between devices, shift(): lax.ppermute(value, axis, [(i, (i + by) % size) for i in range(size)])  8.51 us
    ppermute x4, starting transfers between devices, shift(): lax.ppermute(value, axis, [(i, (i + by) % size) for i in range(size)])  7.28 us
    pallas_call x1, Pallas kernels, shards(): pl.pallas_call(solve_kernel, in_specs=[smem] + [vmem] * 7, out_specs=[vme...  6.56 us
    pallas_call x1, Pallas kernels, shards(): pl.pallas_call(combine_kernel, in_specs=[vmem] * (ITERS + 4), out_specs=[...  2.54 us
  transfers between devices with their start and end apart: 4, of which 3 were waited for; matrix products, arithmetic and copies ran while one was open for 0% of the time, Pallas kernels for 0%

profile of v2, /device:TPU:0, one launch (start us, length us, event | category | flops | bytes accessed | tf_op | source)
XLA Modules:
  0.0 70.0 jit_solution(17351096312613676786)
XLA Ops:
  0.6 1.0 %convert_element_type.3 = f32[256,256]{1,0:T(8,128)S(1)} convert(s32[256,256]{1,0:T(8,128)} %count.1) | non-fusion elementwise | flops 65536 | bytes 524288 | tf_op jit(solution)/shard_map/convert_element_type | solution.py:396
  1.6 1.1 %fusion = (f32[3,8,8,256]{3,2,1,0:T(8,128)S(1)}, f32[3,8,8,256]{3,2,1,0:T(8,128)S(1)}) fusion(f32[3,8,256,256]{3,2,1,0:T(8,128)} %fields.1), kind=kLoop, calls=%fused_computation.6 | loop fusion | bytes 786432 | tf_op jit(solution)/shard_map/slice | solution.py:399
  2.7 0.7 %slice_bitcast_fusion = (f32[1,8,256]{2,1,0:T(8,128)S(1)}, f32[1,8,256]{2,1,0:T(8,128)S(1)}, f32[1,8,256]{2,1,0:T(8,128)S(1)}, f32[1,8,256]{2,1,0:T(8,128)S(1)}) fusion(f32[256,256]{1,0:T(8,128)S(1)} %convert_element_type.3, f32[256,256]{1,0:T(8,128)} %old.1), kind=kLoop, calls=%fused_computation.2 | loop fusion | bytes 65536 | tf_op jit(solution)/shard_map/broadcast_in_dim | solution.py:401
  3.4 0.5 collective-permute-start
  4.0 2.0 %collective-permute-start.1 = (f32[26,8,256]{2,1,0:T(8,128)S(1)}, f32[26,8,256]{2,1,0:T(8,128)S(1)}, u32[]{:S(2)}, u32[]{:S(2)}) collective-permute-start(f32[26,8,256]{2,1,0:T(8,128)S(1)} %pad_maximum_fusion.1), channel_id=1, source_target_pairs={{0,24},{8,0},{16,8},{24,16},{1,25},{9,1},{17,9},{25,17},{2,26},{10... | collective-permute-start | bytes 638984 | tf_op jit(solution)/shard_map/ppermute | solution.py:389
  6.0 3.4 %collective-permute-done.south = f32[26,8,256]{2,1,0:T(8,128)S(1)} collective-permute-done((f32[26,8,256]{2,1,0:T(8,128)S(1)}, f32[26,8,256]{2,1,0:T(8,128)S(1)}, u32[]{:S(2)}, u32[]{:S(2)}) %collective-permute-start) | collective-permute-done | bytes 213024 | tf_op jit(solution)/shard_map/ppermute | solution.py:389
  9.4 0.0 copy-start
  9.4 2.1 %collective-permute-done.1.north = f32[26,8,256]{2,1,0:T(8,128)S(1)} collective-permute-done((f32[26,8,256]{2,1,0:T(8,128)S(1)}, f32[26,8,256]{2,1,0:T(8,128)S(1)}, u32[]{:S(2)}, u32[]{:S(2)}) %collective-permute-start.1) | collective-permute-done | bytes 213024 | tf_op jit(solution)/shard_map/ppermute | solution.py:389
  11.5 0.0 copy-done
  11.5 0.0 copy-start.1
  11.5 0.7 copy-done.1
  12.2 26.2 %forcing.1 = (f32[2,272,128]{2,1,0:T(8,128)}, f32[2,288,128]{2,1,0:T(8,128)}, f32[2,288,128]{2,1,0:T(8,128)}, f32[40,384]{1,0:T(8,128)}, f32[40,384]{1,0:T(8,128)}) custom-call(f32[8]{0:T(128)} %thick.3, f32[3,8,256,256]{3,2,1,0:T(8,128)} %fields.1, f32[26,8,256]{2,1,0:T(8,128)} %copy-done, f32[26,8,256]{2,1,0:T(8,128)} %copy-done.1, s32[256,256]{1,0:T(8,128)} %count.1, ...), custom_call_target="tpu_custom_call" | custom-call | tf_op jit(solution)/shard_map/forcing/pallas_call | solution.py:417
  38.4 1.5 %collective-permute-start.2 = (f32[40,384]{1,0:T(8,128)}, f32[40,384]{1,0:T(8,128)S(1)}, u32[]{:S(2)}, u32[]{:S(2)}) collective-permute-start(f32[40,384]{1,0:T(8,128)} %get-tuple-element.17.to_east), channel_id=1, source_target_pairs={{0,1},{1,2},{2,3},{3,4},{4,5},{5,6},{6,7},{7,0},{8,9},{9,10},{10,1... | collective-permute-start | bytes 184328 | tf_op jit(solution)/shard_map/ppermute | solution.py:389
  39.9 3.2 %collective-permute-start.3 = (f32[40,384]{1,0:T(8,128)}, f32[40,384]{1,0:T(8,128)S(1)}, u32[]{:S(2)}, u32[]{:S(2)}) collective-permute-start(f32[40,384]{1,0:T(8,128)} %get-tuple-element.18.to_west), channel_id=1, source_target_pairs={{0,7},{1,0},{2,1},{3,2},{4,3},{5,4},{6,5},{7,6},{8,15},{9,8},{10,9... | collective-permute-start | bytes 184328 | tf_op jit(solution)/shard_map/ppermute | solution.py:389
  43.1 3.0 %collective-permute-done.2.from_west = f32[40,384]{1,0:T(8,128)S(1)} collective-permute-done((f32[40,384]{1,0:T(8,128)}, f32[40,384]{1,0:T(8,128)S(1)}, u32[]{:S(2)}, u32[]{:S(2)}) %collective-permute-start.2) | collective-permute-done | bytes 61472 | tf_op jit(solution)/shard_map/ppermute | solution.py:389
  46.1 0.0 copy-start.2
  46.1 0.0 collective-permute-done.3.from_east
  46.1 0.0 copy-start.3
  46.1 0.6 copy-done.2
  46.7 0.0 copy-done.3
  46.7 6.6 %krylov.1 = (f32[2,256,128]{2,1,0:T(8,128)}, f32[2,256,128]{2,1,0:T(8,128)}, f32[2,256,128]{2,1,0:T(8,128)}, f32[2,256,128]{2,1,0:T(8,128)}, f32[2,256,128]{2,1,...) custom-call(f32[8]{0:T(128)} %thick.3, f32[2,272,128]{2,1,0:T(8,128)} %get-tuple-element.14.part, ...), custom_call_target="tpu_custom_call" | custom-call | tf_op jit(solution)/shard_map/krylov/pallas_call | solution.py:439
  53.3 14.1 %all_to_all.5.moments = f32[32,1,128]{2,1,0:T(1,128)} all-to-all(f32[32,1,128]{2,1,0:T(1,128)} %get-tuple-element.19), channel_id=1, replica_groups=mesh['by'=4,'bx'=8] {'by','bx'}, dimensions={0} | all-to-all | bytes 32768 | tf_op jit(solution)/shard_map/all_to_all | solution.py:452
  67.4 2.5 %combine.1 = (f32[256,256]{1,0:T(8,128)}, f32[256,256]{1,0:T(8,128)}) custom-call(f32[32,1,128]{2,1,0:T(1,128)} %all_to_all.5.moments, f32[2,288,128]{2,1,0:T(8,128)} %get-tuple-element.16.guess, f32[2,256,128]{2,1,0:T(8,128)} %get-tuple-element.20.base0, f32[2,256,128]{2,1,0:T(8,128)} %get-tuple-element.21.base1, f32[2,256,128]{2,1,0:T(8,128)} %get-tuple-element.22.base2, ...), custom_call_target="tpu_custom_call" | custom-call | tf_op jit(solution)/shard_map/combine/pallas_call | solution.py:454
  (2 shorter events, 0.0 us)
Async XLA Ops:
  3.4 6.0 %collective-permute-start = (f32[26,8,256]{2,1,0:T(8,128)S(1)}, f32[26,8,256]{2,1,0:T(8,128)S(1)}, u32[]{:S(2)}, u32[]{:S(2)}) collective-permute-start(f32[26,8,256]{2,1,0:T(8,128)S(1)} %pad_maximum_fusion), channel_id=1, source_target_pairs={{0,8},{8,16},{16,24},{24,0},{1,9},{9,17},{17,25},{25,1},{2,10},{10... | collective-permute-start | bytes 638984 | tf_op jit(solution)/shard_map/ppermute | solution.py:389
  4.0 7.6 %collective-permute-start.1 = (f32[26,8,256]{2,1,0:T(8,128)S(1)}, f32[26,8,256]{2,1,0:T(8,128)S(1)}, u32[]{:S(2)}, u32[]{:S(2)}) collective-permute-start(f32[26,8,256]{2,1,0:T(8,128)S(1)} %pad_maximum_fusion.1), channel_id=1, source_target_pairs={{0,24},{8,0},{16,8},{24,16},{1,25},{9,1},{17,9},{25,17},{2,26},{10... | collective-permute-start | bytes 638984 | tf_op jit(solution)/shard_map/ppermute | solution.py:389
  9.4 2.1 %copy-start = (f32[26,8,256]{2,1,0:T(8,128)}, f32[26,8,256]{2,1,0:T(8,128)S(1)}, u32[]{:S(2)}) copy-start(f32[26,8,256]{2,1,0:T(8,128)S(1)} %collective-permute-done.south) | copy-start | bytes 638980
  11.5 0.7 copy-start.1
  38.4 7.7 %collective-permute-start.2 = (f32[40,384]{1,0:T(8,128)}, f32[40,384]{1,0:T(8,128)S(1)}, u32[]{:S(2)}, u32[]{:S(2)}) collective-permute-start(f32[40,384]{1,0:T(8,128)} %get-tuple-element.17.to_east), channel_id=1, source_target_pairs={{0,1},{1,2},{2,3},{3,4},{4,5},{5,6},{6,7},{7,0},{8,9},{9,10},{10,1... | collective-permute-start | bytes 184328 | tf_op jit(solution)/shard_map/ppermute | solution.py:389
  39.9 6.2 %collective-permute-start.3 = (f32[40,384]{1,0:T(8,128)}, f32[40,384]{1,0:T(8,128)S(1)}, u32[]{:S(2)}, u32[]{:S(2)}) collective-permute-start(f32[40,384]{1,0:T(8,128)} %get-tuple-element.18.to_west), channel_id=1, source_target_pairs={{0,7},{1,0},{2,1},{3,2},{4,3},{5,4},{6,5},{7,6},{8,15},{9,8},{10,9... | collective-permute-start | bytes 184328 | tf_op jit(solution)/shard_map/ppermute | solution.py:389
  46.1 0.6 copy-start.2
  46.1 0.6 copy-start.3

commit v3 on v2

v3 whole, which is shorter than its diff:
```python
import jax
import jax.numpy as jnp
from jax import lax
from jax.experimental import pallas as pl
from jax.experimental.pallas import tpu as pltpu
from jax.sharding import PartitionSpec as P

ITERS = 4
VISCOSITY = 0.05
IMPLICIT = 0.05

ROWS = 8
PAD = 8
LANES = 128
REACH = 3
DEEP = ITERS
EDGE = ITERS + 1

STEP = 8
MIX_UNROLL = 17
SPREAD_UNROLL = 11
WIDE = 17
WIDE_INNER = 8


def message_rows(levels):
    forcing_at = REACH * levels
    count_at = forcing_at + DEEP
    pressure_at = count_at + EDGE
    total = pressure_at + EDGE
    return forcing_at, count_at, pressure_at, -(-total // 8) * 8


def lane_index():
    return lax.broadcasted_iota(jnp.int32, (STEP, LANES), 1)


def turn(value, by):
    return pltpu.roll(value, by % LANES, 1)


def neighbours(tiles, lane, by=1):
    count = len(tiles)
    back = [None if t is None else turn(t, -by) for t in tiles]
    forth = [None if t is None else turn(t, by) for t in tiles]

    def pick(mask, other, own):
        if other is None and own is None:
            return None
        zero = jnp.zeros((STEP, LANES), jnp.float32)
        return jnp.where(mask, zero if other is None else other, zero if own is None else own)

    east = [pick(lane >= LANES - by, back[(i + 1) % count], back[i]) for i in range(count)]
    west = [pick(lane < by, forth[i - 1], forth[i]) for i in range(count)]
    return east, west


def forcing_kernel(
    thick, fields, south, north, count, old, part, depth, guess, to_east, to_west,
    block, mixed, wet, pack, edges, arrivals,
):
    level = pl.program_id(0)
    levels = pl.num_programs(0)
    static_levels = fields.shape[1]
    height, width = count.shape
    tiles = width // LANES
    ext = height + 2 * ROWS
    base = PAD + ROWS
    forcing_at = message_rows(static_levels)[0]
    lane = lane_index()
    cols = [pl.ds(t * LANES, LANES) for t in range(tiles)]
    both = range(tiles + 1)

    def arrival(at, t):
        return pltpu.make_async_copy(
            fields.at[:, at, :, cols[t]],
            block.at[at, :, t, pl.ds(base, height), :],
            arrivals.at[at, t],
        )

    @pl.when(level == 0)
    def _():
        for at in range(static_levels):
            for t in range(tiles):
                arrival(at, t).start()

    def extended(e, lower, middle, upper):
        if e < ROWS:
            return lower
        if e >= ROWS + height:
            return upper
        return middle(e - ROWS)

    def sweep(body, strips, unroll):
        lax.fori_loop(0, strips, lambda i, c: (body(i), c)[1], 0, unroll=unroll)

    @pl.when(level == 0)
    def _():
        for buf in (mixed, depth, guess):
            for at in (0, PAD + ext):
                buf[:, at : at + PAD, :] = jnp.zeros((buf.shape[0], PAD, LANES), jnp.float32)
        part[...] = jnp.zeros_like(part)
        pack[...] = jnp.zeros_like(pack)
        edges[...] = jnp.zeros_like(edges)
        for t, c in enumerate(cols):
            wet[t, :ROWS, :] = south[3 * static_levels, :, c]
            wet[t, ROWS : ROWS + height, :] = count[:, c].astype(jnp.float32)
            wet[t, ROWS + height :, :] = north[3 * static_levels, :, c]

    zonal, merid, baro = (block.at[level, f] for f in range(3))
    for f, buf in enumerate((zonal, merid, baro)):
        for t, c in enumerate(cols):
            buf[t, :PAD, :] = jnp.zeros((PAD, LANES), jnp.float32)
            buf[t, PAD:base, :] = south[f * static_levels + level, :, c]
            buf[t, base + height : PAD + ext, :] = north[f * static_levels + level, :, c]
            buf[t, PAD + ext :, :] = jnp.zeros((PAD, LANES), jnp.float32)
    for t in range(tiles):
        arrival(level, t).wait()

    def near(i, by=0):
        return pl.ds(PAD + i * STEP + by, STEP)

    def mix(i):
        east, west = neighbours([zonal[t, near(i), :] for t in range(tiles)] + [None], lane)
        for t in both:
            value = east[t] - west[t]
            if t < tiles:
                value += merid[t, near(i, 1), :] - merid[t, near(i, -1), :]
            mixed[t, near(i), :] = value

    sweep(mix, ext // STEP, MIX_UNROLL)
    thickness = thick[level]
    level_number = level.astype(jnp.float32)

    def spread(i):
        rows = pl.ds(ROWS - DEEP + i * STEP, STEP)
        near = lambda i, by=0: pl.ds(PAD + ROWS - DEEP + i * STEP + by, STEP)
        far, once, still = [], [], []
        for t in both:
            own = mixed[t, near(i), :]
            beside = mixed[t, near(i, 1), :] + mixed[t, near(i, -1), :]
            beyond = mixed[t, near(i, 2), :] + mixed[t, near(i, -2), :]
            once.append(2.0 * beside - 8.0 * own)
            still.append(beyond - 8.0 * beside + 20.0 * own)
            if t < tiles:
                pressure = 10.0 * baro[t, near(i), :]
                around = baro[t, near(i, 2), :] + baro[t, near(i, -2), :]
                own = own + pressure
                still[t] += 10.0 * around - 4.0 * pressure
            far.append(own)
        count_of = len(far)
        back = [turn(v, -1) for v in far]
        forth = [turn(v, 1) for v in far]
        last, first = lane == LANES - 1, lane == 0
        easts = [
            once[t] + jnp.where(last, back[(t + 1) % count_of], back[t]) for t in both
        ]
        wests = [once[t] + jnp.where(first, forth[t - 1], forth[t]) for t in both]
        back = [turn(v, -1) for v in easts]
        forth = [turn(v, 1) for v in wests]
        for t in both:
            total = still[t] + (
                jnp.where(last, back[(t + 1) % count_of], back[t])
                + jnp.where(first, forth[t - 1], forth[t])
            )
            if t < tiles:
                weight = jnp.where(wet[t, rows, :] > level_number, thickness, 0.0)
                part[t, rows, :] += weight * total
            else:
                pack[rows, :] += pltpu.roll(total, 8 * level + REACH, 1)

    sweep(spread, (height + 2 * DEEP) // STEP, SPREAD_UNROLL)

    @pl.when(level == levels - 1)
    def _():
        scale = -0.5 * VISCOSITY
        for e in range(0, ext, STEP):
            r = e + PAD
            begin = []
            for t, c in enumerate(cols):
                pressure = extended(
                    e,
                    south[3 * static_levels + 1, :, c],
                    lambda o: old[o : o + STEP, c],
                    north[3 * static_levels + 1, :, c],
                )
                counts = wet[t, e : e + STEP, :]
                deep = sum(
                    jnp.where(counts > float(k), thick[k], 0.0) for k in range(static_levels)
                )
                depth[t, r : r + STEP, :] = deep
                begin.append(jnp.where(counts > 0.0, pressure, 0.0))
                guess[t, r : r + STEP, :] = begin[t]
                part[t, e : e + STEP, :] *= scale
            tile = None
            for t, inner, start in ((tiles - 1, True, 0), (0, False, LANES // 2)):
                at = start
                for piece, size in (
                    (part[t, e : e + STEP, :], DEEP),
                    (wet[t, e : e + STEP, :], EDGE),
                    (begin[t], EDGE),
                ):
                    moved = turn(piece, at + size if inner else at)
                    inside = (lane >= at) & (lane < at + size)
                    tile = jnp.where(inside, moved, 0.0 if tile is None else tile)
                    at += size
            edges[e : e + STEP, :] = tile
        size = DEEP + 2 * EDGE
        for message in (to_east, to_west):
            message[...] = jnp.zeros_like(message)
        for at in range(0, to_east.shape[1], LANES):
            span = slice(at, at + LANES)
            turned = scale * jnp.transpose(pack[span, :])
            for k in range(static_levels):
                mine = slice(REACH * k, REACH * k + REACH)
                to_west[mine, span] = turned[8 * k : 8 * k + REACH, :]
                to_east[mine, span] = turned[8 * k + REACH : 8 * k + 2 * REACH, :]
            turned = jnp.transpose(edges[span, :])
            to_east[forcing_at : forcing_at + size, span] = turned[:size, :]
            to_west[forcing_at : forcing_at + size, span] = turned[
                LANES // 2 : LANES // 2 + size, :
            ]


def solve_kernel(
    thick, part, depth, guess, to_east, to_west, from_west, from_east,
    bases, diag, moments,
    turned, fix, halo_part, halo_depth, halo_guess, half, half_w, inverse, vec_e, vec_w, sums,
):
    tiles, ext, _ = part.shape
    height = ext - 2 * ROWS
    levels = thick.shape[0]
    forcing_at, count_at, pressure_at, _ = message_rows(levels)
    lane = lane_index()

    def weights(counts):
        return [jnp.where(counts > float(k), thick[k], 0.0) for k in range(levels)]

    def weighted(counts, message):
        total = None
        for k, weight in enumerate(weights(counts)):
            term = weight * message[REACH * k : REACH * k + REACH, :]
            total = term if total is None else total + term
        return total

    def rows(message, at, size):
        return message[at : at + size, :]

    skip = EDGE - REACH
    turned[...] = jnp.zeros_like(turned)
    turned[0:DEEP, :] = rows(from_east, forcing_at, DEEP)
    turned[0:REACH, :] += weighted(rows(from_east, count_at, REACH), to_east)
    turned[LANES - DEEP : LANES, :] = rows(from_west, forcing_at, DEEP)
    turned[LANES - REACH : LANES, :] += weighted(rows(from_west, count_at + skip, REACH), to_west)
    turned[40 : 40 + EDGE, :] = sum(weights(rows(from_east, count_at, EDGE)))
    turned[40 - EDGE : 40, :] = sum(weights(rows(from_west, count_at, EDGE)))
    turned[60 : 60 + EDGE, :] = rows(from_east, pressure_at, EDGE)
    turned[60 - EDGE : 60, :] = rows(from_west, pressure_at, EDGE)
    turned[80 : 80 + REACH, :] = weighted(rows(to_west, count_at, REACH), from_west)
    turned[80 - REACH : 80, :] = weighted(rows(to_east, count_at + skip, REACH), from_east)

    for buf in (halo_depth, halo_guess):
        for at in (0, PAD + ext):
            buf[at : at + PAD, :] = jnp.zeros((PAD, LANES), jnp.float32)
    for at in (0, PAD + ext):
        for buf in (half, half_w):
            buf[:, at : at + PAD, :] = jnp.zeros((tiles + 1, PAD, LANES), jnp.float32)
        for buf in (vec_e, vec_w):
            buf[:, :, at : at + PAD, :] = jnp.zeros((2, tiles + 1, PAD, LANES), jnp.float32)
    near = (lane < EDGE) | (lane >= LANES - EDGE)
    close = (lane < DEEP) | (lane >= LANES - DEEP)
    for at in range(0, ext, LANES):
        block = jnp.transpose(turned[:, at : at + LANES])
        for e in range(at, min(at + LANES, ext), STEP):
            r = e + PAD
            tile = block[e - at : e - at + STEP, :]
            halo_depth[r : r + STEP, :] = jnp.where(near, turn(tile, -40), 0.0)
            halo_guess[r : r + STEP, :] = jnp.where(near, turn(tile, -60), 0.0)
            halo_part[e : e + STEP, :] = jnp.where(close, tile, 0.0)
            fix[e : e + STEP, :] = turn(tile, -80)

    def sweep(body, strips, unroll, first=0, stride=1, carry=0):
        step = lambda i, c: body(first + stride * i, c)
        return lax.fori_loop(0, strips, step, carry, unroll=unroll)

    def span(i, by=0):
        return pl.ds(PAD + i * STEP + by, STEP)

    def strip(i):
        return pl.ds(pl.multiple_of(i * STEP, STEP), STEP)

    def read(main, halo, rows):
        return [main[t, rows, :] for t in range(tiles)] + [halo[rows, :]]

    both = range(tiles + 1)
    inner = height // STEP
    above = ROWS // STEP

    def put_beside(values, slot, i):
        east, west = neighbours(values, lane)
        for t in both:
            vec_e[slot, t, span(i), :] = east[t]
            vec_w[slot, t, span(i), :] = west[t]

    def prepare(i, c):
        low = [
            jnp.minimum(a, b)
            for a, b in zip(
                read(depth, halo_depth, span(i)), read(depth, halo_depth, span(i, 1))
            )
        ]
        east, _ = neighbours(low, lane)
        corner = [0.5 * jnp.minimum(a, b) for a, b in zip(low, east)]
        _, west = neighbours(corner, lane)
        for t in both:
            half[t, span(i), :] = corner[t]
            half_w[t, span(i), :] = west[t]
        put_beside(read(guess, halo_guess, span(i)), 0, i)
        return c

    sweep(prepare, ext // STEP, WIDE)

    def around(slot, t, i):
        return (
            (half[t, span(i), :], vec_e[slot, t, span(i, 1), :]),
            (half_w[t, span(i), :], vec_w[slot, t, span(i, 1), :]),
            (half[t, span(i, -1), :], vec_e[slot, t, span(i, -1), :]),
            (half_w[t, span(i, -1), :], vec_w[slot, t, span(i, -1), :]),
        )

    def begin(inside):
        def body(i, c):
            here = read(guess, halo_guess, span(i))
            wide = read(depth, halo_depth, span(i))
            fixes = fix[strip(i), :]
            values = []
            for t in both:
                (ch, ne), (chw, nw), (ch_s, se), (chw_s, sw) = around(0, t, i)
                diagonal = IMPLICIT + ((ch + chw) + (ch_s + chw_s))
                inv = 1.0 / diagonal
                inverse[t, strip(i), :] = inv
                image = IMPLICIT * here[t] + (
                    (ch * (here[t] - ne) + chw * (here[t] - nw))
                    + (ch_s * (here[t] - se) + chw_s * (here[t] - sw))
                )
                total = halo_part[strip(i), :] if t == tiles else part[t, strip(i), :]
                if t == 0:
                    total += jnp.where(lane < REACH, fixes, 0.0)
                if t == tiles - 1:
                    total += jnp.where(lane >= LANES - REACH, fixes, 0.0)
                side = jnp.where(wide[t] > 0.0, total + IMPLICIT * here[t], 0.0)
                values.append((side - image) * inv)
                if inside and t < tiles:
                    bases[0, t, strip(i - above), :] = values[t]
                    diag[t, strip(i - above), :] = diagonal
            put_beside(values, 1, i)
            return c

        return body

    sweep(begin(True), inner, WIDE_INNER, above)
    sweep(begin(False), 2, 2, 0, above + inner)

    zero = jnp.zeros((STEP, LANES), jnp.float32)

    def power(j, c):
        source, target = lax.rem(j + 1, 2), lax.rem(j, 2)

        def apply(inside):
            def body(i, carry):
                even, odd = carry
                values = []
                for t in both:
                    (ch, ne), (chw, nw), (ch_s, se), (chw_s, sw) = around(source, t, i)
                    value = inverse[t, strip(i), :] * (
                        (ch * ne + chw * nw) + (ch_s * se + chw_s * sw)
                    )
                    values.append(value)
                    if inside and t < tiles:
                        now = bases[j, t, strip(i - above), :]
                        scaled = diag[t, strip(i - above), :] * now
                        even = even + scaled * now
                        odd = odd + scaled * value
                        bases[j + 1, t, strip(i - above), :] = value
                put_beside(values, target, i)
                return even, odd

            return body

        even, odd = sweep(apply(True), inner, WIDE_INNER, above, 1, (zero, zero))
        sweep(apply(False), 2, 2, 0, above + inner, (zero, zero))
        sums[2 * j] = even
        sums[2 * j + 1] = odd
        return c

    lax.fori_loop(0, ITERS, power, 0)
    lane_row = lax.broadcasted_iota(jnp.int32, (1, LANES), 1)
    found = jnp.zeros((1, LANES), jnp.float32)
    for m in range(2 * ITERS):
        found = jnp.where(lane_row == m, jnp.sum(sums[m]), found)
    for d in range(moments.shape[0]):
        moments[d] = found


def combine_kernel(moments, guess, bases, diag, pressure, residual):
    height, width = pressure.shape
    total = jnp.sum(moments[...], axis=0)
    h = [jnp.broadcast_to(total[:, m : m + 1], (STEP, LANES)) for m in range(2 * ITERS)]
    one, zero = jnp.ones((STEP, LANES), jnp.float32), None

    def plus(a, b):
        return b if a is None else a if b is None else a + b

    def times(a, b):
        return None if a is None or b is None else a * b

    def minus_n(poly):
        moved = [zero] + list(poly)
        return [
            a if b is None else (-b if a is None else a - b)
            for a, b in zip(list(poly) + [zero], moved)
        ]

    def inner(left, right):
        total = None
        for i, a in enumerate(left):
            part = None
            for j, b in enumerate(right):
                part = plus(part, times(b, h[i + j]))
            total = plus(total, times(a, part))
        return total

    rest, direction, answer = [one], [one], []
    norm = h[0]
    for iteration in range(ITERS):
        image = minus_n(direction)
        alpha = norm / inner(direction, image)
        answer = [
            plus(answer[i] if i < len(answer) else None, alpha * c)
            for i, c in enumerate(direction)
        ]
        rest = [
            plus(rest[i] if i < len(rest) else None, -(alpha * c)) for i, c in enumerate(image)
        ]
        if iteration + 1 < ITERS:
            following = inner(rest, rest)
            ratio = following / norm
            direction = [
                plus(c, ratio * direction[i] if i < len(direction) else None)
                for i, c in enumerate(rest)
            ]
            norm = following
    for t in range(width // LANES):
        for o in range(0, height, STEP):
            vecs = [bases[b, t, o : o + STEP, :] for b in range(ITERS + 1)]
            moved = sum(c * v for c, v in zip(answer, vecs))
            left = sum(c * v for c, v in zip(rest, vecs))
            at = PAD + ROWS + o
            cols = pl.ds(t * LANES, LANES)
            pressure[o : o + STEP, cols] = guess[t, at : at + STEP, :] + moved
            residual[o : o + STEP, cols] = diag[t, o : o + STEP, :] * left


def shift(value, axis, by):
    size = lax.axis_size(axis)
    return lax.ppermute(value, axis, [(i, (i + by) % size) for i in range(size)])


def shards(fields, level_count, thickness, old_pressure):
    levels, height, width = fields.shape[1:]
    ext, tall = height + 2 * ROWS, height + LANES
    f32 = jnp.float32

    def edge(at):
        pick = lambda a: lax.slice_in_dim(a, at, at + ROWS, axis=a.ndim - 2)
        flat = pick(fields).reshape(3 * levels, ROWS, width)
        return jnp.concatenate(
            [flat, pick(level_count).astype(f32)[None], pick(old_pressure)[None]], axis=0
        )

    south = shift(edge(height - ROWS), "by", 1)
    north = shift(edge(0), "by", -1)

    message = message_rows(levels)[3]
    tiles, padded = width // LANES, ext + 2 * PAD
    smem = pl.BlockSpec(memory_space=pltpu.SMEM)
    vmem = pl.BlockSpec(memory_space=pltpu.VMEM)
    whole = lambda *dims: pl.BlockSpec(dims, lambda k: (0,) * len(dims))
    hbm = pl.BlockSpec(memory_space=pl.ANY)
    halo = whole(3 * levels + 2, ROWS, width)
    shaped = lambda *dims: jax.ShapeDtypeStruct(dims, f32)
    scratch = lambda *dims: pltpu.VMEM(dims, f32)
    main = (tiles, ext, LANES)
    loose = (tiles, padded, LANES)
    results = (main, loose, loose, (message, tall), (message, tall))
    part, depth, guess, to_east, to_west = pl.pallas_call(
        forcing_kernel,
        grid=(levels,),
        in_specs=[
            smem,
            hbm, halo, halo,
            whole(height, width), whole(height, width),
        ],
        out_specs=[whole(*dims) for dims in results],
        out_shape=[shaped(*dims) for dims in results],
        scratch_shapes=[
            scratch(levels, 3, *loose),
            scratch(tiles + 1, padded, LANES),
            scratch(*main),
            scratch(tall, LANES),
            scratch(tall, LANES),
            pltpu.SemaphoreType.DMA((levels, tiles)),
        ],
        name="forcing",
    )(thickness, fields, south, north, level_count, old_pressure)

    from_west = shift(to_east, "bx", 1)
    from_east = shift(to_west, "bx", -1)

    devices = lax.axis_size("by") * lax.axis_size("bx")
    bases, diag, moments = pl.pallas_call(
        solve_kernel,
        in_specs=[smem] + [vmem] * 7,
        out_specs=[vmem] * 3,
        out_shape=[
            shaped(ITERS + 1, tiles, height, LANES),
            shaped(tiles, height, LANES),
            shaped(devices, 1, LANES),
        ],
        scratch_shapes=[scratch(LANES, tall), scratch(ext, LANES), scratch(ext, LANES)]
        + [scratch(padded, LANES)] * 2
        + [scratch(tiles + 1, padded, LANES)] * 2
        + [scratch(tiles + 1, ext, LANES)]
        + [scratch(2, tiles + 1, padded, LANES)] * 2
        + [scratch(2 * ITERS, STEP, LANES)],
        name="krylov",
    )(thickness, part, depth, guess, to_east, to_west, from_west, from_east)

    moments = lax.all_to_all(moments, ("by", "bx"), split_axis=0, concat_axis=0, tiled=True)
    return tuple(
        pl.pallas_call(
            combine_kernel,
            in_specs=[vmem] * 4,
            out_specs=[vmem] * 2,
            out_shape=[shaped(height, width)] * 2,
            name="combine",
        )(moments, guess, bases, diag)
    )


def solution(mesh):
    placed = (P(None, None, "by", "bx"), P("by", "bx"), P(), P("by", "bx"))
    return jax.shard_map(
        shards,
        mesh=mesh,
        in_specs=placed,
        out_specs=(P("by", "bx"), P("by", "bx")),
        check_vma=False,
    )
```

time: 70.3 us -> 67.8 us (0.964)
  Pallas kernels: 35.3 us -> 32.8 us
    pallas_call x2, Pallas kernels: 28.7 us -> 16.6 us  [the longest x1 14 us: shards(): pl.pallas_call(forcing_kernel, grid=(levels,), in_specs=[smem, hbm, halo,...]
    pallas_call x1, Pallas kernels: 6.56 us -> 16.2 us  [shards(): pl.pallas_call(solve_kernel, in_specs=[smem] + [vmem] * 7, out_specs=[vme...]
    convert_element_type x1 -> x0, other arithmetic: 0.97 us -> none  [shards(): counts = level_count.astype(f32)]
    broadcast_in_dim x0 -> x1, other arithmetic: none -> 0.72 us  [edge(): pick(level_count).astype(f32)[None]]
where the time goes in v3:
time: 67.8 us; the launch traced here: 67.4 us
  Pallas kernels  32.8 us (48%)
  blocking collectives  14.3 us (21%)
  waiting for transfers between devices  8.51 us (13%)
  starting transfers between devices  7.33 us (11%)
  local copies, waits for them, and re-layouts  3.09 us (5%)
  other arithmetic  0.75 us (1%)
    pallas_call x1, Pallas kernels, shards(): pl.pallas_call(solve_kernel, in_specs=[smem] + [vmem] * 7, out_specs=[vme...  16.2 us
    all_to_all x1, blocking collectives, shards(): lax.all_to_all(moments, ('by', 'bx'), split_axis=0, concat_axis=0, tiled=...  14.3 us
    pallas_call x1, Pallas kernels, shards(): pl.pallas_call(forcing_kernel, grid=(levels,), in_specs=[smem, hbm, halo,...  14 us
    ppermute x4, waiting for transfers between devices, shift(): lax.ppermute(value, axis, [(i, (i + by) % size) for i in range(size)])  8.51 us
    ppermute x4, starting transfers between devices, shift(): lax.ppermute(value, axis, [(i, (i + by) % size) for i in range(size)])  7.33 us
    pallas_call x1, Pallas kernels, shards(): pl.pallas_call(combine_kernel, in_specs=[vmem] * 4, out_specs=[vmem] * 2,...  2.54 us
  transfers between devices with their start and end apart: 4, of which 3 were waited for; matrix products, arithmetic and copies ran while one was open for 0% of the time, Pallas kernels for 0%

profile of v3, /device:TPU:0, one launch (start us, length us, event | category | flops | bytes accessed | tf_op | source)
XLA Modules:
  0.0 67.4 jit_solution(15714286762223652201)
XLA Ops:
  0.6 0.7 %convert_bitcast_fusion = (f32[1,8,256]{2,1,0:T(8,128)S(1)}, f32[1,8,256]{2,1,0:T(8,128)S(1)}) fusion(s32[256,256]{1,0:T(8,128)} %count.1), kind=kLoop, calls=%fused_computation.3 | loop fusion | flops 4096 | bytes 32768 | tf_op jit(solution)/shard_map/broadcast_in_dim | solution.py:478
  1.4 0.7 %slice_bitcast_fusion = (f32[1,8,256]{2,1,0:T(8,128)S(1)}, f32[1,8,256]{2,1,0:T(8,128)S(1)}) fusion(f32[256,256]{1,0:T(8,128)} %old.1), kind=kLoop, calls=%fused_computation.2 | loop fusion | bytes 32768 | tf_op jit(solution)/shard_map/broadcast_in_dim | solution.py:478
  2.1 1.0 %fusion = (f32[3,8,8,256]{3,2,1,0:T(8,128)S(1)}, f32[3,8,8,256]{3,2,1,0:T(8,128)S(1)}) fusion(f32[3,8,256,256]{3,2,1,0:T(8,128)} %fields.1), kind=kLoop, calls=%fused_computation.6 | loop fusion | bytes 786432 | tf_op jit(solution)/shard_map/slice | solution.py:475
  3.1 0.5 collective-permute-start
  3.7 2.0 %collective-permute-start.1 = (f32[26,8,256]{2,1,0:T(8,128)S(1)}, f32[26,8,256]{2,1,0:T(8,128)S(1)}, u32[]{:S(2)}, u32[]{:S(2)}) collective-permute-start(f32[26,8,256]{2,1,0:T(8,128)S(1)} %pad_maximum_fusion.1), channel_id=1, source_target_pairs={{0,24},{8,0},{16,8},{24,16},{1,25},{9,1},{17,9},{25,17},{2,26},{10... | collective-permute-start | bytes 638984 | tf_op jit(solution)/shard_map/ppermute | solution.py:466
  5.7 3.4 %collective-permute-done.south = f32[26,8,256]{2,1,0:T(8,128)S(1)} collective-permute-done((f32[26,8,256]{2,1,0:T(8,128)S(1)}, f32[26,8,256]{2,1,0:T(8,128)S(1)}, u32[]{:S(2)}, u32[]{:S(2)}) %collective-permute-start) | collective-permute-done | bytes 213024 | tf_op jit(solution)/shard_map/ppermute | solution.py:466
  9.2 0.0 copy-start
  9.2 2.1 %collective-permute-done.1.north = f32[26,8,256]{2,1,0:T(8,128)S(1)} collective-permute-done((f32[26,8,256]{2,1,0:T(8,128)S(1)}, f32[26,8,256]{2,1,0:T(8,128)S(1)}, u32[]{:S(2)}, u32[]{:S(2)}) %collective-permute-start.1) | collective-permute-done | bytes 213024 | tf_op jit(solution)/shard_map/ppermute | solution.py:466
  11.3 0.0 copy-done
  11.3 0.0 copy-start.1
  11.3 0.7 %copy-done.1 = f32[26,8,256]{2,1,0:T(8,128)} copy-done((f32[26,8,256]{2,1,0:T(8,128)}, f32[26,8,256]{2,1,0:T(8,128)S(1)}, u32[]{:S(2)}) %copy-start.1) | copy-done | bytes 213016
  11.9 14.0 %forcing.1 = (f32[2,272,128]{2,1,0:T(8,128)}, f32[2,288,128]{2,1,0:T(8,128)}, f32[2,288,128]{2,1,0:T(8,128)}, f32[40,384]{1,0:T(8,128)}, f32[40,384]{1,0:T(8,128)}) custom-call(f32[8]{0:T(128)} %thick.3, f32[3,8,256,256]{3,2,1,0:T(8,128)} %fields.1, f32[26,8,256]{2,1,0:T(8,128)} %copy-done, f32[26,8,256]{2,1,0:T(8,128)} %copy-done.1, s32[256,256]{1,0:T(8,128)} %count.1, ...), custom_call_target="tpu_custom_call" | custom-call | tf_op jit(solution)/shard_map/forcing/pallas_call | solution.py:496
  26.0 1.5 %collective-permute-start.2 = (f32[40,384]{1,0:T(8,128)}, f32[40,384]{1,0:T(8,128)S(1)}, u32[]{:S(2)}, u32[]{:S(2)}) collective-permute-start(f32[40,384]{1,0:T(8,128)} %get-tuple-element.13.to_east), channel_id=1, source_target_pairs={{0,1},{1,2},{2,3},{3,4},{4,5},{5,6},{6,7},{7,0},{8,9},{9,10},{10,1... | collective-permute-start | bytes 184328 | tf_op jit(solution)/shard_map/ppermute | solution.py:466
  27.5 3.2 %collective-permute-start.3 = (f32[40,384]{1,0:T(8,128)}, f32[40,384]{1,0:T(8,128)S(1)}, u32[]{:S(2)}, u32[]{:S(2)}) collective-permute-start(f32[40,384]{1,0:T(8,128)} %get-tuple-element.14.to_west), channel_id=1, source_target_pairs={{0,7},{1,0},{2,1},{3,2},{4,3},{5,4},{6,5},{7,6},{8,15},{9,8},{10,9... | collective-permute-start | bytes 184328 | tf_op jit(solution)/shard_map/ppermute | solution.py:466
  30.8 3.0 %collective-permute-done.2.from_west = f32[40,384]{1,0:T(8,128)S(1)} collective-permute-done((f32[40,384]{1,0:T(8,128)}, f32[40,384]{1,0:T(8,128)S(1)}, u32[]{:S(2)}, u32[]{:S(2)}) %collective-permute-start.2) | collective-permute-done | bytes 61472 | tf_op jit(solution)/shard_map/ppermute | solution.py:466
  33.7 0.0 copy-start.2
  33.7 0.0 collective-permute-done.3.from_east
  33.7 0.0 copy-start.3
  33.7 0.6 copy-done.2
  34.4 0.0 copy-done.3
  34.4 16.2 %krylov.1 = (f32[5,2,256,128]{3,2,1,0:T(8,128)}, f32[2,256,128]{2,1,0:T(8,128)}, f32[32,1,128]{2,1,0:T(1,128)}) custom-call(f32[8]{0:T(128)} %thick.3, f32[2,272,128]{2,1,0:T(8,128)} %get-tuple-element.10.part, f32[2,288,128]{2,1,0:T(8,128)} %get-tuple-element.11.depth, f32[2,288,128]{2,1,0:T(8,128)} %get-tuple-element.12.guess, ...), custom_call_target="tpu_custom_call" | custom-call | tf_op jit(solution)/shard_map/krylov/pallas_call | solution.py:521
  50.6 14.3 %all_to_all.5.moments = f32[32,1,128]{2,1,0:T(1,128)} all-to-all(f32[32,1,128]{2,1,0:T(1,128)} %get-tuple-element.15), channel_id=1, replica_groups=mesh['by'=4,'bx'=8] {'by','bx'}, dimensions={0} | all-to-all | bytes 32768 | tf_op jit(solution)/shard_map/all_to_all | solution.py:539
  64.9 2.5 %combine.1 = (f32[256,256]{1,0:T(8,128)}, f32[256,256]{1,0:T(8,128)}) custom-call(f32[32,1,128]{2,1,0:T(1,128)} %all_to_all.5.moments, f32[2,288,128]{2,1,0:T(8,128)} %get-tuple-element.12.guess, f32[5,2,256,128]{3,2,1,0:T(8,128)} %get-tuple-element.16.bases, f32[2,256,128]{2,1,0:T(8,128)} %get-tuple-element.17.diag), custom_call_target="tpu_custom_call" | custom-call | tf_op jit(solution)/shard_map/combine/pallas_call | solution.py:541
  (2 shorter events, 0.0 us)
Async XLA Ops:
  3.1 6.0 %collective-permute-start = (f32[26,8,256]{2,1,0:T(8,128)S(1)}, f32[26,8,256]{2,1,0:T(8,128)S(1)}, u32[]{:S(2)}, u32[]{:S(2)}) collective-permute-start(f32[26,8,256]{2,1,0:T(8,128)S(1)} %pad_maximum_fusion), channel_id=1, source_target_pairs={{0,8},{8,16},{16,24},{24,0},{1,9},{9,17},{17,25},{25,1},{2,10},{10... | collective-permute-start | bytes 638984 | tf_op jit(solution)/shard_map/ppermute | solution.py:466
  3.7 7.6 %collective-permute-start.1 = (f32[26,8,256]{2,1,0:T(8,128)S(1)}, f32[26,8,256]{2,1,0:T(8,128)S(1)}, u32[]{:S(2)}, u32[]{:S(2)}) collective-permute-start(f32[26,8,256]{2,1,0:T(8,128)S(1)} %pad_maximum_fusion.1), channel_id=1, source_target_pairs={{0,24},{8,0},{16,8},{24,16},{1,25},{9,1},{17,9},{25,17},{2,26},{10... | collective-permute-start | bytes 638984 | tf_op jit(solution)/shard_map/ppermute | solution.py:466
  9.2 2.1 %copy-start = (f32[26,8,256]{2,1,0:T(8,128)}, f32[26,8,256]{2,1,0:T(8,128)S(1)}, u32[]{:S(2)}) copy-start(f32[26,8,256]{2,1,0:T(8,128)S(1)} %collective-permute-done.south) | copy-start | bytes 638980
  11.3 0.7 %copy-start.1 = (f32[26,8,256]{2,1,0:T(8,128)}, f32[26,8,256]{2,1,0:T(8,128)S(1)}, u32[]{:S(2)}) copy-start(f32[26,8,256]{2,1,0:T(8,128)S(1)} %collective-permute-done.1.north) | copy-start | bytes 638980
  26.0 7.7 %collective-permute-start.2 = (f32[40,384]{1,0:T(8,128)}, f32[40,384]{1,0:T(8,128)S(1)}, u32[]{:S(2)}, u32[]{:S(2)}) collective-permute-start(f32[40,384]{1,0:T(8,128)} %get-tuple-element.13.to_east), channel_id=1, source_target_pairs={{0,1},{1,2},{2,3},{3,4},{4,5},{5,6},{6,7},{7,0},{8,9},{9,10},{10,1... | collective-permute-start | bytes 184328 | tf_op jit(solution)/shard_map/ppermute | solution.py:466
  27.5 6.2 %collective-permute-start.3 = (f32[40,384]{1,0:T(8,128)}, f32[40,384]{1,0:T(8,128)S(1)}, u32[]{:S(2)}, u32[]{:S(2)}) collective-permute-start(f32[40,384]{1,0:T(8,128)} %get-tuple-element.14.to_west), channel_id=1, source_target_pairs={{0,7},{1,0},{2,1},{3,2},{4,3},{5,4},{6,5},{7,6},{8,15},{9,8},{10,9... | collective-permute-start | bytes 184328 | tf_op jit(solution)/shard_map/ppermute | solution.py:466
  33.7 0.6 copy-start.2
  33.7 0.6 copy-start.3

commit v4 on v3

--- a/solution.py
+++ b/solution.py
@@ -17,10 +17,11 @@
 EDGE = ITERS + 1
 
 STEP = 8
+GRANT = 16 * 2**20
 MIX_UNROLL = 17
 SPREAD_UNROLL = 11
 WIDE = 17
-WIDE_INNER = 8
+WIDE_INNER = 16
 
 
 def message_rows(levels):
@@ -224,8 +225,8 @@
 
 def solve_kernel(
     thick, part, depth, guess, to_east, to_west, from_west, from_east,
-    bases, diag, moments,
-    turned, fix, halo_part, halo_depth, halo_guess, half, half_w, inverse, vec_e, vec_w, sums,
+    base0, base1, base2, base3, base4, diag, moments,
+    turned, fix, halo_part, halo_depth, halo_guess, half, half_w, inverse, even_e, even_w, odd_e, odd_w,
 ):
     tiles, ext, _ = part.shape
     height = ext - 2 * ROWS
@@ -263,10 +264,8 @@
         for at in (0, PAD + ext):
             buf[at : at + PAD, :] = jnp.zeros((PAD, LANES), jnp.float32)
     for at in (0, PAD + ext):
-        for buf in (half, half_w):
+        for buf in (half, half_w, even_e, even_w, odd_e, odd_w):
             buf[:, at : at + PAD, :] = jnp.zeros((tiles + 1, PAD, LANES), jnp.float32)
-        for buf in (vec_e, vec_w):
-            buf[:, :, at : at + PAD, :] = jnp.zeros((2, tiles + 1, PAD, LANES), jnp.float32)
     near = (lane < EDGE) | (lane >= LANES - EDGE)
     close = (lane < DEEP) | (lane >= LANES - DEEP)
     for at in range(0, ext, LANES):
@@ -292,6 +291,8 @@
     def read(main, halo, rows):
         return [main[t, rows, :] for t in range(tiles)] + [halo[rows, :]]
 
+    shifted = ((even_e, even_w), (odd_e, odd_w))
+    bases = (base0, base1, base2, base3, base4)
     both = range(tiles + 1)
     inner = height // STEP
     above = ROWS // STEP
@@ -299,8 +300,8 @@
     def put_beside(values, slot, i):
         east, west = neighbours(values, lane)
         for t in both:
-            vec_e[slot, t, span(i), :] = east[t]
-            vec_w[slot, t, span(i), :] = west[t]
+            shifted[slot][0][t, span(i), :] = east[t]
+            shifted[slot][1][t, span(i), :] = west[t]
 
     def prepare(i, c):
         low = [
@@ -321,11 +322,12 @@
     sweep(prepare, ext // STEP, WIDE)
 
     def around(slot, t, i):
+        vec_e, vec_w = shifted[slot]
         return (
-            (half[t, span(i), :], vec_e[slot, t, span(i, 1), :]),
-            (half_w[t, span(i), :], vec_w[slot, t, span(i, 1), :]),
-            (half[t, span(i, -1), :], vec_e[slot, t, span(i, -1), :]),
-            (half_w[t, span(i, -1), :], vec_w[slot, t, span(i, -1), :]),
+            (half[t, span(i), :], vec_e[t, span(i, 1), :]),
+            (half_w[t, span(i), :], vec_w[t, span(i, 1), :]),
+            (half[t, span(i, -1), :], vec_e[t, span(i, -1), :]),
+            (half_w[t, span(i, -1), :], vec_w[t, span(i, -1), :]),
         )
 
     def begin(inside):
@@ -351,7 +353,7 @@
                 side = jnp.where(wide[t] > 0.0, total + IMPLICIT * here[t], 0.0)
                 values.append((side - image) * inv)
                 if inside and t < tiles:
-                    bases[0, t, strip(i - above), :] = values[t]
+                    base0[t, strip(i - above), :] = values[t]
                     diag[t, strip(i - above), :] = diagonal
             put_beside(values, 1, i)
             return c
@@ -363,37 +365,37 @@
 
     zero = jnp.zeros((STEP, LANES), jnp.float32)
 
-    def power(j, c):
-        source, target = lax.rem(j + 1, 2), lax.rem(j, 2)
-
-        def apply(inside):
+    sums = []
+    for j in range(ITERS):
+        final = j + 1 == ITERS
+
+        def apply(inside, j=j, final=final):
             def body(i, carry):
                 even, odd = carry
                 values = []
                 for t in both:
-                    (ch, ne), (chw, nw), (ch_s, se), (chw_s, sw) = around(source, t, i)
+                    if final and t == tiles:
+                        continue
+                    (ch, ne), (chw, nw), (ch_s, se), (chw_s, sw) = around((j + 1) % 2, t, i)
                     value = inverse[t, strip(i), :] * (
                         (ch * ne + chw * nw) + (ch_s * se + chw_s * sw)
                     )
                     values.append(value)
                     if inside and t < tiles:
-                        now = bases[j, t, strip(i - above), :]
+                        now = bases[j][t, strip(i - above), :]
                         scaled = diag[t, strip(i - above), :] * now
                         even = even + scaled * now
                         odd = odd + scaled * value
-                        bases[j + 1, t, strip(i - above), :] = value
-                put_beside(values, target, i)
+                        bases[j + 1][t, strip(i - above), :] = value
+                if not final:
+                    put_beside(values, j % 2, i)
                 return even, odd
 
             return body
 
-        even, odd = sweep(apply(True), inner, WIDE_INNER, above, 1, (zero, zero))
-        sweep(apply(False), 2, 2, 0, above + inner, (zero, zero))
-        sums[2 * j] = even
-        sums[2 * j + 1] = odd
-        return c
-
-    lax.fori_loop(0, ITERS, power, 0)
+        sums += sweep(apply(True), inner, WIDE_INNER, above, 1, (zero, zero))
+        if not final:
+            sweep(apply(False), 2, 2, 0, above + inner, (zero, zero))
     lane_row = lax.broadcasted_iota(jnp.int32, (1, LANES), 1)
     found = jnp.zeros((1, LANES), jnp.float32)
     for m in range(2 * ITERS):
@@ -402,7 +404,7 @@
         moments[d] = found
 
 
-def combine_kernel(moments, guess, bases, diag, pressure, residual):
+def combine_kernel(moments, guess, base0, base1, base2, base3, base4, diag, pressure, residual):
     height, width = pressure.shape
     total = jnp.sum(moments[...], axis=0)
     h = [jnp.broadcast_to(total[:, m : m + 1], (STEP, LANES)) for m in range(2 * ITERS)]
@@ -450,9 +452,10 @@
                 for i, c in enumerate(rest)
             ]
             norm = following
+    bases = (base0, base1, base2, base3, base4)
     for t in range(width // LANES):
         for o in range(0, height, STEP):
-            vecs = [bases[b, t, o : o + STEP, :] for b in range(ITERS + 1)]
+            vecs = [b[t, o : o + STEP, :] for b in bases]
             moved = sum(c * v for c, v in zip(answer, vecs))
             left = sum(c * v for c, v in zip(rest, vecs))
             at = PAD + ROWS + o
@@ -511,6 +514,7 @@
             scratch(tall, LANES),
             pltpu.SemaphoreType.DMA((levels, tiles)),
         ],
+        compiler_params=pltpu.CompilerParams(vmem_limit_bytes=GRANT),
         name="forcing",
     )(thickness, fields, south, north, level_count, old_pressure)
 
@@ -518,21 +522,20 @@
     from_east = shift(to_west, "bx", -1)
 
     devices = lax.axis_size("by") * lax.axis_size("bx")
-    bases, diag, moments = pl.pallas_call(
+    *bases, diag, moments = pl.pallas_call(
         solve_kernel,
         in_specs=[smem] + [vmem] * 7,
-        out_specs=[vmem] * 3,
+        out_specs=[vmem] * (ITERS + 3),
         out_shape=[
-            shaped(ITERS + 1, tiles, height, LANES),
-            shaped(tiles, height, LANES),
+            *[shaped(tiles, height, LANES)] * (ITERS + 2),
             shaped(devices, 1, LANES),
         ],
         scratch_shapes=[scratch(LANES, tall), scratch(ext, LANES), scratch(ext, LANES)]
         + [scratch(padded, LANES)] * 2
         + [scratch(tiles + 1, padded, LANES)] * 2
         + [scratch(tiles + 1, ext, LANES)]
-        + [scratch(2, tiles + 1, padded, LANES)] * 2
-        + [scratch(2 * ITERS, STEP, LANES)],
+        + [scratch(tiles + 1, padded, LANES)] * 4,
+        compiler_params=pltpu.CompilerParams(vmem_limit_bytes=GRANT),
         name="krylov",
     )(thickness, part, depth, guess, to_east, to_west, from_west, from_east)
 
@@ -540,11 +543,12 @@
     return tuple(
         pl.pallas_call(
             combine_kernel,
-            in_specs=[vmem] * 4,
+            in_specs=[vmem] * (ITERS + 4),
             out_specs=[vmem] * 2,
             out_shape=[shaped(height, width)] * 2,
+            compiler_params=pltpu.CompilerParams(vmem_limit_bytes=GRANT),
             name="combine",
-        )(moments, guess, bases, diag)
+        )(moments, guess, *bases, diag)
     )
 
 

time: 67.8 us -> 55.9 us (0.82)
  Pallas kernels: 32.8 us -> 18 us
  local copies, waits for them, and re-layouts: 3.09 us -> 7.1 us
  blocking collectives: 14.3 us -> 13.3 us
    pallas_call x1, Pallas kernels: 16.2 us -> 5.16 us  [shards(): pl.pallas_call(solve_kernel, in_specs=[smem] + [vmem] * 7, out_specs=[vme...]
    unnamed x8, local copies, waits for them, and re-layouts: 1.33 us -> 5.34 us
    pallas_call x1, Pallas kernels: 14 us -> 11.7 us  [shards(): pl.pallas_call(forcing_kernel, grid=(levels,), in_specs=[smem, hbm, halo,...]
    pallas_call x1, Pallas kernels: 2.54 us -> 1.18 us  [shards(): pl.pallas_call(combine_kernel, in_specs=[vmem] * (ITERS + 4), out_specs=[...]
    all_to_all x1, blocking collectives: 14.3 us -> 13.3 us  [shards(): lax.all_to_all(moments, ('by', 'bx'), split_axis=0, concat_axis=0, tiled=...]
where the time goes in v4:
time: 55.9 us; the launch traced here: 55.5 us
  Pallas kernels  18 us (32%)
  blocking collectives  13.3 us (24%)
  waiting for transfers between devices  8.3 us (15%)
  starting transfers between devices  7.33 us (13%)
  local copies, waits for them, and re-layouts  7.1 us (13%)
  other arithmetic  0.75 us (1%)
  between operations  0.67 us (1%)
    all_to_all x1, blocking collectives, shards(): lax.all_to_all(moments, ('by', 'bx'), split_axis=0, concat_axis=0, tiled=...  13.3 us
    pallas_call x1, Pallas kernels, shards(): pl.pallas_call(forcing_kernel, grid=(levels,), in_specs=[smem, hbm, halo,...  11.7 us
    ppermute x4, waiting for transfers between devices, shift(): lax.ppermute(value, axis, [(i, (i + by) % size) for i in range(size)])  8.3 us
    ppermute x4, starting transfers between devices, shift(): lax.ppermute(value, axis, [(i, (i + by) % size) for i in range(size)])  7.33 us
    unnamed x8, local copies, waits for them, and re-layouts  5.34 us
    pallas_call x1, Pallas kernels, shards(): pl.pallas_call(solve_kernel, in_specs=[smem] + [vmem] * 7, out_specs=[vme...  5.16 us
    pallas_call x1, Pallas kernels, shards(): pl.pallas_call(combine_kernel, in_specs=[vmem] * (ITERS + 4), out_specs=[...  1.18 us
  transfers between devices with their start and end apart: 4, of which 3 were waited for; matrix products, arithmetic and copies ran while one was open for 0% of the time, Pallas kernels for 0%

profile of v4, /device:TPU:0, one launch (start us, length us, event | category | flops | bytes accessed | tf_op | source)
XLA Modules:
  0.0 55.5 jit_solution(5169480160353695649)
XLA Ops:
  0.6 0.7 %convert_bitcast_fusion = (f32[1,8,256]{2,1,0:T(8,128)S(1)}, f32[1,8,256]{2,1,0:T(8,128)S(1)}) fusion(s32[256,256]{1,0:T(8,128)} %count.1), kind=kLoop, calls=%fused_computation.3 | loop fusion | flops 4096 | bytes 32768 | tf_op jit(solution)/shard_map/broadcast_in_dim | solution.py:481
  1.4 0.7 %slice_bitcast_fusion = (f32[1,8,256]{2,1,0:T(8,128)S(1)}, f32[1,8,256]{2,1,0:T(8,128)S(1)}) fusion(f32[256,256]{1,0:T(8,128)} %old.1), kind=kLoop, calls=%fused_computation.2 | loop fusion | bytes 32768 | tf_op jit(solution)/shard_map/broadcast_in_dim | solution.py:481
  2.1 1.0 %fusion = (f32[3,8,8,256]{3,2,1,0:T(8,128)S(1)}, f32[3,8,8,256]{3,2,1,0:T(8,128)S(1)}) fusion(f32[3,8,256,256]{3,2,1,0:T(8,128)} %fields.1), kind=kLoop, calls=%fused_computation.6 | loop fusion | bytes 786432 | tf_op jit(solution)/shard_map/slice | solution.py:478
  3.1 0.5 collective-permute-start
  3.7 2.0 %collective-permute-start.1 = (f32[26,8,256]{2,1,0:T(8,128)S(1)}, f32[26,8,256]{2,1,0:T(8,128)S(1)}, u32[]{:S(2)}, u32[]{:S(2)}) collective-permute-start(f32[26,8,256]{2,1,0:T(8,128)S(1)} %pad_maximum_fusion.1), channel_id=1, source_target_pairs={{0,24},{8,0},{16,8},{24,16},{1,25},{9,1},{17,9},{25,17},{2,26},{10... | collective-permute-start | bytes 638984 | tf_op jit(solution)/shard_map/ppermute | solution.py:469
  5.7 3.4 %collective-permute-done.south = f32[26,8,256]{2,1,0:T(8,128)S(1)} collective-permute-done((f32[26,8,256]{2,1,0:T(8,128)S(1)}, f32[26,8,256]{2,1,0:T(8,128)S(1)}, u32[]{:S(2)}, u32[]{:S(2)}) %collective-permute-start) | collective-permute-done | bytes 213024 | tf_op jit(solution)/shard_map/ppermute | solution.py:469
  9.2 2.1 %collective-permute-done.1.north = f32[26,8,256]{2,1,0:T(8,128)S(1)} collective-permute-done((f32[26,8,256]{2,1,0:T(8,128)S(1)}, f32[26,8,256]{2,1,0:T(8,128)S(1)}, u32[]{:S(2)}, u32[]{:S(2)}) %collective-permute-start.1) | collective-permute-done | bytes 213024 | tf_op jit(solution)/shard_map/ppermute | solution.py:469
  11.3 0.0 copy-start
  11.3 2.8 %copy-done = f32[3,8,256,256]{3,2,1,0:T(8,128)S(1)} copy-done((f32[3,8,256,256]{3,2,1,0:T(8,128)S(1)}, f32[3,8,256,256]{3,2,1,0:T(8,128)}, u32[]{:S(2)}) %copy-start) | copy-done | bytes 6291480
  14.0 0.0 copy-start.1
  14.0 0.9 %copy-done.1 = f32[256,256]{1,0:T(8,128)S(1)} copy-done((f32[256,256]{1,0:T(8,128)S(1)}, f32[256,256]{1,0:T(8,128)}, u32[]{:S(2)}) %copy-start.1) | copy-done | bytes 262168
  15.0 0.0 copy-start.2
  15.0 0.9 %copy-done.2 = s32[256,256]{1,0:T(8,128)S(1)} copy-done((s32[256,256]{1,0:T(8,128)S(1)}, s32[256,256]{1,0:T(8,128)}, u32[]{:S(2)}) %copy-start.2) | copy-done | bytes 262168
  15.9 0.0 copy-start.3
  15.9 0.7 %copy-done.3 = f32[8]{0:T(128)S(1)} copy-done((f32[8]{0:T(128)S(1)}, f32[8]{0:T(128)}, u32[]{:S(2)}) %copy-start.3) | copy-done | bytes 56
  16.6 11.7 %forcing.1 = (f32[2,272,128]{2,1,0:T(8,128)S(1)}, f32[2,288,128]{2,1,0:T(8,128)S(1)}, f32[2,288,128]{2,1,0:T(8,128)S(1)}, f32[40,384]{1,0:T(8,128)S(1)}, f32[40,384]{1,0:T(8,128)S(1)}) custom-call(f32[8]{0:T(128)S(1)} %copy-done.3, f32[3,8,256,256]{3,2,1,0:T(8,128)S(1)} %copy-done, f32[26,8,256]{2,1,0:T(8,128)S(1)} %collective-permute-done.south, ...), custom_call_target="tpu_custom_call" | custom-call | tf_op jit(solution)/shard_map/forcing/pallas_call | solution.py:499
  28.3 1.5 %collective-permute-start.2 = (f32[40,384]{1,0:T(8,128)S(1)}, f32[40,384]{1,0:T(8,128)S(1)}, u32[]{:S(2)}, u32[]{:S(2)}) collective-permute-start(f32[40,384]{1,0:T(8,128)S(1)} %get-tuple-element.17.to_east), channel_id=1, source_target_pairs={{0,1},{1,2},{2,3},{3,4},{4,5},{5,6},{6,7},{7,0},{8,9},{9,10},{10,1... | collective-permute-start | bytes 184328 | tf_op jit(solution)/shard_map/ppermute | solution.py:469
  29.8 3.2 %collective-permute-start.3 = (f32[40,384]{1,0:T(8,128)S(1)}, f32[40,384]{1,0:T(8,128)S(1)}, u32[]{:S(2)}, u32[]{:S(2)}) collective-permute-start(f32[40,384]{1,0:T(8,128)S(1)} %get-tuple-element.18.to_west), channel_id=1, source_target_pairs={{0,7},{1,0},{2,1},{3,2},{4,3},{5,4},{6,5},{7,6},{8,15},{9,8},{10,9... | collective-permute-start | bytes 184328 | tf_op jit(solution)/shard_map/ppermute | solution.py:469
  33.1 2.8 %collective-permute-done.2.from_west = f32[40,384]{1,0:T(8,128)S(1)} collective-permute-done((f32[40,384]{1,0:T(8,128)S(1)}, f32[40,384]{1,0:T(8,128)S(1)}, u32[]{:S(2)}, u32[]{:S(2)}) %collective-permute-start.2) | collective-permute-done | bytes 61472 | tf_op jit(solution)/shard_map/ppermute | solution.py:469
  35.8 0.0 collective-permute-done.3.from_east
  35.8 5.2 %krylov.1 = (f32[2,256,128]{2,1,0:T(8,128)S(1)}, f32[2,256,128]{2,1,0:T(8,128)S(1)}, f32[2,256,128]{2,1,0:T(8,128)S(1)}, f32[2,256,128]{2,1,0:T(8,128)S(1)}, f32...) custom-call(f32[8]{0:T(128)S(1)} %copy-done.3, ...), custom_call_target="tpu_custom_call" | custom-call | tf_op jit(solution)/shard_map/krylov/pallas_call | solution.py:525
  41.0 13.3 %all_to_all.5.moments = f32[32,1,128]{2,1,0:T(1,128)S(1)} all-to-all(f32[32,1,128]{2,1,0:T(1,128)S(1)} %get-tuple-element.19), channel_id=1, replica_groups=mesh['by'=4,'bx'=8] {'by','bx'}, dimensions={0} | all-to-all | bytes 32768 | tf_op jit(solution)/shard_map/all_to_all | solution.py:542
  54.3 1.2 %combine.1 = (f32[256,256]{1,0:T(8,128)}, f32[256,256]{1,0:T(8,128)}) custom-call(f32[32,1,128]{2,1,0:T(1,128)S(1)} %all_to_all.5.moments, f32[2,288,128]{2,1,0:T(8,128)S(1)} %get-tuple-element.16.guess, f32[2,256,128]{2,1,0:T(8,128)S(1)} %get-tuple-element.20.base0, f32[2,256,128]{2,1,0:T(8,128)S(1)} %get-tuple-element.21.base1, ...), custom_call_target="tpu_custom_call" | custom-call | tf_op jit(solution)/shard_map/combine/pallas_call | solution.py:544
  (2 shorter events, 0.0 us)
Async XLA Ops:
  3.1 6.0 %collective-permute-start = (f32[26,8,256]{2,1,0:T(8,128)S(1)}, f32[26,8,256]{2,1,0:T(8,128)S(1)}, u32[]{:S(2)}, u32[]{:S(2)}) collective-permute-start(f32[26,8,256]{2,1,0:T(8,128)S(1)} %pad_maximum_fusion), channel_id=1, source_target_pairs={{0,8},{8,16},{16,24},{24,0},{1,9},{9,17},{17,25},{25,1},{2,10},{10... | collective-permute-start | bytes 638984 | tf_op jit(solution)/shard_map/ppermute | solution.py:469
  3.7 7.6 %collective-permute-start.1 = (f32[26,8,256]{2,1,0:T(8,128)S(1)}, f32[26,8,256]{2,1,0:T(8,128)S(1)}, u32[]{:S(2)}, u32[]{:S(2)}) collective-permute-start(f32[26,8,256]{2,1,0:T(8,128)S(1)} %pad_maximum_fusion.1), channel_id=1, source_target_pairs={{0,24},{8,0},{16,8},{24,16},{1,25},{9,1},{17,9},{25,17},{2,26},{10... | collective-permute-start | bytes 638984 | tf_op jit(solution)/shard_map/ppermute | solution.py:469
  11.3 2.8 %copy-start = (f32[3,8,256,256]{3,2,1,0:T(8,128)S(1)}, f32[3,8,256,256]{3,2,1,0:T(8,128)}, u32[]{:S(2)}) copy-start(f32[3,8,256,256]{3,2,1,0:T(8,128)} %fields.1) | copy-start | bytes 18874372
  14.0 0.9 %copy-start.1 = (f32[256,256]{1,0:T(8,128)S(1)}, f32[256,256]{1,0:T(8,128)}, u32[]{:S(2)}) copy-start(f32[256,256]{1,0:T(8,128)} %old.1) | copy-start | bytes 786436
  15.0 0.9 %copy-start.2 = (s32[256,256]{1,0:T(8,128)S(1)}, s32[256,256]{1,0:T(8,128)}, u32[]{:S(2)}) copy-start(s32[256,256]{1,0:T(8,128)} %count.1) | copy-start | bytes 786436
  15.9 0.7 %copy-start.3 = (f32[8]{0:T(128)S(1)}, f32[8]{0:T(128)}, u32[]{:S(2)}) copy-start(f32[8]{0:T(128)} %thick.3) | copy-start | bytes 100
  28.3 7.5 %collective-permute-start.2 = (f32[40,384]{1,0:T(8,128)S(1)}, f32[40,384]{1,0:T(8,128)S(1)}, u32[]{:S(2)}, u32[]{:S(2)}) collective-permute-start(f32[40,384]{1,0:T(8,128)S(1)} %get-tuple-element.17.to_east), channel_id=1, source_target_pairs={{0,1},{1,2},{2,3},{3,4},{4,5},{5,6},{6,7},{7,0},{8,9},{9,10},{10,1... | collective-permute-start | bytes 184328 | tf_op jit(solution)/shard_map/ppermute | solution.py:469
  29.8 6.0 %collective-permute-start.3 = (f32[40,384]{1,0:T(8,128)S(1)}, f32[40,384]{1,0:T(8,128)S(1)}, u32[]{:S(2)}, u32[]{:S(2)}) collective-permute-start(f32[40,384]{1,0:T(8,128)S(1)} %get-tuple-element.18.to_west), channel_id=1, source_target_pairs={{0,7},{1,0},{2,1},{3,2},{4,3},{5,4},{6,5},{7,6},{8,15},{9,8},{10,9... | collective-permute-start | bytes 184328 | tf_op jit(solution)/shard_map/ppermute | solution.py:469

commit v5 on v4

--- a/solution.py
+++ b/solution.py
@@ -18,8 +18,9 @@
 
 STEP = 8
 GRANT = 16 * 2**20
-MIX_UNROLL = 17
-SPREAD_UNROLL = 11
+INNER_GRANT = 52 * 2**20
+MIX_UNROLL = 16
+SPREAD_UNROLL = 10
 WIDE = 17
 WIDE_INNER = 16
 
@@ -56,171 +57,249 @@
     return east, west
 
 
-def forcing_kernel(
-    thick, fields, south, north, count, old, part, depth, guess, to_east, to_west,
-    block, mixed, wet, pack, edges, arrivals,
+def mix_strip(zonal, merid, mixed, row, lane):
+    tiles = zonal.shape[0]
+    near = lambda by=0: pl.ds(row + by, STEP)
+    east, west = neighbours([zonal[t, near(), :] for t in range(tiles)] + [None], lane)
+    for t in range(tiles + 1):
+        value = east[t] - west[t]
+        if t < tiles:
+            value += merid[t, near(1), :] - merid[t, near(-1), :]
+        mixed[t, near(), :] = value
+
+
+def spread_strip(baro, mixed, row, lane):
+    tiles = baro.shape[0]
+    both = range(tiles + 1)
+    near = lambda by=0: pl.ds(row + by, STEP)
+    far, once, still = [], [], []
+    for t in both:
+        own = mixed[t, near(), :]
+        beside = mixed[t, near(1), :] + mixed[t, near(-1), :]
+        beyond = mixed[t, near(2), :] + mixed[t, near(-2), :]
+        once.append(2.0 * beside - 8.0 * own)
+        still.append(beyond - 8.0 * beside + 20.0 * own)
+        if t < tiles:
+            pressure = 10.0 * baro[t, near(), :]
+            around = baro[t, near(2), :] + baro[t, near(-2), :]
+            own = own + pressure
+            still[t] += 10.0 * around - 4.0 * pressure
+        far.append(own)
+    last, first = lane == LANES - 1, lane == 0
+    ring = tiles + 1
+    back = [turn(v, -1) for v in far]
+    forth = [turn(v, 1) for v in far]
+    easts = [once[t] + jnp.where(last, back[(t + 1) % ring], back[t]) for t in both]
+    wests = [once[t] + jnp.where(first, forth[t - 1], forth[t]) for t in both]
+    back = [turn(v, -1) for v in easts]
+    forth = [turn(v, 1) for v in wests]
+    return [
+        still[t]
+        + (
+            jnp.where(last, back[(t + 1) % ring], back[t])
+            + jnp.where(first, forth[t - 1], forth[t])
+        )
+        for t in both
+    ]
+
+
+def sweep(body, strips, unroll, carry=0, first=0, stride=1):
+    step = lambda i, c: body(first + stride * i, c)
+    return lax.fori_loop(0, strips, step, carry, unroll=unroll)
+
+
+def lane_tiles(tiles):
+    return [pl.ds(t * LANES, LANES) for t in range(tiles)]
+
+
+def inner_kernel(thick, fields, count_hbm, part, pack, block, mixed, count, arrivals, others):
+    level = pl.program_id(0)
+    levels = fields.shape[1]
+    tiles, height, _ = count.shape
+    lane = lane_index()
+    cols = lane_tiles(tiles)
+
+    def arrival(at, t):
+        return pltpu.make_async_copy(
+            fields.at[:, at, :, cols[t]], block.at[at, :, t, pl.ds(PAD, height), :], arrivals.at[at, t]
+        )
+
+    counted = [
+        pltpu.make_async_copy(count_hbm.at[:, cols[t]], count.at[t], others.at[t])
+        for t in range(tiles)
+    ]
+
+    @pl.when(level == 0)
+    def _():
+        for t in range(tiles):
+            arrival(0, t).start()
+        for copy in counted:
+            copy.start()
+        for at in range(1, levels):
+            for t in range(tiles):
+                arrival(at, t).start()
+        part[...] = jnp.zeros_like(part)
+        pack[...] = jnp.zeros_like(pack)
+        for copy in counted:
+            copy.wait()
+
+    for t in range(tiles):
+        arrival(level, t).wait()
+    zonal, merid, baro = (block.at[level, f] for f in range(3))
+    thickness = thick[level]
+
+    def mix(i, c):
+        mix_strip(zonal, merid, mixed, PAD + i * STEP, lane)
+        return c
+
+    def spread(i, c):
+        row = ROWS - DEEP + i * STEP
+        total = spread_strip(baro, mixed, PAD + row, lane)
+        rows = pl.ds(ROWS + row, STEP)
+        for t in range(tiles):
+            weight = jnp.where(count[t, pl.ds(row, STEP), :] > level, thickness, 0.0)
+            part[t, rows, :] += weight * total[t]
+        pack[rows, :] += pltpu.roll(total[tiles], 8 * level + REACH, 1)
+        return c
+
+    sweep(mix, height // STEP, MIX_UNROLL)
+    strips = height // STEP - 1
+    main = strips // SPREAD_UNROLL * SPREAD_UNROLL
+    sweep(spread, main, SPREAD_UNROLL)
+    for i in range(main, strips):
+        spread(i, 0)
+
+
+def edge_kernel(
+    thick, fields, south, north, count_hbm, old_hbm, part_in, pack_in,
+    part, depth, guess, to_east, to_west,
+    pack, block, mixed, wet, edges, count, old, arrivals, others,
 ):
-    level = pl.program_id(0)
-    levels = pl.num_programs(0)
-    static_levels = fields.shape[1]
+    levels = fields.shape[1]
     height, width = count.shape
     tiles = width // LANES
     ext = height + 2 * ROWS
-    base = PAD + ROWS
-    forcing_at = message_rows(static_levels)[0]
+    forcing_at = message_rows(levels)[0]
     lane = lane_index()
-    cols = [pl.ds(t * LANES, LANES) for t in range(tiles)]
-    both = range(tiles + 1)
-
-    def arrival(at, t):
-        return pltpu.make_async_copy(
-            fields.at[:, at, :, cols[t]],
-            block.at[at, :, t, pl.ds(base, height), :],
-            arrivals.at[at, t],
-        )
-
-    @pl.when(level == 0)
-    def _():
-        for at in range(static_levels):
+    cols = lane_tiles(tiles)
+
+    copies = [
+        pltpu.make_async_copy(count_hbm, count, others.at[0]),
+        pltpu.make_async_copy(old_hbm, old, others.at[1]),
+    ]
+    for f in range(3):
+        for t, c in enumerate(cols):
+            for side, (here, there, halo, row) in enumerate(
+                ((ROWS, 0, south, 0), (0, 2 * ROWS, north, height - 2 * ROWS))
+            ):
+                at = 4 * (f * tiles + t) + 2 * side
+                group = block.at[side, f, :, t]
+                copies += [
+                    pltpu.make_async_copy(
+                        fields.at[f, :, pl.ds(row, 2 * ROWS), c],
+                        group.at[:, pl.ds(here, 2 * ROWS), :],
+                        arrivals.at[at],
+                    ),
+                    pltpu.make_async_copy(
+                        halo.at[pl.ds(f * levels, levels), :, c],
+                        group.at[:, pl.ds(there, ROWS), :],
+                        arrivals.at[at + 1],
+                    ),
+                ]
+    for copy in copies:
+        copy.start()
+    low, high = slice(0, ROWS - DEEP), slice(ext - (ROWS - DEEP), ext)
+    for buf in (depth, guess):
+        for at in (0, PAD + ext):
+            buf[:, at : at + PAD, :] = jnp.zeros((tiles, PAD, LANES), jnp.float32)
+    inner = slice(2 * ROWS - DEEP, ext - (2 * ROWS - DEEP))
+    part[:, inner, :] = part_in[:, inner, :]
+    pack[inner, :] = pack_in[inner, :]
+    for outer in (low, high, slice(ext, pack.shape[0])):
+        if outer.start < ext:
+            part[:, outer, :] = jnp.zeros((tiles, ROWS - DEEP, LANES), jnp.float32)
+        pack[outer, :] = jnp.zeros((outer.stop - outer.start, LANES), jnp.float32)
+    edges[ext:, :] = jnp.zeros((edges.shape[0] - ext, LANES), jnp.float32)
+    for copy in copies:
+        copy.wait()
+    for t, c in enumerate(cols):
+        wet[t, :ROWS, :] = south[3 * levels, :, c]
+        wet[t, ROWS : ROWS + height, :] = count[:, c].astype(jnp.float32)
+        wet[t, ROWS + height :, :] = north[3 * levels, :, c]
+
+    plans = ((ROWS - DEEP, (2, 10)), (2 * ROWS - DEEP, (10, 14)))
+    starts = (ROWS - DEEP, ext - (2 * ROWS - DEEP))
+
+    def mix(k, c):
+        for side, (_, rows) in enumerate(plans):
+            for row in rows:
+                mix_strip(block.at[side, 0, k], block.at[side, 1, k], mixed.at[side, k], row, lane)
+        return c
+
+    def spread(k, carry):
+        found = []
+        number, thickness = k.astype(jnp.float32), thick[k]
+        for side, (row, _) in enumerate(plans):
+            total = spread_strip(block.at[side, 2, k], mixed.at[side, k], row, lane)
+            e = starts[side]
             for t in range(tiles):
-                arrival(at, t).start()
-
-    def extended(e, lower, middle, upper):
-        if e < ROWS:
-            return lower
-        if e >= ROWS + height:
-            return upper
-        return middle(e - ROWS)
-
-    def sweep(body, strips, unroll):
-        lax.fori_loop(0, strips, lambda i, c: (body(i), c)[1], 0, unroll=unroll)
-
-    @pl.when(level == 0)
-    def _():
-        for buf in (mixed, depth, guess):
-            for at in (0, PAD + ext):
-                buf[:, at : at + PAD, :] = jnp.zeros((buf.shape[0], PAD, LANES), jnp.float32)
-        part[...] = jnp.zeros_like(part)
-        pack[...] = jnp.zeros_like(pack)
-        edges[...] = jnp.zeros_like(edges)
+                weight = jnp.where(wet[t, e : e + STEP, :] > number, thickness, 0.0)
+                found.append(weight * total[t])
+            found.append(pltpu.roll(total[tiles], 8 * k + REACH, 1))
+        return tuple(a + b for a, b in zip(carry, found))
+
+    sweep(mix, levels, 4)
+    zero = jnp.zeros((STEP, LANES), jnp.float32)
+    found = sweep(spread, levels, 4, (zero,) * (2 * (tiles + 1)))
+    for side, e in enumerate(starts):
+        for t in range(tiles):
+            part[t, e : e + STEP, :] = found[side * (tiles + 1) + t]
+        pack[e : e + STEP, :] = found[side * (tiles + 1) + tiles]
+
+    scale = -0.5 * VISCOSITY
+    for e in range(0, ext, STEP):
+        r = e + PAD
+        begin = []
         for t, c in enumerate(cols):
-            wet[t, :ROWS, :] = south[3 * static_levels, :, c]
-            wet[t, ROWS : ROWS + height, :] = count[:, c].astype(jnp.float32)
-            wet[t, ROWS + height :, :] = north[3 * static_levels, :, c]
-
-    zonal, merid, baro = (block.at[level, f] for f in range(3))
-    for f, buf in enumerate((zonal, merid, baro)):
-        for t, c in enumerate(cols):
-            buf[t, :PAD, :] = jnp.zeros((PAD, LANES), jnp.float32)
-            buf[t, PAD:base, :] = south[f * static_levels + level, :, c]
-            buf[t, base + height : PAD + ext, :] = north[f * static_levels + level, :, c]
-            buf[t, PAD + ext :, :] = jnp.zeros((PAD, LANES), jnp.float32)
-    for t in range(tiles):
-        arrival(level, t).wait()
-
-    def near(i, by=0):
-        return pl.ds(PAD + i * STEP + by, STEP)
-
-    def mix(i):
-        east, west = neighbours([zonal[t, near(i), :] for t in range(tiles)] + [None], lane)
-        for t in both:
-            value = east[t] - west[t]
-            if t < tiles:
-                value += merid[t, near(i, 1), :] - merid[t, near(i, -1), :]
-            mixed[t, near(i), :] = value
-
-    sweep(mix, ext // STEP, MIX_UNROLL)
-    thickness = thick[level]
-    level_number = level.astype(jnp.float32)
-
-    def spread(i):
-        rows = pl.ds(ROWS - DEEP + i * STEP, STEP)
-        near = lambda i, by=0: pl.ds(PAD + ROWS - DEEP + i * STEP + by, STEP)
-        far, once, still = [], [], []
-        for t in both:
-            own = mixed[t, near(i), :]
-            beside = mixed[t, near(i, 1), :] + mixed[t, near(i, -1), :]
-            beyond = mixed[t, near(i, 2), :] + mixed[t, near(i, -2), :]
-            once.append(2.0 * beside - 8.0 * own)
-            still.append(beyond - 8.0 * beside + 20.0 * own)
-            if t < tiles:
-                pressure = 10.0 * baro[t, near(i), :]
-                around = baro[t, near(i, 2), :] + baro[t, near(i, -2), :]
-                own = own + pressure
-                still[t] += 10.0 * around - 4.0 * pressure
-            far.append(own)
-        count_of = len(far)
-        back = [turn(v, -1) for v in far]
-        forth = [turn(v, 1) for v in far]
-        last, first = lane == LANES - 1, lane == 0
-        easts = [
-            once[t] + jnp.where(last, back[(t + 1) % count_of], back[t]) for t in both
-        ]
-        wests = [once[t] + jnp.where(first, forth[t - 1], forth[t]) for t in both]
-        back = [turn(v, -1) for v in easts]
-        forth = [turn(v, 1) for v in wests]
-        for t in both:
-            total = still[t] + (
-                jnp.where(last, back[(t + 1) % count_of], back[t])
-                + jnp.where(first, forth[t - 1], forth[t])
+            if e < ROWS:
+                pressure = south[3 * levels + 1, :, c]
+            elif e >= ROWS + height:
+                pressure = north[3 * levels + 1, :, c]
+            else:
+                pressure = old[e - ROWS : e - ROWS + STEP, c]
+            counts = wet[t, e : e + STEP, :]
+            depth[t, r : r + STEP, :] = sum(
+                jnp.where(counts > float(k), thick[k], 0.0) for k in range(levels)
             )
-            if t < tiles:
-                weight = jnp.where(wet[t, rows, :] > level_number, thickness, 0.0)
-                part[t, rows, :] += weight * total
-            else:
-                pack[rows, :] += pltpu.roll(total, 8 * level + REACH, 1)
-
-    sweep(spread, (height + 2 * DEEP) // STEP, SPREAD_UNROLL)
-
-    @pl.when(level == levels - 1)
-    def _():
-        scale = -0.5 * VISCOSITY
-        for e in range(0, ext, STEP):
-            r = e + PAD
-            begin = []
-            for t, c in enumerate(cols):
-                pressure = extended(
-                    e,
-                    south[3 * static_levels + 1, :, c],
-                    lambda o: old[o : o + STEP, c],
-                    north[3 * static_levels + 1, :, c],
-                )
-                counts = wet[t, e : e + STEP, :]
-                deep = sum(
-                    jnp.where(counts > float(k), thick[k], 0.0) for k in range(static_levels)
-                )
-                depth[t, r : r + STEP, :] = deep
-                begin.append(jnp.where(counts > 0.0, pressure, 0.0))
-                guess[t, r : r + STEP, :] = begin[t]
-                part[t, e : e + STEP, :] *= scale
-            tile = None
-            for t, inner, start in ((tiles - 1, True, 0), (0, False, LANES // 2)):
-                at = start
-                for piece, size in (
-                    (part[t, e : e + STEP, :], DEEP),
-                    (wet[t, e : e + STEP, :], EDGE),
-                    (begin[t], EDGE),
-                ):
-                    moved = turn(piece, at + size if inner else at)
-                    inside = (lane >= at) & (lane < at + size)
-                    tile = jnp.where(inside, moved, 0.0 if tile is None else tile)
-                    at += size
-            edges[e : e + STEP, :] = tile
-        size = DEEP + 2 * EDGE
-        for message in (to_east, to_west):
-            message[...] = jnp.zeros_like(message)
-        for at in range(0, to_east.shape[1], LANES):
-            span = slice(at, at + LANES)
-            turned = scale * jnp.transpose(pack[span, :])
-            for k in range(static_levels):
-                mine = slice(REACH * k, REACH * k + REACH)
-                to_west[mine, span] = turned[8 * k : 8 * k + REACH, :]
-                to_east[mine, span] = turned[8 * k + REACH : 8 * k + 2 * REACH, :]
-            turned = jnp.transpose(edges[span, :])
-            to_east[forcing_at : forcing_at + size, span] = turned[:size, :]
-            to_west[forcing_at : forcing_at + size, span] = turned[
-                LANES // 2 : LANES // 2 + size, :
-            ]
+            begin.append(jnp.where(counts > 0.0, pressure, 0.0))
+            guess[t, r : r + STEP, :] = begin[t]
+            part[t, e : e + STEP, :] *= scale
+        tile = None
+        for t, inside, start in ((tiles - 1, True, 0), (0, False, LANES // 2)):
+            at = start
+            for piece, size in (
+                (part[t, e : e + STEP, :], DEEP),
+                (wet[t, e : e + STEP, :], EDGE),
+                (begin[t], EDGE),
+            ):
+                moved = turn(piece, at + size if inside else at)
+                mask = (lane >= at) & (lane < at + size)
+                tile = jnp.where(mask, moved, 0.0 if tile is None else tile)
+                at += size
+        edges[e : e + STEP, :] = tile
+    size = DEEP + 2 * EDGE
+    for message in (to_east, to_west):
+        message[...] = jnp.zeros_like(message)
+    for at in range(0, to_east.shape[1], LANES):
+        span = slice(at, at + LANES)
+        turned = scale * jnp.transpose(pack[span, :])
+        for k in range(levels):
+            mine = slice(REACH * k, REACH * k + REACH)
+            to_west[mine, span] = turned[8 * k : 8 * k + REACH, :]
+            to_east[mine, span] = turned[8 * k + REACH : 8 * k + 2 * REACH, :]
+        turned = jnp.transpose(edges[span, :])
+        to_east[forcing_at : forcing_at + size, span] = turned[:size, :]
+        to_west[forcing_at : forcing_at + size, span] = turned[LANES // 2 : LANES // 2 + size, :]
 
 
 def solve_kernel(
@@ -277,10 +356,6 @@
             halo_guess[r : r + STEP, :] = jnp.where(near, turn(tile, -60), 0.0)
             halo_part[e : e + STEP, :] = jnp.where(close, tile, 0.0)
             fix[e : e + STEP, :] = turn(tile, -80)
-
-    def sweep(body, strips, unroll, first=0, stride=1, carry=0):
-        step = lambda i, c: body(first + stride * i, c)
-        return lax.fori_loop(0, strips, step, carry, unroll=unroll)
 
     def span(i, by=0):
         return pl.ds(PAD + i * STEP + by, STEP)
@@ -360,8 +435,8 @@
 
         return body
 
-    sweep(begin(True), inner, WIDE_INNER, above)
-    sweep(begin(False), 2, 2, 0, above + inner)
+    sweep(begin(True), inner, WIDE_INNER, 0, above)
+    sweep(begin(False), 2, 2, 0, 0, above + inner)
 
     zero = jnp.zeros((STEP, LANES), jnp.float32)
 
@@ -393,9 +468,9 @@
 
             return body
 
-        sums += sweep(apply(True), inner, WIDE_INNER, above, 1, (zero, zero))
+        sums += sweep(apply(True), inner, WIDE_INNER, (zero, zero), above)
         if not final:
-            sweep(apply(False), 2, 2, 0, above + inner, (zero, zero))
+            sweep(apply(False), 2, 2, (zero, zero), 0, above + inner)
     lane_row = lax.broadcasted_iota(jnp.int32, (1, LANES), 1)
     found = jnp.zeros((1, LANES), jnp.float32)
     for m in range(2 * ITERS):
@@ -489,34 +564,52 @@
     smem = pl.BlockSpec(memory_space=pltpu.SMEM)
     vmem = pl.BlockSpec(memory_space=pltpu.VMEM)
     whole = lambda *dims: pl.BlockSpec(dims, lambda k: (0,) * len(dims))
-    hbm = pl.BlockSpec(memory_space=pl.ANY)
-    halo = whole(3 * levels + 2, ROWS, width)
+    hbm = pl.BlockSpec(memory_space=pltpu.HBM)
     shaped = lambda *dims: jax.ShapeDtypeStruct(dims, f32)
     scratch = lambda *dims: pltpu.VMEM(dims, f32)
     main = (tiles, ext, LANES)
     loose = (tiles, padded, LANES)
+    params = lambda size: pltpu.CompilerParams(vmem_limit_bytes=size)
+    partial, packed = pl.pallas_call(
+        inner_kernel,
+        grid=(levels,),
+        in_specs=[smem, hbm, hbm],
+        out_specs=[whole(*main), whole(ext, LANES)],
+        out_shape=[shaped(*main), shaped(ext, LANES)],
+        scratch_shapes=[
+            scratch(levels, 3, tiles, height + 2 * PAD, LANES),
+            scratch(tiles + 1, height + 2 * PAD, LANES),
+            pltpu.VMEM((tiles, height, LANES), level_count.dtype),
+            pltpu.SemaphoreType.DMA((levels, tiles)),
+            pltpu.SemaphoreType.DMA((tiles,)),
+        ],
+        compiler_params=params(INNER_GRANT),
+        cost_estimate=pl.CostEstimate(
+            flops=40 * fields.size // 3, bytes_accessed=4 * fields.size, transcendentals=0
+        ),
+        name="inner_forcing",
+    )(thickness, fields, level_count)
+
     results = (main, loose, loose, (message, tall), (message, tall))
     part, depth, guess, to_east, to_west = pl.pallas_call(
-        forcing_kernel,
-        grid=(levels,),
-        in_specs=[
-            smem,
-            hbm, halo, halo,
-            whole(height, width), whole(height, width),
-        ],
-        out_specs=[whole(*dims) for dims in results],
+        edge_kernel,
+        in_specs=[smem, hbm, vmem, vmem, hbm, hbm, vmem, vmem],
+        out_specs=[vmem] * 5,
         out_shape=[shaped(*dims) for dims in results],
         scratch_shapes=[
-            scratch(levels, 3, *loose),
-            scratch(tiles + 1, padded, LANES),
+            scratch(tall, LANES),
+            scratch(2, 3, levels, tiles, 3 * ROWS, LANES),
+            scratch(2, levels, tiles + 1, 3 * ROWS, LANES),
             scratch(*main),
             scratch(tall, LANES),
-            scratch(tall, LANES),
-            pltpu.SemaphoreType.DMA((levels, tiles)),
+            pltpu.VMEM((height, width), level_count.dtype),
+            scratch(height, width),
+            pltpu.SemaphoreType.DMA((12 * tiles,)),
+            pltpu.SemaphoreType.DMA((2,)),
         ],
-        compiler_params=pltpu.CompilerParams(vmem_limit_bytes=GRANT),
-        name="forcing",
-    )(thickness, fields, south, north, level_count, old_pressure)
+        compiler_params=params(GRANT),
+        name="edge_forcing",
+    )(thickness, fields, south, north, level_count, old_pressure, partial, packed)
 
     from_west = shift(to_east, "bx", 1)
     from_east = shift(to_west, "bx", -1)

time: 55.9 us -> 49.8 us (0.89)
  waiting for transfers between devices: 8.3 us -> 2.44 us
  local copies, waits for them, and re-layouts: 7.1 us -> 3.66 us
  Pallas kernels: 18 us -> 20.9 us
  starting transfers between devices: 7.33 us -> 7.97 us
    ppermute x4, waiting for transfers between devices: 8.3 us -> 2.44 us  [shift(): lax.ppermute(value, axis, [(i, (i + by) % size) for i in range(size)])]
    unnamed x8, local copies, waits for them, and re-layouts: 5.34 us -> 1.61 us
    pallas_call x1 -> x2, Pallas kernels: 11.7 us -> 14.5 us  [the longest x1 12.2 us: shards(): pl.pallas_call(inner_kernel, grid=(levels,), in_specs=[smem, hbm, hbm], o...]
    ppermute x4, starting transfers between devices: 7.33 us -> 7.97 us  [shift(): lax.ppermute(value, axis, [(i, (i + by) % size) for i in range(size)])]
  transfers between devices with their start and end apart: 4 -> 4, of which waited for: 3 -> 2; matrix products, arithmetic and copies ran while one was open for 0% -> 0% of each run, Pallas kernels for 0% -> 25%
where the time goes in v5:
time: 49.8 us; the launch traced here: 49.5 us
  Pallas kernels  20.9 us (42%)
  blocking collectives  12.9 us (26%)
  starting transfers between devices  7.97 us (16%)
  local copies, waits for them, and re-layouts  3.66 us (7%)
  waiting for transfers between devices  2.44 us (5%)
  other arithmetic  0.9 us (2%)
  between operations  0.71 us (1%)
    all_to_all x1, blocking collectives, shards(): lax.all_to_all(moments, ('by', 'bx'), split_axis=0, concat_axis=0, tiled=...  12.9 us
    pallas_call x1, Pallas kernels, shards(): pl.pallas_call(inner_kernel, grid=(levels,), in_specs=[smem, hbm, hbm], o...  12.2 us
    ppermute x4, starting transfers between devices, shift(): lax.ppermute(value, axis, [(i, (i + by) % size) for i in range(size)])  7.97 us
    pallas_call x1, Pallas kernels, shards(): pl.pallas_call(solve_kernel, in_specs=[smem] + [vmem] * 7, out_specs=[vme...  5.18 us
    ppermute x4, waiting for transfers between devices, shift(): lax.ppermute(value, axis, [(i, (i + by) % size) for i in range(size)])  2.44 us
    pallas_call x1, Pallas kernels, shards(): pl.pallas_call(edge_kernel, in_specs=[smem, hbm, vmem, vmem, hbm, hbm, vm...  2.26 us
    unnamed x8, local copies, waits for them, and re-layouts  1.61 us
    pallas_call x1, Pallas kernels, shards(): pl.pallas_call(combine_kernel, in_specs=[vmem] * (ITERS + 4), out_specs=[...  1.21 us
  transfers between devices with their start and end apart: 4, of which 2 were waited for; matrix products, arithmetic and copies ran while one was open for 0% of the time, Pallas kernels for 25%

profile of v5, /device:TPU:0, one launch (start us, length us, event | category | flops | bytes accessed | tf_op | source)
XLA Modules:
  0.0 49.5 jit_solution(15328174283545913447)
XLA Ops:
  0.6 0.0 copy-start
  0.6 0.9 %slice_bitcast_fusion = (f32[1,8,256]{2,1,0:T(8,128)S(1)}, f32[1,8,256]{2,1,0:T(8,128)S(1)}) fusion(f32[256,256]{1,0:T(8,128)} %old_hbm.1), kind=kLoop, calls=%fused_computation.2 | loop fusion | bytes 32768 | tf_op jit(solution)/shard_map/broadcast_in_dim | solution.py:556
  1.5 0.9 %convert_bitcast_fusion = (f32[1,8,256]{2,1,0:T(8,128)S(1)}, f32[1,8,256]{2,1,0:T(8,128)S(1)}) fusion(s32[256,256]{1,0:T(8,128)} %count_hbm.3), kind=kLoop, calls=%fused_computation.3 | loop fusion | flops 4096 | bytes 32768 | tf_op jit(solution)/shard_map/broadcast_in_dim | solution.py:556
  2.4 1.2 %fusion = (f32[3,8,8,256]{3,2,1,0:T(8,128)S(1)}, f32[3,8,8,256]{3,2,1,0:T(8,128)S(1)}) fusion(f32[3,8,256,256]{3,2,1,0:T(8,128)} %fields.3), kind=kLoop, calls=%fused_computation.6 | loop fusion | bytes 786432 | tf_op jit(solution)/shard_map/slice | solution.py:553
  3.6 0.5 %collective-permute-start = (f32[26,8,256]{2,1,0:T(8,128)S(1)}, f32[26,8,256]{2,1,0:T(8,128)S(1)}, u32[]{:S(2)}, u32[]{:S(2)}) collective-permute-start(f32[26,8,256]{2,1,0:T(8,128)S(1)} %pad_maximum_fusion), channel_id=1, source_target_pairs={{0,8},{8,16},{16,24},{24,0},{1,9},{9,17},{17,25},{25,1},{2,10},{10... | collective-permute-start | bytes 638984 | tf_op jit(solution)/shard_map/ppermute | solution.py:544
  4.1 2.0 %collective-permute-start.1 = (f32[26,8,256]{2,1,0:T(8,128)S(1)}, f32[26,8,256]{2,1,0:T(8,128)S(1)}, u32[]{:S(2)}, u32[]{:S(2)}) collective-permute-start(f32[26,8,256]{2,1,0:T(8,128)S(1)} %pad_maximum_fusion.1), channel_id=1, source_target_pairs={{0,24},{8,0},{16,8},{24,16},{1,25},{9,1},{17,9},{25,17},{2,26},{10... | collective-permute-start | bytes 638984 | tf_op jit(solution)/shard_map/ppermute | solution.py:544
  6.2 0.0 copy-start.1
  6.2 0.9 %copy-done.1 = s32[256,256]{1,0:T(8,128)S(1)} copy-done((s32[256,256]{1,0:T(8,128)S(1)}, s32[256,256]{1,0:T(8,128)}, u32[]{:S(2)}) %copy-start.1) | copy-done | bytes 262168
  7.1 0.0 copy-start.3
  7.1 0.7 %copy-done.3 = f32[8]{0:T(128)S(1)} copy-done((f32[8]{0:T(128)S(1)}, f32[8]{0:T(128)}, u32[]{:S(2)}) %copy-start.3) | copy-done | bytes 56
  7.8 0.0 copy-start.2
  7.8 12.2 %inner_forcing.1 = (f32[2,272,128]{2,1,0:T(8,128)S(1)}, f32[272,128]{1,0:T(8,128)S(1)}) custom-call(f32[8]{0:T(128)S(1)} %copy-done.3, f32[3,8,256,256]{3,2,1,0:T(8,128)} %fields.3, s32[256,256]{1,0:T(8,128)S(1)} %copy-done.1), custom_call_target="tpu_custom_call" | custom-call | flops 20971520 | bytes 6291456 | tf_op jit(solution)/shard_map/inner_forcing/pallas_call | solution.py:573
  20.0 0.0 collective-permute-done.south
  20.0 0.0 collective-permute-done.1.north
  20.0 0.0 copy-done
  20.0 0.0 copy-done.2
  20.1 2.3 %edge_forcing.1 = (f32[2,272,128]{2,1,0:T(8,128)S(1)}, f32[2,288,128]{2,1,0:T(8,128)S(1)}, f32[2,288,128]{2,1,0:T(8,128)S(1)}, f32[40,384]{1,0:T(8,128)S(1)}, f32[40,384]{1,0:T(8,128)S(1)}) custom-call(f32[8]{0:T(128)S(1)} %copy-done.3, f32[3,8,256,256]{3,2,1,0:T(8,128)S(1)} %copy-done, f32[26,8,256]{2,1,0:T(8,128)S(1)} %collective-permute-done.south, ...), custom_call_target="tpu_custom_call" | custom-call | tf_op jit(solution)/shard_map/edge_forcing/pallas_call | solution.py:594
  22.3 2.3 %collective-permute-start.2 = (f32[40,384]{1,0:T(8,128)S(1)}, f32[40,384]{1,0:T(8,128)S(1)}, u32[]{:S(2)}, u32[]{:S(2)}) collective-permute-start(f32[40,384]{1,0:T(8,128)S(1)} %get-tuple-element.21.to_east), channel_id=1, source_target_pairs={{0,1},{1,2},{2,3},{3,4},{4,5},{5,6},{6,7},{7,0},{8,9},{9,10},{10,1... | collective-permute-start | bytes 184328 | tf_op jit(solution)/shard_map/ppermute | solution.py:544
  24.6 3.1 %collective-permute-start.3 = (f32[40,384]{1,0:T(8,128)S(1)}, f32[40,384]{1,0:T(8,128)S(1)}, u32[]{:S(2)}, u32[]{:S(2)}) collective-permute-start(f32[40,384]{1,0:T(8,128)S(1)} %get-tuple-element.22.to_west), channel_id=1, source_target_pairs={{0,7},{1,0},{2,1},{3,2},{4,3},{5,4},{6,5},{7,6},{8,15},{9,8},{10,9... | collective-permute-start | bytes 184328 | tf_op jit(solution)/shard_map/ppermute | solution.py:544
  27.7 2.1 %collective-permute-done.2.from_west = f32[40,384]{1,0:T(8,128)S(1)} collective-permute-done((f32[40,384]{1,0:T(8,128)S(1)}, f32[40,384]{1,0:T(8,128)S(1)}, u32[]{:S(2)}, u32[]{:S(2)}) %collective-permute-start.2) | collective-permute-done | bytes 61472 | tf_op jit(solution)/shard_map/ppermute | solution.py:544
  29.9 0.3 collective-permute-done.3.from_east
  30.2 5.2 %krylov.1 = (f32[2,256,128]{2,1,0:T(8,128)S(1)}, f32[2,256,128]{2,1,0:T(8,128)S(1)}, f32[2,256,128]{2,1,0:T(8,128)S(1)}, f32[2,256,128]{2,1,0:T(8,128)S(1)}, f32...) custom-call(f32[8]{0:T(128)S(1)} %copy-done.3, ...), custom_call_target="tpu_custom_call" | custom-call | tf_op jit(solution)/shard_map/krylov/pallas_call | solution.py:618
  35.4 12.9 %all_to_all.5.moments = f32[32,1,128]{2,1,0:T(1,128)S(1)} all-to-all(f32[32,1,128]{2,1,0:T(1,128)S(1)} %get-tuple-element.23), channel_id=1, replica_groups=mesh['by'=4,'bx'=8] {'by','bx'}, dimensions={0} | all-to-all | bytes 32768 | tf_op jit(solution)/shard_map/all_to_all | solution.py:635
  48.3 1.2 %combine.1 = (f32[256,256]{1,0:T(8,128)}, f32[256,256]{1,0:T(8,128)}) custom-call(f32[32,1,128]{2,1,0:T(1,128)S(1)} %all_to_all.5.moments, f32[2,288,128]{2,1,0:T(8,128)S(1)} %get-tuple-element.20.guess, f32[2,256,128]{2,1,0:T(8,128)S(1)} %get-tuple-element.24.base0, f32[2,256,128]{2,1,0:T(8,128)S(1)} %get-tuple-element.25.base1, ...), custom_call_target="tpu_custom_call" | custom-call | tf_op jit(solution)/shard_map/combine/pallas_call | solution.py:637
  (2 shorter events, 0.0 us)
Async XLA Ops:
  0.6 19.4 %copy-start = (f32[3,8,256,256]{3,2,1,0:T(8,128)S(1)}, f32[3,8,256,256]{3,2,1,0:T(8,128)}, u32[]{:S(2)}) copy-start(f32[3,8,256,256]{3,2,1,0:T(8,128)} %fields.3) | copy-start | bytes 18874372
  3.6 16.4 %collective-permute-start = (f32[26,8,256]{2,1,0:T(8,128)S(1)}, f32[26,8,256]{2,1,0:T(8,128)S(1)}, u32[]{:S(2)}, u32[]{:S(2)}) collective-permute-start(f32[26,8,256]{2,1,0:T(8,128)S(1)} %pad_maximum_fusion), channel_id=1, source_target_pairs={{0,8},{8,16},{16,24},{24,0},{1,9},{9,17},{17,25},{25,1},{2,10},{10... | collective-permute-start | bytes 638984 | tf_op jit(solution)/shard_map/ppermute | solution.py:544
  4.1 15.9 %collective-permute-start.1 = (f32[26,8,256]{2,1,0:T(8,128)S(1)}, f32[26,8,256]{2,1,0:T(8,128)S(1)}, u32[]{:S(2)}, u32[]{:S(2)}) collective-permute-start(f32[26,8,256]{2,1,0:T(8,128)S(1)} %pad_maximum_fusion.1), channel_id=1, source_target_pairs={{0,24},{8,0},{16,8},{24,16},{1,25},{9,1},{17,9},{25,17},{2,26},{10... | collective-permute-start | bytes 638984 | tf_op jit(solution)/shard_map/ppermute | solution.py:544
  6.2 0.9 %copy-start.1 = (s32[256,256]{1,0:T(8,128)S(1)}, s32[256,256]{1,0:T(8,128)}, u32[]{:S(2)}) copy-start(s32[256,256]{1,0:T(8,128)} %count_hbm.3) | copy-start | bytes 786436
  7.1 0.7 %copy-start.3 = (f32[8]{0:T(128)S(1)}, f32[8]{0:T(128)}, u32[]{:S(2)}) copy-start(f32[8]{0:T(128)} %thick.5) | copy-start | bytes 100
  7.8 12.3 %copy-start.2 = (f32[256,256]{1,0:T(8,128)S(1)}, f32[256,256]{1,0:T(8,128)}, u32[]{:S(2)}) copy-start(f32[256,256]{1,0:T(8,128)} %old_hbm.1) | copy-start | bytes 786436
  22.3 7.6 %collective-permute-start.2 = (f32[40,384]{1,0:T(8,128)S(1)}, f32[40,384]{1,0:T(8,128)S(1)}, u32[]{:S(2)}, u32[]{:S(2)}) collective-permute-start(f32[40,384]{1,0:T(8,128)S(1)} %get-tuple-element.21.to_east), channel_id=1, source_target_pairs={{0,1},{1,2},{2,3},{3,4},{4,5},{5,6},{6,7},{7,0},{8,9},{9,10},{10,1... | collective-permute-start | bytes 184328 | tf_op jit(solution)/shard_map/ppermute | solution.py:544
  24.6 5.5 %collective-permute-start.3 = (f32[40,384]{1,0:T(8,128)S(1)}, f32[40,384]{1,0:T(8,128)S(1)}, u32[]{:S(2)}, u32[]{:S(2)}) collective-permute-start(f32[40,384]{1,0:T(8,128)S(1)} %get-tuple-element.22.to_west), channel_id=1, source_target_pairs={{0,7},{1,0},{2,1},{3,2},{4,3},{5,4},{6,5},{7,6},{8,15},{9,8},{10,9... | collective-permute-start | bytes 184328 | tf_op jit(solution)/shard_map/ppermute | solution.py:544

commit v6 on v5

--- a/solution.py
+++ b/solution.py
@@ -1,3 +1,5 @@
+import math
+
 import jax
 import jax.numpy as jnp
 from jax import lax
@@ -19,8 +21,7 @@
 STEP = 8
 GRANT = 16 * 2**20
 INNER_GRANT = 52 * 2**20
-MIX_UNROLL = 16
-SPREAD_UNROLL = 10
+CHUNK = 32
 WIDE = 17
 WIDE_INNER = 16
 
@@ -41,19 +42,16 @@
     return pltpu.roll(value, by % LANES, 1)
 
 
-def neighbours(tiles, lane, by=1):
+def neighbours(tiles, lane, by=1, want_east=True, want_west=True):
     count = len(tiles)
-    back = [None if t is None else turn(t, -by) for t in tiles]
-    forth = [None if t is None else turn(t, by) for t in tiles]
-
-    def pick(mask, other, own):
-        if other is None and own is None:
-            return None
-        zero = jnp.zeros((STEP, LANES), jnp.float32)
-        return jnp.where(mask, zero if other is None else other, zero if own is None else own)
-
-    east = [pick(lane >= LANES - by, back[(i + 1) % count], back[i]) for i in range(count)]
-    west = [pick(lane < by, forth[i - 1], forth[i]) for i in range(count)]
+    zero = jnp.zeros((STEP, LANES), jnp.float32)
+    east = west = None
+    if want_east:
+        back = [zero if t is None else turn(t, -by) for t in tiles]
+        east = [jnp.where(lane >= LANES - by, back[(i + 1) % count], back[i]) for i in range(count)]
+    if want_west:
+        forth = [zero if t is None else turn(t, by) for t in tiles]
+        west = [jnp.where(lane < by, forth[i - 1], forth[i]) for i in range(count)]
     return east, west
 
 
@@ -68,39 +66,35 @@
         mixed[t, near(), :] = value
 
 
-def spread_strip(baro, mixed, row, lane):
+def spread_strip(baro, mixed, row, out, at, lane):
     tiles = baro.shape[0]
     both = range(tiles + 1)
     near = lambda by=0: pl.ds(row + by, STEP)
-    far, once, still = [], [], []
+    far, once = [], []
     for t in both:
         own = mixed[t, near(), :]
         beside = mixed[t, near(1), :] + mixed[t, near(-1), :]
         beyond = mixed[t, near(2), :] + mixed[t, near(-2), :]
         once.append(2.0 * beside - 8.0 * own)
-        still.append(beyond - 8.0 * beside + 20.0 * own)
+        still = beyond - 8.0 * beside + 20.0 * own
         if t < tiles:
             pressure = 10.0 * baro[t, near(), :]
             around = baro[t, near(2), :] + baro[t, near(-2), :]
             own = own + pressure
-            still[t] += 10.0 * around - 4.0 * pressure
+            still += 10.0 * around - 4.0 * pressure
         far.append(own)
-    last, first = lane == LANES - 1, lane == 0
-    ring = tiles + 1
-    back = [turn(v, -1) for v in far]
-    forth = [turn(v, 1) for v in far]
-    easts = [once[t] + jnp.where(last, back[(t + 1) % ring], back[t]) for t in both]
-    wests = [once[t] + jnp.where(first, forth[t - 1], forth[t]) for t in both]
-    back = [turn(v, -1) for v in easts]
-    forth = [turn(v, 1) for v in wests]
-    return [
-        still[t]
-        + (
-            jnp.where(last, back[(t + 1) % ring], back[t])
-            + jnp.where(first, forth[t - 1], forth[t])
-        )
-        for t in both
-    ]
+        out[2, t, at, :] = still
+    east, west = neighbours(far, lane)
+    for t in both:
+        out[0, t, at, :] = once[t] + east[t]
+        out[1, t, at, :] = once[t] + west[t]
+
+
+def gather_strip(staged, at, lane):
+    both = range(staged.shape[1])
+    east, _ = neighbours([staged[0, t, at, :] for t in both], lane, 1, True, False)
+    _, west = neighbours([staged[1, t, at, :] for t in both], lane, 1, False, True)
+    return [staged[2, t, at, :] + (east[t] + west[t]) for t in both]
 
 
 def sweep(body, strips, unroll, carry=0, first=0, stride=1):
@@ -112,12 +106,15 @@
     return [pl.ds(t * LANES, LANES) for t in range(tiles)]
 
 
-def inner_kernel(thick, fields, count_hbm, part, pack, block, mixed, count, arrivals, others):
-    level = pl.program_id(0)
+def inner_kernel(
+    thick, fields, count_hbm, part, pack, block, mixed, staged, beyond, count, arrivals, others
+):
     levels = fields.shape[1]
     tiles, height, _ = count.shape
     lane = lane_index()
     cols = lane_tiles(tiles)
+    strips = height // STEP
+    size = math.gcd(strips, CHUNK)
 
     def arrival(at, t):
         return pltpu.make_async_copy(
@@ -128,52 +125,67 @@
         pltpu.make_async_copy(count_hbm.at[:, cols[t]], count.at[t], others.at[t])
         for t in range(tiles)
     ]
-
-    @pl.when(level == 0)
-    def _():
+    for at in range(levels):
         for t in range(tiles):
-            arrival(0, t).start()
-        for copy in counted:
-            copy.start()
-        for at in range(1, levels):
+            arrival(at, t).start()
+    for copy in counted:
+        copy.start()
+    part[...] = jnp.zeros_like(part)
+    pack[...] = jnp.zeros_like(pack)
+
+    def mix(n, c):
+        chunks = strips // size
+        level, chunk = lax.div(n, chunks), lax.rem(n, chunks)
+
+        @pl.when(chunk == 0)
+        def _():
             for t in range(tiles):
-                arrival(at, t).start()
-        part[...] = jnp.zeros_like(part)
-        pack[...] = jnp.zeros_like(pack)
-        for copy in counted:
-            copy.wait()
-
-    for t in range(tiles):
-        arrival(level, t).wait()
-    zonal, merid, baro = (block.at[level, f] for f in range(3))
-    thickness = thick[level]
-
-    def mix(i, c):
-        mix_strip(zonal, merid, mixed, PAD + i * STEP, lane)
+                arrival(level, t).wait()
+
+        for q in range(size):
+            row = PAD + pl.multiple_of(chunk * (size * STEP), STEP) + q * STEP
+            mix_strip(block.at[level, 0], block.at[level, 1], mixed.at[level], row, lane)
         return c
 
-    def spread(i, c):
-        row = ROWS - DEEP + i * STEP
-        total = spread_strip(baro, mixed, PAD + row, lane)
+    def chunked(body):
+        chunks = strips // size
+
+        def step(n, c):
+            level, chunk = lax.div(n, chunks), lax.rem(n, chunks)
+            for q in range(size):
+                body(level, pl.multiple_of(chunk * (size * STEP), STEP) + q * STEP)
+            return c
+
+        sweep(step, levels * chunks, 1)
+
+    def spread(level, row):
+        at = pl.ds(row, STEP)
+        spread_strip(block.at[level, 2], mixed.at[level], PAD + row, staged.at[level], at, lane)
+
+    def weigh(level, row):
+        at, rows = pl.ds(row, STEP), pl.ds(ROWS + row, STEP)
+        total = gather_strip(staged.at[level], at, lane)
+        for t in range(tiles):
+            weight = jnp.where(count[t, at, :] > level, thick[level], 0.0)
+            part[t, rows, :] += weight * total[t]
+        beyond[level, at, :] = total[tiles]
+
+    def put(level, row):
         rows = pl.ds(ROWS + row, STEP)
-        for t in range(tiles):
-            weight = jnp.where(count[t, pl.ds(row, STEP), :] > level, thickness, 0.0)
-            part[t, rows, :] += weight * total[t]
-        pack[rows, :] += pltpu.roll(total[tiles], 8 * level + REACH, 1)
-        return c
-
-    sweep(mix, height // STEP, MIX_UNROLL)
-    strips = height // STEP - 1
-    main = strips // SPREAD_UNROLL * SPREAD_UNROLL
-    sweep(spread, main, SPREAD_UNROLL)
-    for i in range(main, strips):
-        spread(i, 0)
+        pack[rows, :] += pltpu.roll(beyond[level, pl.ds(row, STEP), :], 8 * level + REACH, 1)
+
+    sweep(mix, levels * (strips // size), 1)
+    for copy in counted:
+        copy.wait()
+    chunked(spread)
+    chunked(weigh)
+    chunked(put)
 
 
 def edge_kernel(
     thick, fields, south, north, count_hbm, old_hbm, part_in, pack_in,
     part, depth, guess, to_east, to_west,
-    pack, block, mixed, wet, edges, count, old, arrivals, others,
+    pack, block, mixed, staged, beyond, wet, edges, count, old, arrivals, others,
 ):
     levels = fields.shape[1]
     height, width = count.shape
@@ -236,25 +248,32 @@
                 mix_strip(block.at[side, 0, k], block.at[side, 1, k], mixed.at[side, k], row, lane)
         return c
 
-    def spread(k, carry):
+    every = pl.ds(0, STEP)
+
+    def spread(k, c):
+        for side, (row, _) in enumerate(plans):
+            spread_strip(block.at[side, 2, k], mixed.at[side, k], row, staged.at[side, k], every, lane)
+        return c
+
+    def weigh(k, carry):
         found = []
         number, thickness = k.astype(jnp.float32), thick[k]
-        for side, (row, _) in enumerate(plans):
-            total = spread_strip(block.at[side, 2, k], mixed.at[side, k], row, lane)
-            e = starts[side]
+        for side, e in enumerate(starts):
+            total = gather_strip(staged.at[side, k], every, lane)
             for t in range(tiles):
                 weight = jnp.where(wet[t, e : e + STEP, :] > number, thickness, 0.0)
                 found.append(weight * total[t])
-            found.append(pltpu.roll(total[tiles], 8 * k + REACH, 1))
+            beyond[side, k] = total[tiles]
         return tuple(a + b for a, b in zip(carry, found))
 
     sweep(mix, levels, 4)
+    sweep(spread, levels, 4)
     zero = jnp.zeros((STEP, LANES), jnp.float32)
-    found = sweep(spread, levels, 4, (zero,) * (2 * (tiles + 1)))
+    found = sweep(weigh, levels, 4, (zero,) * (2 * tiles))
     for side, e in enumerate(starts):
         for t in range(tiles):
-            part[t, e : e + STEP, :] = found[side * (tiles + 1) + t]
-        pack[e : e + STEP, :] = found[side * (tiles + 1) + tiles]
+            part[t, e : e + STEP, :] = found[side * tiles + t]
+        pack[e : e + STEP, :] = sum(turn(beyond[side, k], 8 * k + REACH) for k in range(levels))
 
     scale = -0.5 * VISCOSITY
     for e in range(0, ext, STEP):
@@ -305,7 +324,7 @@
 def solve_kernel(
     thick, part, depth, guess, to_east, to_west, from_west, from_east,
     base0, base1, base2, base3, base4, diag, moments,
-    turned, fix, halo_part, halo_depth, halo_guess, half, half_w, inverse, even_e, even_w, odd_e, odd_w,
+    turned, upright, fix, halo_part, halo_depth, halo_guess, half, half_w, inverse, even_e, even_w, odd_e, odd_w,
 ):
     tiles, ext, _ = part.shape
     height = ext - 2 * ROWS
@@ -347,15 +366,15 @@
             buf[:, at : at + PAD, :] = jnp.zeros((tiles + 1, PAD, LANES), jnp.float32)
     near = (lane < EDGE) | (lane >= LANES - EDGE)
     close = (lane < DEEP) | (lane >= LANES - DEEP)
-    for at in range(0, ext, LANES):
-        block = jnp.transpose(turned[:, at : at + LANES])
-        for e in range(at, min(at + LANES, ext), STEP):
-            r = e + PAD
-            tile = block[e - at : e - at + STEP, :]
-            halo_depth[r : r + STEP, :] = jnp.where(near, turn(tile, -40), 0.0)
-            halo_guess[r : r + STEP, :] = jnp.where(near, turn(tile, -60), 0.0)
-            halo_part[e : e + STEP, :] = jnp.where(close, tile, 0.0)
-            fix[e : e + STEP, :] = turn(tile, -80)
+    for at in range(0, turned.shape[1], LANES):
+        upright[at : at + LANES, :] = jnp.transpose(turned[:, at : at + LANES])
+    for e in range(0, ext, STEP):
+        r = e + PAD
+        tile = upright[e : e + STEP, :]
+        halo_depth[r : r + STEP, :] = jnp.where(near, turn(tile, -40), 0.0)
+        halo_guess[r : r + STEP, :] = jnp.where(near, turn(tile, -60), 0.0)
+        halo_part[e : e + STEP, :] = jnp.where(close, tile, 0.0)
+        fix[e : e + STEP, :] = turn(tile, -80)
 
     def span(i, by=0):
         return pl.ds(PAD + i * STEP + by, STEP)
@@ -385,9 +404,9 @@
                 read(depth, halo_depth, span(i)), read(depth, halo_depth, span(i, 1))
             )
         ]
-        east, _ = neighbours(low, lane)
+        east, west = neighbours(low, lane)
         corner = [0.5 * jnp.minimum(a, b) for a, b in zip(low, east)]
-        _, west = neighbours(corner, lane)
+        west = [0.5 * jnp.minimum(a, b) for a, b in zip(low, west)]
         for t in both:
             half[t, span(i), :] = corner[t]
             half_w[t, span(i), :] = west[t]
@@ -563,7 +582,6 @@
     tiles, padded = width // LANES, ext + 2 * PAD
     smem = pl.BlockSpec(memory_space=pltpu.SMEM)
     vmem = pl.BlockSpec(memory_space=pltpu.VMEM)
-    whole = lambda *dims: pl.BlockSpec(dims, lambda k: (0,) * len(dims))
     hbm = pl.BlockSpec(memory_space=pltpu.HBM)
     shaped = lambda *dims: jax.ShapeDtypeStruct(dims, f32)
     scratch = lambda *dims: pltpu.VMEM(dims, f32)
@@ -572,13 +590,14 @@
     params = lambda size: pltpu.CompilerParams(vmem_limit_bytes=size)
     partial, packed = pl.pallas_call(
         inner_kernel,
-        grid=(levels,),
         in_specs=[smem, hbm, hbm],
-        out_specs=[whole(*main), whole(ext, LANES)],
+        out_specs=[vmem] * 2,
         out_shape=[shaped(*main), shaped(ext, LANES)],
         scratch_shapes=[
             scratch(levels, 3, tiles, height + 2 * PAD, LANES),
-            scratch(tiles + 1, height + 2 * PAD, LANES),
+            scratch(levels, tiles + 1, height + 2 * PAD, LANES),
+            scratch(levels, 3, tiles + 1, height, LANES),
+            scratch(levels, height, LANES),
             pltpu.VMEM((tiles, height, LANES), level_count.dtype),
             pltpu.SemaphoreType.DMA((levels, tiles)),
             pltpu.SemaphoreType.DMA((tiles,)),
@@ -600,6 +619,8 @@
             scratch(tall, LANES),
             scratch(2, 3, levels, tiles, 3 * ROWS, LANES),
             scratch(2, levels, tiles + 1, 3 * ROWS, LANES),
+            scratch(2, levels, 3, tiles + 1, STEP, LANES),
+            scratch(2, levels, STEP, LANES),
             scratch(*main),
             scratch(tall, LANES),
             pltpu.VMEM((height, width), level_count.dtype),
@@ -623,7 +644,8 @@
             *[shaped(tiles, height, LANES)] * (ITERS + 2),
             shaped(devices, 1, LANES),
         ],
-        scratch_shapes=[scratch(LANES, tall), scratch(ext, LANES), scratch(ext, LANES)]
+        scratch_shapes=[scratch(LANES, tall), scratch(tall, LANES)]
+        + [scratch(ext, LANES)] * 2
         + [scratch(padded, LANES)] * 2
         + [scratch(tiles + 1, padded, LANES)] * 2
         + [scratch(tiles + 1, ext, LANES)]

time: 49.8 us -> 45.9 us (0.922)
  Pallas kernels: 20.9 us -> 17 us
    pallas_call x1, Pallas kernels: 12.2 us -> 9.36 us  [shards(): pl.pallas_call(inner_kernel, in_specs=[smem, hbm, hbm], out_specs=[vmem]...]
    pallas_call x1, Pallas kernels: 5.18 us -> 4.15 us  [shards(): pl.pallas_call(solve_kernel, in_specs=[smem] + [vmem] * 7, out_specs=[vme...]
  transfers between devices with their start and end apart: 4 -> 4, of which waited for: 2 -> 2; matrix products, arithmetic and copies ran while one was open for 0% -> 0% of each run, Pallas kernels for 25% -> 21%
where the time goes in v6:
time: 45.9 us; the launch traced here: 45.5 us
  Pallas kernels  17 us (37%)
  blocking collectives  12.9 us (28%)
  starting transfers between devices  7.97 us (17%)
  local copies, waits for them, and re-layouts  3.66 us (8%)
  waiting for transfers between devices  2.44 us (5%)
  other arithmetic  0.9 us (2%)
  between operations  0.71 us (2%)
    all_to_all x1, blocking collectives, shards(): lax.all_to_all(moments, ('by', 'bx'), split_axis=0, concat_axis=0, tiled=...  12.9 us
    pallas_call x1, Pallas kernels, shards(): pl.pallas_call(inner_kernel, in_specs=[smem, hbm, hbm], out_specs=[vmem]...  9.36 us
    ppermute x4, starting transfers between devices, shift(): lax.ppermute(value, axis, [(i, (i + by) % size) for i in range(size)])  7.97 us
    pallas_call x1, Pallas kernels, shards(): pl.pallas_call(solve_kernel, in_specs=[smem] + [vmem] * 7, out_specs=[vme...  4.15 us
    ppermute x4, waiting for transfers between devices, shift(): lax.ppermute(value, axis, [(i, (i + by) % size) for i in range(size)])  2.44 us
    pallas_call x1, Pallas kernels, shards(): pl.pallas_call(edge_kernel, in_specs=[smem, hbm, vmem, vmem, hbm, hbm, vm...  2.24 us
    unnamed x8, local copies, waits for them, and re-layouts  1.61 us
    pallas_call x1, Pallas kernels, shards(): pl.pallas_call(combine_kernel, in_specs=[vmem] * (ITERS + 4), out_specs=[...  1.21 us
  transfers between devices with their start and end apart: 4, of which 2 were waited for; matrix products, arithmetic and copies ran while one was open for 0% of the time, Pallas kernels for 21%

profile of v6, /device:TPU:0, one launch (start us, length us, event | category | flops | bytes accessed | tf_op | source)
XLA Modules:
  0.0 45.5 jit_solution(8761549963875535451)
XLA Ops:
  0.6 0.0 copy-start
  0.6 0.9 %slice_bitcast_fusion = (f32[1,8,256]{2,1,0:T(8,128)S(1)}, f32[1,8,256]{2,1,0:T(8,128)S(1)}) fusion(f32[256,256]{1,0:T(8,128)} %old_hbm.1), kind=kLoop, calls=%fused_computation.2 | loop fusion | bytes 32768 | tf_op jit(solution)/shard_map/broadcast_in_dim | solution.py:575
  1.5 0.9 %convert_bitcast_fusion = (f32[1,8,256]{2,1,0:T(8,128)S(1)}, f32[1,8,256]{2,1,0:T(8,128)S(1)}) fusion(s32[256,256]{1,0:T(8,128)} %count_hbm.3), kind=kLoop, calls=%fused_computation.3 | loop fusion | flops 4096 | bytes 32768 | tf_op jit(solution)/shard_map/broadcast_in_dim | solution.py:575
  2.4 1.2 %fusion = (f32[3,8,8,256]{3,2,1,0:T(8,128)S(1)}, f32[3,8,8,256]{3,2,1,0:T(8,128)S(1)}) fusion(f32[3,8,256,256]{3,2,1,0:T(8,128)} %fields.3), kind=kLoop, calls=%fused_computation.6 | loop fusion | bytes 786432 | tf_op jit(solution)/shard_map/slice | solution.py:572
  3.6 0.5 %collective-permute-start = (f32[26,8,256]{2,1,0:T(8,128)S(1)}, f32[26,8,256]{2,1,0:T(8,128)S(1)}, u32[]{:S(2)}, u32[]{:S(2)}) collective-permute-start(f32[26,8,256]{2,1,0:T(8,128)S(1)} %pad_maximum_fusion), channel_id=1, source_target_pairs={{0,8},{8,16},{16,24},{24,0},{1,9},{9,17},{17,25},{25,1},{2,10},{10... | collective-permute-start | bytes 638984 | tf_op jit(solution)/shard_map/ppermute | solution.py:563
  4.1 2.0 %collective-permute-start.1 = (f32[26,8,256]{2,1,0:T(8,128)S(1)}, f32[26,8,256]{2,1,0:T(8,128)S(1)}, u32[]{:S(2)}, u32[]{:S(2)}) collective-permute-start(f32[26,8,256]{2,1,0:T(8,128)S(1)} %pad_maximum_fusion.1), channel_id=1, source_target_pairs={{0,24},{8,0},{16,8},{24,16},{1,25},{9,1},{17,9},{25,17},{2,26},{10... | collective-permute-start | bytes 638984 | tf_op jit(solution)/shard_map/ppermute | solution.py:563
  6.2 0.0 copy-start.1
  6.2 0.9 %copy-done.1 = s32[256,256]{1,0:T(8,128)S(1)} copy-done((s32[256,256]{1,0:T(8,128)S(1)}, s32[256,256]{1,0:T(8,128)}, u32[]{:S(2)}) %copy-start.1) | copy-done | bytes 262168
  7.1 0.0 copy-start.3
  7.1 0.7 %copy-done.3 = f32[8]{0:T(128)S(1)} copy-done((f32[8]{0:T(128)S(1)}, f32[8]{0:T(128)}, u32[]{:S(2)}) %copy-start.3) | copy-done | bytes 56
  7.8 0.0 copy-start.2
  7.8 9.4 %inner_forcing.1 = (f32[2,272,128]{2,1,0:T(8,128)S(1)}, f32[272,128]{1,0:T(8,128)S(1)}) custom-call(f32[8]{0:T(128)S(1)} %copy-done.3, f32[3,8,256,256]{3,2,1,0:T(8,128)} %fields.3, s32[256,256]{1,0:T(8,128)S(1)} %copy-done.1), custom_call_target="tpu_custom_call" | custom-call | flops 20971520 | bytes 6291456 | tf_op jit(solution)/shard_map/inner_forcing/pallas_call | solution.py:591
  17.1 0.0 collective-permute-done.south
  17.1 0.0 collective-permute-done.1.north
  17.2 0.0 copy-done
  17.2 0.0 copy-done.2
  17.2 2.2 %edge_forcing.1 = (f32[2,272,128]{2,1,0:T(8,128)S(1)}, f32[2,288,128]{2,1,0:T(8,128)S(1)}, f32[2,288,128]{2,1,0:T(8,128)S(1)}, f32[40,384]{1,0:T(8,128)S(1)}, f32[40,384]{1,0:T(8,128)S(1)}) custom-call(f32[8]{0:T(128)S(1)} %copy-done.3, f32[3,8,256,256]{3,2,1,0:T(8,128)S(1)} %copy-done, f32[26,8,256]{2,1,0:T(8,128)S(1)} %collective-permute-done.south, ...), custom_call_target="tpu_custom_call" | custom-call | tf_op jit(solution)/shard_map/edge_forcing/pallas_call | solution.py:613
  19.4 2.3 %collective-permute-start.2 = (f32[40,384]{1,0:T(8,128)S(1)}, f32[40,384]{1,0:T(8,128)S(1)}, u32[]{:S(2)}, u32[]{:S(2)}) collective-permute-start(f32[40,384]{1,0:T(8,128)S(1)} %get-tuple-element.21.to_east), channel_id=1, source_target_pairs={{0,1},{1,2},{2,3},{3,4},{4,5},{5,6},{6,7},{7,0},{8,9},{9,10},{10,1... | collective-permute-start | bytes 184328 | tf_op jit(solution)/shard_map/ppermute | solution.py:563
  21.7 3.1 %collective-permute-start.3 = (f32[40,384]{1,0:T(8,128)S(1)}, f32[40,384]{1,0:T(8,128)S(1)}, u32[]{:S(2)}, u32[]{:S(2)}) collective-permute-start(f32[40,384]{1,0:T(8,128)S(1)} %get-tuple-element.22.to_west), channel_id=1, source_target_pairs={{0,7},{1,0},{2,1},{3,2},{4,3},{5,4},{6,5},{7,6},{8,15},{9,8},{10,9... | collective-permute-start | bytes 184328 | tf_op jit(solution)/shard_map/ppermute | solution.py:563
  24.8 2.1 %collective-permute-done.2.from_west = f32[40,384]{1,0:T(8,128)S(1)} collective-permute-done((f32[40,384]{1,0:T(8,128)S(1)}, f32[40,384]{1,0:T(8,128)S(1)}, u32[]{:S(2)}, u32[]{:S(2)}) %collective-permute-start.2) | collective-permute-done | bytes 61472 | tf_op jit(solution)/shard_map/ppermute | solution.py:563
  27.0 0.3 collective-permute-done.3.from_east
  27.3 4.2 %krylov.1 = (f32[2,256,128]{2,1,0:T(8,128)S(1)}, f32[2,256,128]{2,1,0:T(8,128)S(1)}, f32[2,256,128]{2,1,0:T(8,128)S(1)}, f32[2,256,128]{2,1,0:T(8,128)S(1)}, f32...) custom-call(f32[8]{0:T(128)S(1)} %copy-done.3, ...), custom_call_target="tpu_custom_call" | custom-call | tf_op jit(solution)/shard_map/krylov/pallas_call | solution.py:639
  31.4 12.9 %all_to_all.5.moments = f32[32,1,128]{2,1,0:T(1,128)S(1)} all-to-all(f32[32,1,128]{2,1,0:T(1,128)S(1)} %get-tuple-element.23), channel_id=1, replica_groups=mesh['by'=4,'bx'=8] {'by','bx'}, dimensions={0} | all-to-all | bytes 32768 | tf_op jit(solution)/shard_map/all_to_all | solution.py:657
  44.3 1.2 %combine.1 = (f32[256,256]{1,0:T(8,128)}, f32[256,256]{1,0:T(8,128)}) custom-call(f32[32,1,128]{2,1,0:T(1,128)S(1)} %all_to_all.5.moments, f32[2,288,128]{2,1,0:T(8,128)S(1)} %get-tuple-element.20.guess, f32[2,256,128]{2,1,0:T(8,128)S(1)} %get-tuple-element.24.base0, f32[2,256,128]{2,1,0:T(8,128)S(1)} %get-tuple-element.25.base1, ...), custom_call_target="tpu_custom_call" | custom-call | tf_op jit(solution)/shard_map/combine/pallas_call | solution.py:659
  (2 shorter events, 0.0 us)
Async XLA Ops:
  0.6 16.5 %copy-start = (f32[3,8,256,256]{3,2,1,0:T(8,128)S(1)}, f32[3,8,256,256]{3,2,1,0:T(8,128)}, u32[]{:S(2)}) copy-start(f32[3,8,256,256]{3,2,1,0:T(8,128)} %fields.3) | copy-start | bytes 18874372
  3.6 13.6 %collective-permute-start = (f32[26,8,256]{2,1,0:T(8,128)S(1)}, f32[26,8,256]{2,1,0:T(8,128)S(1)}, u32[]{:S(2)}, u32[]{:S(2)}) collective-permute-start(f32[26,8,256]{2,1,0:T(8,128)S(1)} %pad_maximum_fusion), channel_id=1, source_target_pairs={{0,8},{8,16},{16,24},{24,0},{1,9},{9,17},{17,25},{25,1},{2,10},{10... | collective-permute-start | bytes 638984 | tf_op jit(solution)/shard_map/ppermute | solution.py:563
  4.1 13.0 %collective-permute-start.1 = (f32[26,8,256]{2,1,0:T(8,128)S(1)}, f32[26,8,256]{2,1,0:T(8,128)S(1)}, u32[]{:S(2)}, u32[]{:S(2)}) collective-permute-start(f32[26,8,256]{2,1,0:T(8,128)S(1)} %pad_maximum_fusion.1), channel_id=1, source_target_pairs={{0,24},{8,0},{16,8},{24,16},{1,25},{9,1},{17,9},{25,17},{2,26},{10... | collective-permute-start | bytes 638984 | tf_op jit(solution)/shard_map/ppermute | solution.py:563
  6.2 0.9 %copy-start.1 = (s32[256,256]{1,0:T(8,128)S(1)}, s32[256,256]{1,0:T(8,128)}, u32[]{:S(2)}) copy-start(s32[256,256]{1,0:T(8,128)} %count_hbm.3) | copy-start | bytes 786436
  7.1 0.7 %copy-start.3 = (f32[8]{0:T(128)S(1)}, f32[8]{0:T(128)}, u32[]{:S(2)}) copy-start(f32[8]{0:T(128)} %thick.5) | copy-start | bytes 100
  7.8 9.4 %copy-start.2 = (f32[256,256]{1,0:T(8,128)S(1)}, f32[256,256]{1,0:T(8,128)}, u32[]{:S(2)}) copy-start(f32[256,256]{1,0:T(8,128)} %old_hbm.1) | copy-start | bytes 786436
  19.4 7.6 %collective-permute-start.2 = (f32[40,384]{1,0:T(8,128)S(1)}, f32[40,384]{1,0:T(8,128)S(1)}, u32[]{:S(2)}, u32[]{:S(2)}) collective-permute-start(f32[40,384]{1,0:T(8,128)S(1)} %get-tuple-element.21.to_east), channel_id=1, source_target_pairs={{0,1},{1,2},{2,3},{3,4},{4,5},{5,6},{6,7},{7,0},{8,9},{9,10},{10,1... | collective-permute-start | bytes 184328 | tf_op jit(solution)/shard_map/ppermute | solution.py:563
  21.7 5.5 %collective-permute-start.3 = (f32[40,384]{1,0:T(8,128)S(1)}, f32[40,384]{1,0:T(8,128)S(1)}, u32[]{:S(2)}, u32[]{:S(2)}) collective-permute-start(f32[40,384]{1,0:T(8,128)S(1)} %get-tuple-element.22.to_west), channel_id=1, source_target_pairs={{0,7},{1,0},{2,1},{3,2},{4,3},{5,4},{6,5},{7,6},{8,15},{9,8},{10,9... | collective-permute-start | bytes 184328 | tf_op jit(solution)/shard_map/ppermute | solution.py:563

commit v7 on v6

--- a/solution.py
+++ b/solution.py
@@ -22,8 +22,8 @@
 GRANT = 16 * 2**20
 INNER_GRANT = 52 * 2**20
 CHUNK = 32
-WIDE = 17
-WIDE_INNER = 16
+WIDE = 34
+WIDE_INNER = 32
 
 
 def message_rows(levels):
@@ -107,10 +107,11 @@
 
 
 def inner_kernel(
-    thick, fields, count_hbm, part, pack, block, mixed, staged, beyond, count, arrivals, others
+    thick, fields, counts, part, beyond, block, mixed, staged, arrivals
 ):
     levels = fields.shape[1]
-    tiles, height, _ = count.shape
+    height, width = counts.shape
+    tiles = width // LANES
     lane = lane_index()
     cols = lane_tiles(tiles)
     strips = height // STEP
@@ -121,17 +122,10 @@
             fields.at[:, at, :, cols[t]], block.at[at, :, t, pl.ds(PAD, height), :], arrivals.at[at, t]
         )
 
-    counted = [
-        pltpu.make_async_copy(count_hbm.at[:, cols[t]], count.at[t], others.at[t])
-        for t in range(tiles)
-    ]
     for at in range(levels):
         for t in range(tiles):
             arrival(at, t).start()
-    for copy in counted:
-        copy.start()
     part[...] = jnp.zeros_like(part)
-    pack[...] = jnp.zeros_like(pack)
 
     def mix(n, c):
         chunks = strips // size
@@ -156,7 +150,7 @@
                 body(level, pl.multiple_of(chunk * (size * STEP), STEP) + q * STEP)
             return c
 
-        sweep(step, levels * chunks, 1)
+        sweep(step, levels * chunks, 2)
 
     def spread(level, row):
         at = pl.ds(row, STEP)
@@ -165,30 +159,24 @@
     def weigh(level, row):
         at, rows = pl.ds(row, STEP), pl.ds(ROWS + row, STEP)
         total = gather_strip(staged.at[level], at, lane)
+        number = level.astype(jnp.float32)
         for t in range(tiles):
-            weight = jnp.where(count[t, at, :] > level, thick[level], 0.0)
+            weight = jnp.where(counts[at, cols[t]] > number, thick[level], 0.0)
             part[t, rows, :] += weight * total[t]
         beyond[level, at, :] = total[tiles]
 
-    def put(level, row):
-        rows = pl.ds(ROWS + row, STEP)
-        pack[rows, :] += pltpu.roll(beyond[level, pl.ds(row, STEP), :], 8 * level + REACH, 1)
-
     sweep(mix, levels * (strips // size), 1)
-    for copy in counted:
-        copy.wait()
     chunked(spread)
     chunked(weigh)
-    chunked(put)
 
 
 def edge_kernel(
-    thick, fields, south, north, count_hbm, old_hbm, part_in, pack_in,
+    thick, fields, south, north, counts, old_hbm, part_in, beyond_in,
     part, depth, guess, to_east, to_west,
-    pack, block, mixed, staged, beyond, wet, edges, count, old, arrivals, others,
+    block, mixed, staged, beyond, wet, edges, old, arrivals, others,
 ):
     levels = fields.shape[1]
-    height, width = count.shape
+    height, width = counts.shape
     tiles = width // LANES
     ext = height + 2 * ROWS
     forcing_at = message_rows(levels)[0]
@@ -196,8 +184,7 @@
     cols = lane_tiles(tiles)
 
     copies = [
-        pltpu.make_async_copy(count_hbm, count, others.at[0]),
-        pltpu.make_async_copy(old_hbm, old, others.at[1]),
+        pltpu.make_async_copy(old_hbm, old, others.at[0]),
     ]
     for f in range(3):
         for t, c in enumerate(cols):
@@ -226,17 +213,17 @@
             buf[:, at : at + PAD, :] = jnp.zeros((tiles, PAD, LANES), jnp.float32)
     inner = slice(2 * ROWS - DEEP, ext - (2 * ROWS - DEEP))
     part[:, inner, :] = part_in[:, inner, :]
-    pack[inner, :] = pack_in[inner, :]
-    for outer in (low, high, slice(ext, pack.shape[0])):
-        if outer.start < ext:
-            part[:, outer, :] = jnp.zeros((tiles, ROWS - DEEP, LANES), jnp.float32)
-        pack[outer, :] = jnp.zeros((outer.stop - outer.start, LANES), jnp.float32)
+    beyond[:, inner, :] = beyond_in[:, inner.start - ROWS : inner.stop - ROWS, :]
+    for outer in (low, high):
+        part[:, outer, :] = jnp.zeros((tiles, ROWS - DEEP, LANES), jnp.float32)
+    for outer in (low, slice(high.start, beyond.shape[1])):
+        beyond[:, outer, :] = jnp.zeros((levels, outer.stop - outer.start, LANES), jnp.float32)
     edges[ext:, :] = jnp.zeros((edges.shape[0] - ext, LANES), jnp.float32)
     for copy in copies:
         copy.wait()
     for t, c in enumerate(cols):
         wet[t, :ROWS, :] = south[3 * levels, :, c]
-        wet[t, ROWS : ROWS + height, :] = count[:, c].astype(jnp.float32)
+        wet[t, ROWS : ROWS + height, :] = counts[:, c]
         wet[t, ROWS + height :, :] = north[3 * levels, :, c]
 
     plans = ((ROWS - DEEP, (2, 10)), (2 * ROWS - DEEP, (10, 14)))
@@ -263,17 +250,16 @@
             for t in range(tiles):
                 weight = jnp.where(wet[t, e : e + STEP, :] > number, thickness, 0.0)
                 found.append(weight * total[t])
-            beyond[side, k] = total[tiles]
+            beyond[k, e : e + STEP, :] = total[tiles]
         return tuple(a + b for a, b in zip(carry, found))
 
-    sweep(mix, levels, 4)
-    sweep(spread, levels, 4)
+    sweep(mix, levels, levels)
+    sweep(spread, levels, levels)
     zero = jnp.zeros((STEP, LANES), jnp.float32)
-    found = sweep(weigh, levels, 4, (zero,) * (2 * tiles))
+    found = sweep(weigh, levels, levels, (zero,) * (2 * tiles))
     for side, e in enumerate(starts):
         for t in range(tiles):
             part[t, e : e + STEP, :] = found[side * tiles + t]
-        pack[e : e + STEP, :] = sum(turn(beyond[side, k], 8 * k + REACH) for k in range(levels))
 
     scale = -0.5 * VISCOSITY
     for e in range(0, ext, STEP):
@@ -311,11 +297,11 @@
         message[...] = jnp.zeros_like(message)
     for at in range(0, to_east.shape[1], LANES):
         span = slice(at, at + LANES)
-        turned = scale * jnp.transpose(pack[span, :])
         for k in range(levels):
             mine = slice(REACH * k, REACH * k + REACH)
-            to_west[mine, span] = turned[8 * k : 8 * k + REACH, :]
-            to_east[mine, span] = turned[8 * k + REACH : 8 * k + 2 * REACH, :]
+            turned = scale * jnp.transpose(beyond[k, span, :])
+            to_west[mine, span] = turned[LANES - REACH :, :]
+            to_east[mine, span] = turned[:REACH, :]
         turned = jnp.transpose(edges[span, :])
         to_east[forcing_at : forcing_at + size, span] = turned[:size, :]
         to_west[forcing_at : forcing_at + size, span] = turned[LANES // 2 : LANES // 2 + size, :]
@@ -568,11 +554,13 @@
     ext, tall = height + 2 * ROWS, height + LANES
     f32 = jnp.float32
 
+    counts = level_count.astype(f32)
+
     def edge(at):
         pick = lambda a: lax.slice_in_dim(a, at, at + ROWS, axis=a.ndim - 2)
         flat = pick(fields).reshape(3 * levels, ROWS, width)
         return jnp.concatenate(
-            [flat, pick(level_count).astype(f32)[None], pick(old_pressure)[None]], axis=0
+            [flat, pick(counts)[None], pick(old_pressure)[None]], axis=0
         )
 
     south = shift(edge(height - ROWS), "by", 1)
@@ -588,49 +576,44 @@
     main = (tiles, ext, LANES)
     loose = (tiles, padded, LANES)
     params = lambda size: pltpu.CompilerParams(vmem_limit_bytes=size)
-    partial, packed = pl.pallas_call(
+    partial, outside = pl.pallas_call(
         inner_kernel,
-        in_specs=[smem, hbm, hbm],
+        in_specs=[smem, hbm, vmem],
         out_specs=[vmem] * 2,
-        out_shape=[shaped(*main), shaped(ext, LANES)],
+        out_shape=[shaped(*main), shaped(levels, height, LANES)],
         scratch_shapes=[
             scratch(levels, 3, tiles, height + 2 * PAD, LANES),
             scratch(levels, tiles + 1, height + 2 * PAD, LANES),
             scratch(levels, 3, tiles + 1, height, LANES),
-            scratch(levels, height, LANES),
-            pltpu.VMEM((tiles, height, LANES), level_count.dtype),
             pltpu.SemaphoreType.DMA((levels, tiles)),
-            pltpu.SemaphoreType.DMA((tiles,)),
         ],
         compiler_params=params(INNER_GRANT),
         cost_estimate=pl.CostEstimate(
             flops=40 * fields.size // 3, bytes_accessed=4 * fields.size, transcendentals=0
         ),
         name="inner_forcing",
-    )(thickness, fields, level_count)
+    )(thickness, fields, counts)
 
     results = (main, loose, loose, (message, tall), (message, tall))
     part, depth, guess, to_east, to_west = pl.pallas_call(
         edge_kernel,
-        in_specs=[smem, hbm, vmem, vmem, hbm, hbm, vmem, vmem],
+        in_specs=[smem, hbm, vmem, vmem, vmem, hbm, vmem, vmem],
         out_specs=[vmem] * 5,
         out_shape=[shaped(*dims) for dims in results],
         scratch_shapes=[
-            scratch(tall, LANES),
             scratch(2, 3, levels, tiles, 3 * ROWS, LANES),
             scratch(2, levels, tiles + 1, 3 * ROWS, LANES),
             scratch(2, levels, 3, tiles + 1, STEP, LANES),
-            scratch(2, levels, STEP, LANES),
+            scratch(levels, tall, LANES),
             scratch(*main),
             scratch(tall, LANES),
-            pltpu.VMEM((height, width), level_count.dtype),
             scratch(height, width),
             pltpu.SemaphoreType.DMA((12 * tiles,)),
-            pltpu.SemaphoreType.DMA((2,)),
+            pltpu.SemaphoreType.DMA((1,)),
         ],
         compiler_params=params(GRANT),
         name="edge_forcing",
-    )(thickness, fields, south, north, level_count, old_pressure, partial, packed)
+    )(thickness, fields, south, north, counts, old_pressure, partial, outside)
 
     from_west = shift(to_east, "bx", 1)
     from_east = shift(to_west, "bx", -1)

time: 45.9 us -> 42.8 us (0.932)
  Pallas kernels: 17 us -> 14.4 us
  local copies, waits for them, and re-layouts: 3.66 us -> 2.93 us
    pallas_call x2, Pallas kernels: 11.6 us -> 9.97 us  [the longest x1 7.68 us: shards(): pl.pallas_call(inner_kernel, in_specs=[smem, hbm, vmem], out_specs=[vmem]...]
    convert_element_type x0 -> x1, other arithmetic: none -> 1.12 us  [shards(): counts = level_count.astype(f32)]
    unnamed x8 -> x6, local copies, waits for them, and re-layouts: 1.61 us -> 0.67 us
    pallas_call x1, Pallas kernels: 4.15 us -> 3.24 us  [shards(): pl.pallas_call(solve_kernel, in_specs=[smem] + [vmem] * 7, out_specs=[vme...]
    broadcast_in_dim x1 -> x0, other arithmetic: 0.87 us -> none  [edge(): pick(level_count).astype(f32)[None]]
  transfers between devices with their start and end apart: 4 -> 4, of which waited for: 2 -> 2; matrix products, arithmetic and copies ran while one was open for 0% -> 0% of each run, Pallas kernels for 21% -> 18%
where the time goes in v7:
time: 42.8 us; the launch traced here: 42.5 us
  Pallas kernels  14.4 us (34%)
  blocking collectives  12.9 us (30%)
  starting transfers between devices  7.97 us (19%)
  local copies, waits for them, and re-layouts  2.93 us (7%)
  waiting for transfers between devices  2.44 us (6%)
  other arithmetic  1.15 us (3%)
  between operations  0.72 us (2%)
    all_to_all x1, blocking collectives, shards(): lax.all_to_all(moments, ('by', 'bx'), split_axis=0, concat_axis=0, tiled=...  12.9 us
    ppermute x4, starting transfers between devices, shift(): lax.ppermute(value, axis, [(i, (i + by) % size) for i in range(size)])  7.97 us
    pallas_call x1, Pallas kernels, shards(): pl.pallas_call(inner_kernel, in_specs=[smem, hbm, vmem], out_specs=[vmem]...  7.68 us
    pallas_call x1, Pallas kernels, shards(): pl.pallas_call(solve_kernel, in_specs=[smem] + [vmem] * 7, out_specs=[vme...  3.24 us
    ppermute x4, waiting for transfers between devices, shift(): lax.ppermute(value, axis, [(i, (i + by) % size) for i in range(size)])  2.44 us
    pallas_call x1, Pallas kernels, shards(): pl.pallas_call(edge_kernel, in_specs=[smem, hbm, vmem, vmem, vmem, hbm, v...  2.29 us
    slice x1, local copies, waits for them, and re-layouts, edge(): pick = lambda a: lax.slice_in_dim(a, at, at + ROWS, axis=a.ndim - 2)  1.54 us
    pallas_call x1, Pallas kernels, shards(): pl.pallas_call(combine_kernel, in_specs=[vmem] * (ITERS + 4), out_specs=[...  1.18 us
  transfers between devices with their start and end apart: 4, of which 2 were waited for; matrix products, arithmetic and copies ran while one was open for 0% of the time, Pallas kernels for 18%

profile of v7, /device:TPU:0, one launch (start us, length us, event | category | flops | bytes accessed | tf_op | source)
XLA Modules:
  0.0 42.5 jit_solution(18400911941077701067)
XLA Ops:
  0.6 0.0 copy-start
  0.6 0.0 copy-start.1
  0.7 1.1 %convert_element_type.3.counts = f32[256,256]{1,0:T(8,128)S(1)} convert(s32[256,256]{1,0:T(8,128)} %param.5) | non-fusion elementwise | flops 65536 | bytes 524288 | tf_op jit(solution)/shard_map/convert_element_type | solution.py:557
  1.8 1.5 %fusion = (f32[3,8,8,256]{3,2,1,0:T(8,128)S(1)}, f32[3,8,8,256]{3,2,1,0:T(8,128)S(1)}) fusion(f32[3,8,256,256]{3,2,1,0:T(8,128)} %fields.3), kind=kLoop, calls=%fused_computation.6 | loop fusion | bytes 786432 | tf_op jit(solution)/shard_map/slice | solution.py:560
  3.3 0.7 %slice_bitcast_fusion = (f32[1,8,256]{2,1,0:T(8,128)S(1)}, f32[1,8,256]{2,1,0:T(8,128)S(1)}, f32[1,8,256]{2,1,0:T(8,128)S(1)}, f32[1,8,256]{2,1,0:T(8,128)S(1)}) fusion(f32[256,256]{1,0:T(8,128)S(1)} %convert_element_type.3.counts, f32[256,256]{1,0:T(8,128)} %old_hbm.1), kind=kLoop, calls=%fused_computation.2 | loop fusion | bytes 65536 | tf_op jit(solution)/shard_map/broadcast_in_dim | solution.py:563
  4.1 0.5 %collective-permute-start = (f32[26,8,256]{2,1,0:T(8,128)S(1)}, f32[26,8,256]{2,1,0:T(8,128)S(1)}, u32[]{:S(2)}, u32[]{:S(2)}) collective-permute-start(f32[26,8,256]{2,1,0:T(8,128)S(1)} %pad_maximum_fusion), channel_id=1, source_target_pairs={{0,8},{8,16},{16,24},{24,0},{1,9},{9,17},{17,25},{25,1},{2,10},{10... | collective-permute-start | bytes 638984 | tf_op jit(solution)/shard_map/ppermute | solution.py:549
  4.6 2.0 %collective-permute-start.1 = (f32[26,8,256]{2,1,0:T(8,128)S(1)}, f32[26,8,256]{2,1,0:T(8,128)S(1)}, u32[]{:S(2)}, u32[]{:S(2)}) collective-permute-start(f32[26,8,256]{2,1,0:T(8,128)S(1)} %pad_maximum_fusion.1), channel_id=1, source_target_pairs={{0,24},{8,0},{16,8},{24,16},{1,25},{9,1},{17,9},{25,17},{2,26},{10... | collective-permute-start | bytes 638984 | tf_op jit(solution)/shard_map/ppermute | solution.py:549
  6.6 0.0 copy-start.2
  6.6 0.7 %copy-done.2 = f32[8]{0:T(128)S(1)} copy-done((f32[8]{0:T(128)S(1)}, f32[8]{0:T(128)}, u32[]{:S(2)}) %copy-start.2) | copy-done | bytes 56
  7.3 7.7 %inner_forcing.1 = (f32[2,272,128]{2,1,0:T(8,128)S(1)}, f32[8,256,128]{2,1,0:T(8,128)S(1)}) custom-call(f32[8]{0:T(128)S(1)} %copy-done.2, f32[3,8,256,256]{3,2,1,0:T(8,128)} %fields.3, f32[256,256]{1,0:T(8,128)S(1)} %convert_element_type.3.counts), custom_call_target="tpu_custom_call" | custom-call | flops 20971520 | bytes 6291456 | tf_op jit(solution)/shard_map/inner_forcing/pallas_call | solution.py:579
  15.0 0.0 collective-permute-done.south
  15.0 0.0 collective-permute-done.1.north
  15.0 0.0 copy-done
  15.0 0.0 copy-done.1
  15.0 2.3 %edge_forcing.1 = (f32[2,272,128]{2,1,0:T(8,128)S(1)}, f32[2,288,128]{2,1,0:T(8,128)S(1)}, f32[2,288,128]{2,1,0:T(8,128)S(1)}, f32[40,384]{1,0:T(8,128)S(1)}, f32[40,384]{1,0:T(8,128)S(1)}) custom-call(f32[8]{0:T(128)S(1)} %copy-done.2, f32[3,8,256,256]{3,2,1,0:T(8,128)S(1)} %copy-done, f32[26,8,256]{2,1,0:T(8,128)S(1)} %collective-permute-done.south, ...), custom_call_target="tpu_custom_call" | custom-call | tf_op jit(solution)/shard_map/edge_forcing/pallas_call | solution.py:598
  17.3 2.3 %collective-permute-start.2 = (f32[40,384]{1,0:T(8,128)S(1)}, f32[40,384]{1,0:T(8,128)S(1)}, u32[]{:S(2)}, u32[]{:S(2)}) collective-permute-start(f32[40,384]{1,0:T(8,128)S(1)} %get-tuple-element.21.to_east), channel_id=1, source_target_pairs={{0,1},{1,2},{2,3},{3,4},{4,5},{5,6},{6,7},{7,0},{8,9},{9,10},{10,1... | collective-permute-start | bytes 184328 | tf_op jit(solution)/shard_map/ppermute | solution.py:549
  19.6 3.1 %collective-permute-start.3 = (f32[40,384]{1,0:T(8,128)S(1)}, f32[40,384]{1,0:T(8,128)S(1)}, u32[]{:S(2)}, u32[]{:S(2)}) collective-permute-start(f32[40,384]{1,0:T(8,128)S(1)} %get-tuple-element.22.to_west), channel_id=1, source_target_pairs={{0,7},{1,0},{2,1},{3,2},{4,3},{5,4},{6,5},{7,6},{8,15},{9,8},{10,9... | collective-permute-start | bytes 184328 | tf_op jit(solution)/shard_map/ppermute | solution.py:549
  22.7 2.1 %collective-permute-done.2.from_west = f32[40,384]{1,0:T(8,128)S(1)} collective-permute-done((f32[40,384]{1,0:T(8,128)S(1)}, f32[40,384]{1,0:T(8,128)S(1)}, u32[]{:S(2)}, u32[]{:S(2)}) %collective-permute-start.2) | collective-permute-done | bytes 61472 | tf_op jit(solution)/shard_map/ppermute | solution.py:549
  24.9 0.3 collective-permute-done.3.from_east
  25.2 3.2 %krylov.1 = (f32[2,256,128]{2,1,0:T(8,128)S(1)}, f32[2,256,128]{2,1,0:T(8,128)S(1)}, f32[2,256,128]{2,1,0:T(8,128)S(1)}, f32[2,256,128]{2,1,0:T(8,128)S(1)}, f32...) custom-call(f32[8]{0:T(128)S(1)} %copy-done.2, ...), custom_call_target="tpu_custom_call" | custom-call | tf_op jit(solution)/shard_map/krylov/pallas_call | solution.py:622
  28.4 12.9 %all_to_all.5.moments = f32[32,1,128]{2,1,0:T(1,128)S(1)} all-to-all(f32[32,1,128]{2,1,0:T(1,128)S(1)} %get-tuple-element.23), channel_id=1, replica_groups=mesh['by'=4,'bx'=8] {'by','bx'}, dimensions={0} | all-to-all | bytes 32768 | tf_op jit(solution)/shard_map/all_to_all | solution.py:640
  41.3 1.2 %combine.1 = (f32[256,256]{1,0:T(8,128)}, f32[256,256]{1,0:T(8,128)}) custom-call(f32[32,1,128]{2,1,0:T(1,128)S(1)} %all_to_all.5.moments, f32[2,288,128]{2,1,0:T(8,128)S(1)} %get-tuple-element.20.guess, f32[2,256,128]{2,1,0:T(8,128)S(1)} %get-tuple-element.24.base0, f32[2,256,128]{2,1,0:T(8,128)S(1)} %get-tuple-element.25.base1, ...), custom_call_target="tpu_custom_call" | custom-call | tf_op jit(solution)/shard_map/combine/pallas_call | solution.py:642
  (2 shorter events, 0.0 us)
Async XLA Ops:
  0.6 14.4 %copy-start = (f32[3,8,256,256]{3,2,1,0:T(8,128)S(1)}, f32[3,8,256,256]{3,2,1,0:T(8,128)}, u32[]{:S(2)}) copy-start(f32[3,8,256,256]{3,2,1,0:T(8,128)} %fields.3) | copy-start | bytes 18874372
  0.6 14.4 %copy-start.1 = (f32[256,256]{1,0:T(8,128)S(1)}, f32[256,256]{1,0:T(8,128)}, u32[]{:S(2)}) copy-start(f32[256,256]{1,0:T(8,128)} %old_hbm.1) | copy-start | bytes 786436
  4.1 10.9 %collective-permute-start = (f32[26,8,256]{2,1,0:T(8,128)S(1)}, f32[26,8,256]{2,1,0:T(8,128)S(1)}, u32[]{:S(2)}, u32[]{:S(2)}) collective-permute-start(f32[26,8,256]{2,1,0:T(8,128)S(1)} %pad_maximum_fusion), channel_id=1, source_target_pairs={{0,8},{8,16},{16,24},{24,0},{1,9},{9,17},{17,25},{25,1},{2,10},{10... | collective-permute-start | bytes 638984 | tf_op jit(solution)/shard_map/ppermute | solution.py:549
  4.6 10.4 %collective-permute-start.1 = (f32[26,8,256]{2,1,0:T(8,128)S(1)}, f32[26,8,256]{2,1,0:T(8,128)S(1)}, u32[]{:S(2)}, u32[]{:S(2)}) collective-permute-start(f32[26,8,256]{2,1,0:T(8,128)S(1)} %pad_maximum_fusion.1), channel_id=1, source_target_pairs={{0,24},{8,0},{16,8},{24,16},{1,25},{9,1},{17,9},{25,17},{2,26},{10... | collective-permute-start | bytes 638984 | tf_op jit(solution)/shard_map/ppermute | solution.py:549
  6.6 0.7 %copy-start.2 = (f32[8]{0:T(128)S(1)}, f32[8]{0:T(128)}, u32[]{:S(2)}) copy-start(f32[8]{0:T(128)} %thick.5) | copy-start | bytes 100
  17.3 7.6 %collective-permute-start.2 = (f32[40,384]{1,0:T(8,128)S(1)}, f32[40,384]{1,0:T(8,128)S(1)}, u32[]{:S(2)}, u32[]{:S(2)}) collective-permute-start(f32[40,384]{1,0:T(8,128)S(1)} %get-tuple-element.21.to_east), channel_id=1, source_target_pairs={{0,1},{1,2},{2,3},{3,4},{4,5},{5,6},{6,7},{7,0},{8,9},{9,10},{10,1... | collective-permute-start | bytes 184328 | tf_op jit(solution)/shard_map/ppermute | solution.py:549
  19.6 5.5 %collective-permute-start.3 = (f32[40,384]{1,0:T(8,128)S(1)}, f32[40,384]{1,0:T(8,128)S(1)}, u32[]{:S(2)}, u32[]{:S(2)}) collective-permute-start(f32[40,384]{1,0:T(8,128)S(1)} %get-tuple-element.22.to_west), channel_id=1, source_target_pairs={{0,7},{1,0},{2,1},{3,2},{4,3},{5,4},{6,5},{7,6},{8,15},{9,8},{10,9... | collective-permute-start | bytes 184328 | tf_op jit(solution)/shard_map/ppermute | solution.py:549

commit v8 on v7

--- a/solution.py
+++ b/solution.py
@@ -534,14 +534,19 @@
             norm = following
     bases = (base0, base1, base2, base3, base4)
     for t in range(width // LANES):
-        for o in range(0, height, STEP):
-            vecs = [b[t, o : o + STEP, :] for b in bases]
+        cols = pl.ds(t * LANES, LANES)
+
+        def join(i, c, t=t, cols=cols):
+            rows = pl.ds(pl.multiple_of(i * STEP, STEP), STEP)
+            vecs = [b[t, rows, :] for b in bases]
             moved = sum(c * v for c, v in zip(answer, vecs))
             left = sum(c * v for c, v in zip(rest, vecs))
-            at = PAD + ROWS + o
-            cols = pl.ds(t * LANES, LANES)
-            pressure[o : o + STEP, cols] = guess[t, at : at + STEP, :] + moved
-            residual[o : o + STEP, cols] = diag[t, o : o + STEP, :] * left
+            there = pl.ds(pl.multiple_of(PAD + ROWS + i * STEP, STEP), STEP)
+            pressure[rows, cols] = guess[t, there, :] + moved
+            residual[rows, cols] = diag[t, rows, :] * left
+            return c
+
+        sweep(join, height // STEP, 8)
 
 
 def shift(value, axis, by):

time: 42.8 us -> 42.8 us (level)
  no operation moved by 1% of the time
where the time goes in v8:
time: 42.8 us; the launch traced here: 42.5 us
  Pallas kernels  14.4 us (34%)
  blocking collectives  12.9 us (30%)
  starting transfers between devices  7.97 us (19%)
  local copies, waits for them, and re-layouts  2.93 us (7%)
  waiting for transfers between devices  2.44 us (6%)
  other arithmetic  1.15 us (3%)
  between operations  0.72 us (2%)
    all_to_all x1, blocking collectives, shards(): lax.all_to_all(moments, ('by', 'bx'), split_axis=0, concat_axis=0, tiled=...  12.9 us
    ppermute x4, starting transfers between devices, shift(): lax.ppermute(value, axis, [(i, (i + by) % size) for i in range(size)])  7.97 us
    pallas_call x1, Pallas kernels, shards(): pl.pallas_call(inner_kernel, in_specs=[smem, hbm, vmem], out_specs=[vmem]...  7.68 us
    pallas_call x1, Pallas kernels, shards(): pl.pallas_call(solve_kernel, in_specs=[smem] + [vmem] * 7, out_specs=[vme...  3.24 us
    ppermute x4, waiting for transfers between devices, shift(): lax.ppermute(value, axis, [(i, (i + by) % size) for i in range(size)])  2.44 us
    pallas_call x1, Pallas kernels, shards(): pl.pallas_call(edge_kernel, in_specs=[smem, hbm, vmem, vmem, vmem, hbm, v...  2.29 us
    slice x1, local copies, waits for them, and re-layouts, edge(): pick = lambda a: lax.slice_in_dim(a, at, at + ROWS, axis=a.ndim - 2)  1.54 us
    pallas_call x1, Pallas kernels, shards(): pl.pallas_call(combine_kernel, in_specs=[vmem] * (ITERS + 4), out_specs=[...  1.21 us
  transfers between devices with their start and end apart: 4, of which 2 were waited for; matrix products, arithmetic and copies ran while one was open for 0% of the time, Pallas kernels for 18%

profile of v8, /device:TPU:0, one launch (start us, length us, event | category | flops | bytes accessed | tf_op | source)
XLA Modules:
  0.0 42.5 jit_solution(14070523199790093184)
XLA Ops:
  0.6 0.0 copy-start
  0.6 0.0 copy-start.1
  0.7 1.1 %convert_element_type.3.counts = f32[256,256]{1,0:T(8,128)S(1)} convert(s32[256,256]{1,0:T(8,128)} %param.5) | non-fusion elementwise | flops 65536 | bytes 524288 | tf_op jit(solution)/shard_map/convert_element_type | solution.py:562
  1.8 1.5 %fusion = (f32[3,8,8,256]{3,2,1,0:T(8,128)S(1)}, f32[3,8,8,256]{3,2,1,0:T(8,128)S(1)}) fusion(f32[3,8,256,256]{3,2,1,0:T(8,128)} %fields.3), kind=kLoop, calls=%fused_computation.6 | loop fusion | bytes 786432 | tf_op jit(solution)/shard_map/slice | solution.py:565
  3.3 0.7 %slice_bitcast_fusion = (f32[1,8,256]{2,1,0:T(8,128)S(1)}, f32[1,8,256]{2,1,0:T(8,128)S(1)}, f32[1,8,256]{2,1,0:T(8,128)S(1)}, f32[1,8,256]{2,1,0:T(8,128)S(1)}) fusion(f32[256,256]{1,0:T(8,128)S(1)} %convert_element_type.3.counts, f32[256,256]{1,0:T(8,128)} %old_hbm.1), kind=kLoop, calls=%fused_computation.2 | loop fusion | bytes 65536 | tf_op jit(solution)/shard_map/broadcast_in_dim | solution.py:568
  4.1 0.5 %collective-permute-start = (f32[26,8,256]{2,1,0:T(8,128)S(1)}, f32[26,8,256]{2,1,0:T(8,128)S(1)}, u32[]{:S(2)}, u32[]{:S(2)}) collective-permute-start(f32[26,8,256]{2,1,0:T(8,128)S(1)} %pad_maximum_fusion), channel_id=1, source_target_pairs={{0,8},{8,16},{16,24},{24,0},{1,9},{9,17},{17,25},{25,1},{2,10},{10... | collective-permute-start | bytes 638984 | tf_op jit(solution)/shard_map/ppermute | solution.py:554
  4.6 2.0 %collective-permute-start.1 = (f32[26,8,256]{2,1,0:T(8,128)S(1)}, f32[26,8,256]{2,1,0:T(8,128)S(1)}, u32[]{:S(2)}, u32[]{:S(2)}) collective-permute-start(f32[26,8,256]{2,1,0:T(8,128)S(1)} %pad_maximum_fusion.1), channel_id=1, source_target_pairs={{0,24},{8,0},{16,8},{24,16},{1,25},{9,1},{17,9},{25,17},{2,26},{10... | collective-permute-start | bytes 638984 | tf_op jit(solution)/shard_map/ppermute | solution.py:554
  6.6 0.0 copy-start.2
  6.6 0.7 %copy-done.2 = f32[8]{0:T(128)S(1)} copy-done((f32[8]{0:T(128)S(1)}, f32[8]{0:T(128)}, u32[]{:S(2)}) %copy-start.2) | copy-done | bytes 56
  7.3 7.7 %inner_forcing.1 = (f32[2,272,128]{2,1,0:T(8,128)S(1)}, f32[8,256,128]{2,1,0:T(8,128)S(1)}) custom-call(f32[8]{0:T(128)S(1)} %copy-done.2, f32[3,8,256,256]{3,2,1,0:T(8,128)} %fields.3, f32[256,256]{1,0:T(8,128)S(1)} %convert_element_type.3.counts), custom_call_target="tpu_custom_call" | custom-call | flops 20971520 | bytes 6291456 | tf_op jit(solution)/shard_map/inner_forcing/pallas_call | solution.py:584
  15.0 0.0 collective-permute-done.south
  15.0 0.0 collective-permute-done.1.north
  15.0 0.0 copy-done
  15.0 0.0 copy-done.1
  15.0 2.3 %edge_forcing.1 = (f32[2,272,128]{2,1,0:T(8,128)S(1)}, f32[2,288,128]{2,1,0:T(8,128)S(1)}, f32[2,288,128]{2,1,0:T(8,128)S(1)}, f32[40,384]{1,0:T(8,128)S(1)}, f32[40,384]{1,0:T(8,128)S(1)}) custom-call(f32[8]{0:T(128)S(1)} %copy-done.2, f32[3,8,256,256]{3,2,1,0:T(8,128)S(1)} %copy-done, f32[26,8,256]{2,1,0:T(8,128)S(1)} %collective-permute-done.south, ...), custom_call_target="tpu_custom_call" | custom-call | tf_op jit(solution)/shard_map/edge_forcing/pallas_call | solution.py:603
  17.3 2.3 %collective-permute-start.2 = (f32[40,384]{1,0:T(8,128)S(1)}, f32[40,384]{1,0:T(8,128)S(1)}, u32[]{:S(2)}, u32[]{:S(2)}) collective-permute-start(f32[40,384]{1,0:T(8,128)S(1)} %get-tuple-element.21.to_east), channel_id=1, source_target_pairs={{0,1},{1,2},{2,3},{3,4},{4,5},{5,6},{6,7},{7,0},{8,9},{9,10},{10,1... | collective-permute-start | bytes 184328 | tf_op jit(solution)/shard_map/ppermute | solution.py:554
  19.6 3.1 %collective-permute-start.3 = (f32[40,384]{1,0:T(8,128)S(1)}, f32[40,384]{1,0:T(8,128)S(1)}, u32[]{:S(2)}, u32[]{:S(2)}) collective-permute-start(f32[40,384]{1,0:T(8,128)S(1)} %get-tuple-element.22.to_west), channel_id=1, source_target_pairs={{0,7},{1,0},{2,1},{3,2},{4,3},{5,4},{6,5},{7,6},{8,15},{9,8},{10,9... | collective-permute-start | bytes 184328 | tf_op jit(solution)/shard_map/ppermute | solution.py:554
  22.7 2.1 %collective-permute-done.2.from_west = f32[40,384]{1,0:T(8,128)S(1)} collective-permute-done((f32[40,384]{1,0:T(8,128)S(1)}, f32[40,384]{1,0:T(8,128)S(1)}, u32[]{:S(2)}, u32[]{:S(2)}) %collective-permute-start.2) | collective-permute-done | bytes 61472 | tf_op jit(solution)/shard_map/ppermute | solution.py:554
  24.9 0.3 collective-permute-done.3.from_east
  25.2 3.2 %krylov.1 = (f32[2,256,128]{2,1,0:T(8,128)S(1)}, f32[2,256,128]{2,1,0:T(8,128)S(1)}, f32[2,256,128]{2,1,0:T(8,128)S(1)}, f32[2,256,128]{2,1,0:T(8,128)S(1)}, f32...) custom-call(f32[8]{0:T(128)S(1)} %copy-done.2, ...), custom_call_target="tpu_custom_call" | custom-call | tf_op jit(solution)/shard_map/krylov/pallas_call | solution.py:627
  28.4 12.9 %all_to_all.5.moments = f32[32,1,128]{2,1,0:T(1,128)S(1)} all-to-all(f32[32,1,128]{2,1,0:T(1,128)S(1)} %get-tuple-element.23), channel_id=1, replica_groups=mesh['by'=4,'bx'=8] {'by','bx'}, dimensions={0} | all-to-all | bytes 32768 | tf_op jit(solution)/shard_map/all_to_all | solution.py:645
  41.3 1.2 %combine.1 = (f32[256,256]{1,0:T(8,128)}, f32[256,256]{1,0:T(8,128)}) custom-call(f32[32,1,128]{2,1,0:T(1,128)S(1)} %all_to_all.5.moments, f32[2,288,128]{2,1,0:T(8,128)S(1)} %get-tuple-element.20.guess, f32[2,256,128]{2,1,0:T(8,128)S(1)} %get-tuple-element.24.base0, f32[2,256,128]{2,1,0:T(8,128)S(1)} %get-tuple-element.25.base1, ...), custom_call_target="tpu_custom_call" | custom-call | tf_op jit(solution)/shard_map/combine/pallas_call | solution.py:647
  (2 shorter events, 0.0 us)
Async XLA Ops:
  0.6 14.4 %copy-start = (f32[3,8,256,256]{3,2,1,0:T(8,128)S(1)}, f32[3,8,256,256]{3,2,1,0:T(8,128)}, u32[]{:S(2)}) copy-start(f32[3,8,256,256]{3,2,1,0:T(8,128)} %fields.3) | copy-start | bytes 18874372
  0.6 14.4 %copy-start.1 = (f32[256,256]{1,0:T(8,128)S(1)}, f32[256,256]{1,0:T(8,128)}, u32[]{:S(2)}) copy-start(f32[256,256]{1,0:T(8,128)} %old_hbm.1) | copy-start | bytes 786436
  4.1 10.9 %collective-permute-start = (f32[26,8,256]{2,1,0:T(8,128)S(1)}, f32[26,8,256]{2,1,0:T(8,128)S(1)}, u32[]{:S(2)}, u32[]{:S(2)}) collective-permute-start(f32[26,8,256]{2,1,0:T(8,128)S(1)} %pad_maximum_fusion), channel_id=1, source_target_pairs={{0,8},{8,16},{16,24},{24,0},{1,9},{9,17},{17,25},{25,1},{2,10},{10... | collective-permute-start | bytes 638984 | tf_op jit(solution)/shard_map/ppermute | solution.py:554
  4.6 10.4 %collective-permute-start.1 = (f32[26,8,256]{2,1,0:T(8,128)S(1)}, f32[26,8,256]{2,1,0:T(8,128)S(1)}, u32[]{:S(2)}, u32[]{:S(2)}) collective-permute-start(f32[26,8,256]{2,1,0:T(8,128)S(1)} %pad_maximum_fusion.1), channel_id=1, source_target_pairs={{0,24},{8,0},{16,8},{24,16},{1,25},{9,1},{17,9},{25,17},{2,26},{10... | collective-permute-start | bytes 638984 | tf_op jit(solution)/shard_map/ppermute | solution.py:554
  6.6 0.7 %copy-start.2 = (f32[8]{0:T(128)S(1)}, f32[8]{0:T(128)}, u32[]{:S(2)}) copy-start(f32[8]{0:T(128)} %thick.5) | copy-start | bytes 100
  17.3 7.6 %collective-permute-start.2 = (f32[40,384]{1,0:T(8,128)S(1)}, f32[40,384]{1,0:T(8,128)S(1)}, u32[]{:S(2)}, u32[]{:S(2)}) collective-permute-start(f32[40,384]{1,0:T(8,128)S(1)} %get-tuple-element.21.to_east), channel_id=1, source_target_pairs={{0,1},{1,2},{2,3},{3,4},{4,5},{5,6},{6,7},{7,0},{8,9},{9,10},{10,1... | collective-permute-start | bytes 184328 | tf_op jit(solution)/shard_map/ppermute | solution.py:554
  19.6 5.5 %collective-permute-start.3 = (f32[40,384]{1,0:T(8,128)S(1)}, f32[40,384]{1,0:T(8,128)S(1)}, u32[]{:S(2)}, u32[]{:S(2)}) collective-permute-start(f32[40,384]{1,0:T(8,128)S(1)} %get-tuple-element.22.to_west), channel_id=1, source_target_pairs={{0,7},{1,0},{2,1},{3,2},{4,3},{5,4},{6,5},{7,6},{8,15},{9,8},{10,9... | collective-permute-start | bytes 184328 | tf_op jit(solution)/shard_map/ppermute | solution.py:554
